TPU v7x, 512 devices: a whole 4x4x16 slice. The times are simulated.
512 devices in a mesh: prow: 16 (over y, z_hi), pcol: 32 (over x, z_lo, core).
Axes of the slice: x: 4, y: 4, z: 16 (z_hi: 4, z_lo: 4; z = z_hi * 4 + z_lo), core: 2. Of those that a mesh axis runs over, the one named last changes fastest.
Arguments:
- window: float32 [16384, 16384], P('prow', 'pcol'), may hold values from -6 to 6
- panel: float32 [16384, 256], P(('prow', 'pcol')), may hold values from -0.046875 to 0.046875
- factor: float32 [256, 256], replicated, may hold values from -1 to 1
- col_check: float32 [16384], P('pcol'), may hold values from -6 to 6
- row_check: float32 [16384], P('prow'), may hold values from -6 to 6
Outputs:
- new_window: float32 [16384, 16384], P('prow', 'pcol')
- new_col: float32 [16384], P('pcol')
- new_row: float32 [16384], P('prow')
All inputs are finite; a program needn't handle non-finite values.
Results may differ from a plain program's by a relative error of at most 0.00005.
Values sent between devices are 32-bit elements; how exact they have to be, the bound alone decides.
No kernel may reach another device: no remote copies, remote signals or barrier semaphores. Data moves between devices by JAX's collectives and lax.ppermute only.
A program may use at most 64 MiB of HBM per device.

v0:
```python
import math

import jax
import jax.numpy as jnp
from jax import lax
from jax.sharding import PartitionSpec as P

N = 16384


def spread(block, axis, holder):
    block = jnp.where(lax.axis_index(axis) == holder, block, jnp.zeros_like(block))
    return lax.psum(block, axis)


def unit_lower(values, row_start):
    rows = row_start + jnp.arange(values.shape[0], dtype=jnp.int32)[:, None]
    cols = jnp.arange(values.shape[1], dtype=jnp.int32)[None, :]
    ones = jnp.where(rows == cols, jnp.ones_like(values), jnp.zeros_like(values))
    return jnp.where(rows > cols, values, ones)


def matmul(left, right):
    return jnp.dot(left, right, precision=lax.Precision.HIGHEST)


def inner_rows(left, right):
    return lax.dot_general(left, right, (((0,), (0,)), ((), ())), precision=lax.Precision.HIGHEST)


def outer_cols(left, right):
    return lax.dot_general(left, right, (((1,), (1,)), ((), ())), precision=lax.Precision.HIGHEST)


def on_device(window, panel, factor, col_check, row_check):
    n_rows = lax.axis_size("prow")
    n_cols = lax.axis_size("pcol")
    prow_idx = lax.axis_index("prow")
    pcol_idx = lax.axis_index("pcol")
    rows_blk = window.shape[0]
    cols_blk = window.shape[1]
    ratio = n_cols // n_rows
    upper = jnp.triu(factor)
    gathered = lax.all_gather(panel, "pcol", axis=0, tiled=True)
    v_rows = unit_lower(gathered, prow_idx * rows_blk)
    half_part = lax.dynamic_slice_in_dim(gathered, pcol_idx % ratio * cols_blk, cols_blk, 0)
    raw_cols = spread(half_part, "prow", pcol_idx // ratio)
    v_cols = unit_lower(raw_cols, pcol_idx * cols_blk)
    col_proj, col_sums = lax.psum((matmul(col_check, v_cols), jnp.sum(v_cols, axis=0)), "pcol")
    row_part = matmul(row_check, v_rows)
    x_rows = lax.psum(matmul(window, v_cols), "pcol")
    w_trans, row_proj = lax.psum((inner_rows(window, v_rows), row_part), "prow")
    y_rows = matmul(x_rows, upper)
    coupled = lax.psum(inner_rows(v_rows, y_rows), "prow")
    m_trans = matmul(w_trans - outer_cols(v_cols, coupled), upper)
    left = jnp.concatenate([y_rows, v_rows], axis=1)
    right = jnp.concatenate([v_cols, m_trans], axis=1)
    new_window = window - outer_cols(left, right)
    scaled = col_sums / math.sqrt(N)
    new_col = col_check - matmul(v_cols, matmul(col_proj, upper)) - matmul(m_trans, scaled)
    inner = row_proj - matmul(coupled, scaled)
    new_row = row_check - matmul(y_rows, scaled) - matmul(v_rows, matmul(inner, upper))
    return (new_window, new_col, new_row)


def solution(mesh):
    placed = (P("prow", "pcol"), P(("prow", "pcol"), None), P(), P("pcol"), P("prow"))
    return jax.shard_map(
        on_device,
        mesh=mesh,
        in_specs=placed,
        out_specs=(P("prow", "pcol"), P("pcol"), P("prow")),
        check_vma=False,
    )
```

profile of v0, /device:TPU:6, one launch (start us, length us, event | category | flops | bytes accessed | tf_op | source)
XLA Modules:
  0.0 811.9 jit_solution(8223633421973068316)
XLA Ops:
  7.2 0.7 all-gather.2.cloned.1.call-update
  8.0 69.5 %all-gather.2.cloned.1.call-done = f32[1024,256]{1,0:T(8,128)} async-done(((f32[32,256]{1,0:T(8,128)}), f32[1024,256]{1,0:T(8,128)}) %all-gather.2.cloned.1.call-update) | async-done | bytes 1048592 | tf_op jit(solution)/shard_map/all_gather | solution.py:44
  77.5 2.5 copy.9
  80.0 1.9 dynamic-slice_select_fusion
  82.0 208.6 %all-reduce.6.cloned.1.call-done = f32[512,256]{0,1:T(8,128)} async-done(((f32[512,256]{0,1:T(8,128)}), f32[512,256]{0,1:T(8,128)}) %all-reduce.6.cloned.1.call-update) | async-done | bytes 524304 | tf_op jit(solution)/shard_map/psum | solution.py:13
  290.6 1.2 fusion.30
  291.8 2.9 convolution_bitcast_fusion
  294.8 1.4 select_select_fusion
  296.2 0.9 fusion.36
  297.1 49.6 %psum.55 = f32[256]{0:T(256)S(1)} all-reduce(f32[256]{0:T(256)S(1)} %bitcast.62), channel_id=1, replica_groups=mesh['prow'=16,'pcol'=32] {'prow'}, use_global_device_ids=true, to_apply=%region_7.8 | all-reduce | flops 256 | bytes 2048 | tf_op jit(solution)/shard_map/psum | solution.py:52
  346.8 4.4 convolution_bitcast_fusion.1
  351.6 58.0 %all-reduce = (f32[256]{0:T(256)S(1)}, f32[256]{0:T(256)S(1)}) all-reduce(f32[256]{0:T(256)S(1)} %get-tuple-element.7, f32[256]{0:T(256)S(1)} %bitcast.61), channel_id=1, replica_groups=mesh['prow'=16,'pcol'=32] {'pcol'}, use_global_device_ids=true, to_apply=%region_6.7 | all-reduce | flops 512 | bytes 4096 | tf_op jit(solution)/shard_map/psum | solution.py:49
  409.6 156.4 %all-reduce.8.cloned.1.call-done = f32[1024,256]{0,1:T(8,128)} async-done(((f32[1024,256]{0,1:T(8,128)}), f32[1024,256]{0,1:T(8,128)}) %all-reduce.8.cloned.1.call-update) | async-done | bytes 1048592 | tf_op jit(solution)/shard_map/psum | solution.py:51
  566.0 2.3 fusion.15
  568.4 1.7 fusion.31
  570.8 0.7 fusion.35
  571.5 222.5 %all-reduce.10.cloned.1.call-done = (f32[512,256]{0,1:T(8,128)}, f32[256,256]{1,0:T(8,128)}) async-done(((f32[512,256]{0,1:T(8,128)}, f32[256,256]{1,0:T(8,128)}), (f32[512,256]{0,1:T(8,128)}, f32[256,256]{1,0:T(8,128)})) %all-reduce.10.cloned.1.call-update) | async-done | bytes 786448 | tf_op jit(solution)/shard_map/psum | solution.py:52
  794.0 1.4 fusion.37
  795.4 1.8 convolution_subtract_fusion
  797.2 0.7 fusion.13
  798.3 4.8 fusion.4
  803.5 0.7 fusion.38
  804.1 0.6 subtract_subtract_fusion
  804.8 0.6 subtract_subtract_fusion.1
  (27 shorter events, 2.1 us)
Async XLA Ops:
  7.2 70.3 %all-gather.2.cloned.1.call-start = ((), (), s32[]{:S(2)}) async-start(), calls=%async_computation | async-start | bytes 1081344 | tf_op jit(solution)/shard_map/all_gather | solution.py:44
  7.9 282.7 %all-reduce.6.cloned.1.call-start = ((), (), s32[]{:S(2)}) async-start(), calls=%async_computation.1 | async-start | bytes 1048576 | tf_op jit(solution)/shard_map/psum | solution.py:13
  8.0 283.8 %copy-start = (f32[1024,512]{1,0:T(8,128)S(1)}, f32[1024,512]{1,0:T(8,128)}, u32[]{:S(2)}) copy-start(f32[1024,512]{1,0:T(8,128)} %param.5) | copy-start | bytes 6291460
  81.9 484.1 %all-reduce.8.cloned.1.call-start = ((), (), s32[]{:S(2)}) async-start(), calls=%async_computation.2 | async-start | bytes 2097152 | tf_op jit(solution)/shard_map/psum | solution.py:51
  294.7 1.5 copy-start.3
  294.8 499.3 %all-reduce.10.cloned.1.call-start = ((), (), s32[]{:S(2)}) async-start(), calls=%async_computation.3 | async-start | bytes 1572864 | tf_op jit(solution)/shard_map/psum | solution.py:52
  297.1 54.0 %copy-start.4 = (f32[512]{0:T(512)S(1)}, f32[512]{0:T(512)}, u32[]{:S(2)}) copy-start(f32[512]{0:T(512)} %param.8) | copy-start | bytes 6148
  346.8 219.3 %copy-start.2 = (f32[256,256]{1,0:T(8,128)S(1)}, f32[256,256]{1,0:T(8,128)}, u32[]{:S(2)}) copy-start(f32[256,256]{1,0:T(8,128)} %param.7) | copy-start | bytes 786436
  794.0 4.3 copy-start.1
Sparse Core Ops, SparseCore 0:
  10.1 67.2 all-gather.1
  82.0 208.5 all-reduce.5
  294.9 271.0 all-reduce.7
  570.3 223.7 all-reduce.9
where the time goes:
time: 812 us
  waiting for transfers between devices  658 us (81%)
  blocking collectives  108 us (13%)
  matrix products  24.2 us (3%)
  between operations  13.9 us (2%)
    psum x1, waiting for transfers between devices, on_device(): w_trans, row_proj = lax.psum((inner_rows(window, v_rows), row_part), 'prow')  223 us
    psum x1, waiting for transfers between devices, spread(): return lax.psum(block, axis)  209 us
    psum x1, waiting for transfers between devices, on_device(): x_rows = lax.psum(matmul(window, v_cols), 'pcol')  156 us
    all_gather x1, waiting for transfers between devices, on_device(): gathered = lax.all_gather(panel, 'pcol', axis=0, tiled=True)  69.5 us
    psum x1, blocking collectives, on_device(): lax.psum((matmul(col_check, v_cols), jnp.sum(v_cols, axis=0)), 'pcol')  58 us
    psum x1, blocking collectives, on_device(): w_trans, row_proj = lax.psum((inner_rows(window, v_rows), row_part), 'prow')  49.6 us
  transfers between devices with their start and end apart: 4, of which 4 were waited for; matrix products, arithmetic and copies ran while one was open for 1% of the time, Pallas kernels for 0%

commit v1 on v0

v1 whole, which is shorter than its diff:
```python
import math

import jax
import jax.numpy as jnp
from jax import lax
from jax.sharding import Mesh, PartitionSpec as P

N = 16384
AXES = ("y", "zh", "x", "zl", "core")
SIZES = (4, 4, 4, 4, 2)
PREC = lax.Precision.HIGHEST


def dot(left, right, dims=((1,), (0,))):
    return lax.dot_general(left, right, (dims, ((), ())), precision=PREC)


def unit_lower(values, row_start):
    rows = row_start + lax.broadcasted_iota(jnp.int32, values.shape, 0)
    cols = lax.broadcasted_iota(jnp.int32, values.shape, 1)
    return jnp.where(rows > cols, values, jnp.where(rows == cols, 1.0, 0.0))


def exchange(parts, axis):
    return lax.all_to_all(parts, axis, 0, 0)


def gather(block, axis, size):
    parts = exchange(jnp.broadcast_to(block[None], (size,) + block.shape), axis)
    return parts.reshape((size * block.shape[0],) + block.shape[1:])


def reduce_scatter(block, axis, size):
    rows = block.shape[0] // size
    return jnp.sum(exchange(block.reshape(size, rows, block.shape[1]), axis), axis=0)


def reduce_both(block, small, axis, size):
    rows = block.shape[0] // size
    cut = block.reshape(size, rows, block.shape[1])
    both = jnp.concatenate([cut, jnp.broadcast_to(small[None], (size,) + small.shape)], axis=1)
    total = jnp.sum(exchange(both, axis), axis=0)
    return total[:rows], total[rows:]


def transposition():
    pairs = []
    for y in range(4):
        for zh in range(4):
            for x in range(4):
                for zl in range(4):
                    for core in range(2):
                        src = (((y * 4 + zh) * 4 + x) * 4 + zl) * 2 + core
                        dst = (((x * 4 + zl) * 4 + y) * 4 + zh) * 2 + core
                        pairs.append((src, dst))
    return pairs


def on_device(window, panel, factor, col_check, row_check):
    y, zh, core = lax.axis_index("y"), lax.axis_index("zh"), lax.axis_index("core")
    prow = y * 4 + zh
    kdim = panel.shape[1]
    shard = panel.shape[0]
    n_rows, n_cols = window.shape
    upper = jnp.triu(factor)

    mine = gather(panel, ("x", "zl"), 16)
    other = lax.ppermute(mine, "core", [(0, 1), (1, 0)])
    mine, other = (v.reshape(16, 1, shard, kdim) for v in (mine, other))
    first = jnp.where(core == 0, mine, other)
    second = jnp.where(core == 0, other, mine)
    v_rows = jnp.concatenate([first, second], axis=1).reshape(n_rows, kdim)
    v_rows = unit_lower(v_rows, prow * n_rows)

    half = lax.dynamic_slice_in_dim(v_rows, core * n_cols, n_cols, 0)
    v_cols = lax.ppermute(half, AXES, transposition())

    w_part = dot(v_rows, window, ((0,), (0,)))
    w_part = reduce_scatter(w_part, "y", 4)
    w_slice = reduce_scatter(w_part, "zh", 4)
    row_part = dot(row_check[None], v_rows)

    x_part = dot(window, v_cols)
    p_part = dot(w_slice, v_cols)
    col_part = dot(col_check[None], v_cols)
    sum_part = jnp.sum(v_cols, axis=0, keepdims=True)
    small = jnp.concatenate([p_part, col_part, sum_part, jnp.zeros((6, kdim), jnp.float32)], axis=0)
    x_part, small = reduce_both(x_part, small, "core", 2)
    x_part, small = reduce_both(x_part, small, "x", 4)
    x_slice, small = reduce_both(x_part, small, "zl", 4)
    k_rows = w_slice.shape[0]
    p_slice, col_proj, sums = small[:k_rows], small[k_rows], small[k_rows + 1]
    scaled = sums / math.sqrt(N)

    z_slice = dot(p_slice, upper)
    g_slice = w_slice - dot(z_slice, v_cols, ((1,), (1,)))
    z_scaled = dot(scaled[None], z_slice, ((1,), (1,)))
    lanes = 128
    extra = jnp.concatenate(
        [
            row_part.reshape(kdim // lanes, lanes),
            jnp.pad(z_scaled, ((0, 0), (0, lanes - k_rows))),
            jnp.zeros((k_rows - kdim // lanes - 1, lanes), jnp.float32),
        ],
        axis=0,
    )
    g_all = gather(jnp.concatenate([g_slice, extra], axis=1), "zh", 4)
    g_all = gather(g_all, "y", 4)
    g_full = g_all[:, :n_cols]
    extras = g_all[:, n_cols:].reshape(16, k_rows, lanes)
    row_proj = jnp.sum(extras[:, : kdim // lanes], axis=0).reshape(kdim)
    inner = row_proj - extras[:, kdim // lanes, :k_rows].reshape(kdim)

    x_rows = gather(x_slice, "zl", 4)
    x_rows = gather(x_rows, "x", 4)
    x_rows = gather(x_rows, "core", 2)

    y_rows = dot(x_rows, upper)
    m_trans = dot(g_full, upper, ((0,), (0,)))
    left = jnp.concatenate([y_rows, v_rows], axis=1)
    right = jnp.concatenate([v_cols, m_trans], axis=1)
    new_window = window - dot(left, right, ((1,), (1,)))
    col_vec = jnp.concatenate([dot(col_proj[None], upper)[0], scaled])
    row_vec = jnp.concatenate([scaled, dot(inner[None], upper)[0]])
    new_col = col_check - dot(col_vec[None], right, ((1,), (1,)))[0]
    new_row = row_check - dot(row_vec[None], left, ((1,), (1,)))[0]
    return (new_window, new_col, new_row)


def solution(mesh):
    fine = Mesh(mesh.devices.reshape(SIZES), AXES)
    rows, cols = ("y", "zh"), ("x", "zl", "core")
    placed = (P(rows, cols), P(AXES, None), P(), P(cols), P(rows))
    return jax.shard_map(
        on_device,
        mesh=fine,
        in_specs=placed,
        out_specs=(P(rows, cols), P(cols), P(rows)),
        check_vma=False,
    )
```

time: 812 us -> 212 us (0.26)
  waiting for transfers between devices: 658 us -> 56.4 us
  starting transfers between devices: 0.16 us -> 43.8 us
  blocking collectives: 108 us -> 73.9 us
  between operations: 13.9 us -> 0.96 us
    psum x3 -> x0, waiting for transfers between devices: 588 us -> none  [the longest x1 223 us: on_device(): w_trans, row_proj = lax.psum((inner_rows(window, v_rows), row_part), 'prow')]
    psum x2 -> x0, blocking collectives: 108 us -> none  [the longest x1 58 us: on_device(): lax.psum((matmul(col_check, v_cols), jnp.sum(v_cols, axis=0)), 'pcol')]
    all_to_all x0 -> x5, blocking collectives: none -> 73.9 us  [exchange(): return lax.all_to_all(parts, axis, 0, 0)]
    all_gather x1 -> x0, waiting for transfers between devices: 69.5 us -> none  [on_device(): gathered = lax.all_gather(panel, 'pcol', axis=0, tiled=True)]
    all_to_all x0 -> x6, waiting for transfers between devices: none -> 54.6 us  [exchange(): return lax.all_to_all(parts, axis, 0, 0)]
    all_to_all x0 -> x6, starting transfers between devices: none -> 35.1 us  [exchange(): return lax.all_to_all(parts, axis, 0, 0)]
    ppermute x0 -> x2, starting transfers between devices: none -> 8.78 us  [the longest x1 6.87 us: on_device(): v_cols = lax.ppermute(half, AXES, transposition())]
    dot_general x16 -> x15, matrix products: 24.2 us -> 20.1 us  [dot(): return lax.dot_general(left, right, (dims, ((), ())), precision=PREC)]
  transfers between devices with their start and end apart: 4 -> 8, of which waited for: 4 -> 7; matrix products, arithmetic and copies ran while one was open for 1% -> 7% of each run, Pallas kernels for 0% -> 0%
where the time goes in v1:
time: 212 us; the launch traced here: 209 us
  blocking collectives  73.9 us (35%)
  waiting for transfers between devices  56.4 us (27%)
  starting transfers between devices  43.8 us (21%)
  matrix products  20.1 us (9%)
  local copies, waits for them, and re-layouts  8.4 us (4%)
  other arithmetic  4.94 us (2%)
    all_to_all x5, blocking collectives, exchange(): return lax.all_to_all(parts, axis, 0, 0)  73.9 us
    all_to_all x6, waiting for transfers between devices, exchange(): return lax.all_to_all(parts, axis, 0, 0)  54.6 us
    all_to_all x6, starting transfers between devices, exchange(): return lax.all_to_all(parts, axis, 0, 0)  35.1 us
    dot_general x15, matrix products, dot(): return lax.dot_general(left, right, (dims, ((), ())), precision=PREC)  20.1 us
    ppermute x1, starting transfers between devices, on_device(): v_cols = lax.ppermute(half, AXES, transposition())  6.87 us
  transfers between devices with their start and end apart: 8, of which 7 were waited for; matrix products, arithmetic and copies ran while one was open for 7% of the time, Pallas kernels for 0%

profile of v1, /device:TPU:6, one launch (start us, length us, event | category | flops | bytes accessed | tf_op | source)
XLA Modules:
  0.0 208.6 jit_solution(6102721226516364259)
XLA Ops:
  1.4 22.9 %all_to_all.55 = f32[16,32,256]{2,1,0:T(8,128)S(1)} all-to-all(f32[16,32,256]{2,1,0:T(8,128)S(1)} %broadcast_in_dim.42), channel_id=1, replica_groups=mesh['y'=4,'zh'=4,'x'=4,'zl'=4,'core'=2] {'x','zl'}, dimensions={0} | all-to-all | bytes 1048576 | tf_op jit(solution)/shard_map/all_to_all | solution.py:25
  24.3 1.9 collective-permute-start
  26.2 1.9 collective-permute-done
  31.2 6.9 %collective-permute-start.1 = (f32[512,256]{0,1:T(8,128)S(1)}, f32[512,256]{0,1:T(8,128)S(1)}, u32[]{:S(2)}, u32[]{:S(2)}) collective-permute-start(f32[512,256]{0,1:T(8,128)S(1)} %constant_dynamic-slice_fusion), channel_id=1, source_target_pairs={{0,0},{1,1},{2,32},{3,33},{4,64},{5,65},{6,96},{7,97},{8,128},{9,1... | collective-permute-start | bytes 1572872 | tf_op jit(solution)/shard_map/ppermute | solution.py:76
  38.1 2.7 %fusion = f32[4,64,512]{2,1,0:T(8,128)} fusion(f32[4,64,1024]{2,1,0:T(8,128)S(1)} %bitcast.67, f32[1024,512]{1,0:T(8,128)S(1)} %copy-done), kind=kOutput, calls=%fused_computation.1 | convolution fusion | flops 1610612736 | bytes 3670016 | tf_op jit(solution)/shard_map/dot_general | solution.py:15
  40.8 3.5 %all-to-all-start.1 = ((f32[4,64,512]{2,1,0:T(8,128)}), f32[4,64,512]{2,1,0:T(8,128)S(1)}, u32[]{:S(2)}, u32[]{:S(2)}) async-start(f32[4,64,512]{2,1,0:T(8,128)} %fusion), calls=%async_computation.1 | async-start | bytes 1048576 | tf_op jit(solution)/shard_map/all_to_all | solution.py:25
  44.4 12.8 %all-to-all-done.1 = f32[4,64,512]{2,1,0:T(8,128)S(1)} async-done(((f32[4,64,512]{2,1,0:T(8,128)}), f32[4,64,512]{2,1,0:T(8,128)S(1)}, u32[]{:S(2)}, u32[]{:S(2)}) %all-to-all-start.1) | async-done | bytes 524320 | tf_op jit(solution)/shard_map/all_to_all | solution.py:25
  57.8 6.7 %all-to-all-start.2 = ((f32[4,16,512]{2,1,0:T(8,128)}), f32[4,16,512]{2,1,0:T(8,128)S(1)}, u32[]{:S(2)}, u32[]{:S(2)}) async-start(f32[4,16,512]{2,1,0:T(8,128)} %bitcast.10), calls=%async_computation.2 | async-start | bytes 262144 | tf_op jit(solution)/shard_map/all_to_all | solution.py:25
  64.5 3.5 %convolution_bitcast_fusion = f32[1024,256]{0,1:T(8,128)S(1)} fusion(f32[512,256]{0,1:T(8,128)S(1)} %collective-permute-done.1, f32[1024,512]{1,0:T(8,128)} %param.5), kind=kOutput, calls=%fused_computation.6 | convolution fusion | flops 1610612736 | bytes 3670016 | tf_op jit(solution)/shard_map/dot_general | solution.py:15
  70.0 16.9 %all-to-all-done.2 = f32[4,16,512]{2,1,0:T(8,128)S(1)} async-done(((f32[4,16,512]{2,1,0:T(8,128)}), f32[4,16,512]{2,1,0:T(8,128)S(1)}, u32[]{:S(2)}, u32[]{:S(2)}) %all-to-all-start.2) | async-done | bytes 131104 | tf_op jit(solution)/shard_map/all_to_all | solution.py:25
  87.6 4.6 %all_to_all.56 = f32[2,536,256]{2,1,0:T(8,128)S(1)} all-to-all(f32[2,536,256]{2,1,0:T(8,128)S(1)} %pad_maximum_fusion.5), channel_id=1, replica_groups=mesh['y'=4,'zh'=4,'x'=4,'zl'=4,'core'=2] {'core'}, dimensions={0} | all-to-all | bytes 2195456 | tf_op jit(solution)/shard_map/all_to_all | solution.py:25
  92.4 19.9 %all_to_all.57 = f32[4,152,256]{2,1,0:T(8,128)S(1)} all-to-all(f32[4,152,256]{2,1,0:T(8,128)S(1)} %pad_maximum_fusion.10), channel_id=1, replica_groups=mesh['y'=4,'zh'=4,'x'=4,'zl'=4,'core'=2] {'x'}, dimensions={0} | all-to-all | bytes 1245184 | tf_op jit(solution)/shard_map/all_to_all | solution.py:25
  113.2 9.7 %all-to-all-start.5 = ((f32[4,56,256]{2,1,0:T(8,128)}), f32[4,56,256]{2,1,0:T(8,128)S(1)}, u32[]{:S(2)}, u32[]{:S(2)}) async-start(f32[4,56,256]{2,1,0:T(8,128)} %pad_maximum_fusion.11), calls=%async_computation.5 | async-start | bytes 458752 | tf_op jit(solution)/shard_map/all_to_all | solution.py:25
  123.7 5.9 %all-to-all-done.5 = f32[4,56,256]{2,1,0:T(8,128)S(1)} async-done(((f32[4,56,256]{2,1,0:T(8,128)}), f32[4,56,256]{2,1,0:T(8,128)S(1)}, u32[]{:S(2)}, u32[]{:S(2)}) %all-to-all-start.5) | async-done | bytes 229408 | tf_op jit(solution)/shard_map/all_to_all | solution.py:25
  130.3 3.3 %all-to-all-start.6 = ((f32[4,32,256]{2,1,0:T(8,128)}), f32[4,32,256]{2,1,0:T(8,128)S(1)}, u32[]{:S(2)}, u32[]{:S(2)}) async-start(f32[4,32,256]{2,1,0:T(8,128)} %broadcast_in_dim.92), calls=%async_computation.6 | async-start | bytes 262144 | tf_op jit(solution)/shard_map/all_to_all | solution.py:25
  134.5 5.0 %all-to-all-done.6 = f32[4,32,256]{2,1,0:T(8,128)S(1)} async-done(((f32[4,32,256]{2,1,0:T(8,128)}), f32[4,32,256]{2,1,0:T(8,128)S(1)}, u32[]{:S(2)}, u32[]{:S(2)}) %all-to-all-start.6) | async-done | bytes 131104 | tf_op jit(solution)/shard_map/all_to_all | solution.py:25
  139.5 21.2 %all_to_all.58 = f32[4,16,640]{2,1,0:T(8,128)S(1)} all-to-all(f32[4,16,640]{2,1,0:T(8,128)S(1)} %broadcast_in_dim.99), channel_id=1, replica_groups=mesh['y'=4,'zh'=4,'x'=4,'zl'=4,'core'=2] {'zh'}, dimensions={0} | all-to-all | bytes 327680 | tf_op jit(solution)/shard_map/all_to_all | solution.py:25
  161.5 5.5 %all-to-all-start.7 = ((f32[4,128,256]{2,1,0:T(8,128)}), f32[4,128,256]{2,1,0:T(8,128)S(1)}, u32[]{:S(2)}, u32[]{:S(2)}) async-start(f32[4,128,256]{2,1,0:T(8,128)} %broadcast_in_dim.94), calls=%async_computation.7 | async-start | bytes 1048576 | tf_op jit(solution)/shard_map/all_to_all | solution.py:25
  167.3 5.7 %all-to-all-done.7 = f32[4,128,256]{2,1,0:T(8,128)S(1)} async-done(((f32[4,128,256]{2,1,0:T(8,128)}), f32[4,128,256]{2,1,0:T(8,128)S(1)}, u32[]{:S(2)}, u32[]{:S(2)}) %all-to-all-start.7) | async-done | bytes 524320 | tf_op jit(solution)/shard_map/all_to_all | solution.py:25
  173.1 5.4 %all_to_all.59 = f32[2,512,256]{2,1,0:T(8,128)} all-to-all(f32[2,512,256]{2,1,0:T(8,128)S(1)} %broadcast_in_dim.96), channel_id=1, replica_groups=mesh['y'=4,'zh'=4,'x'=4,'zl'=4,'core'=2] {'core'}, dimensions={0} | all-to-all | bytes 2097152 | tf_op jit(solution)/shard_map/all_to_all | solution.py:25
  179.4 6.4 %all-to-all-start.10 = ((f32[4,64,640]{2,1,0:T(8,128)}), f32[4,64,640]{2,1,0:T(8,128)S(1)}, u32[]{:S(2)}, u32[]{:S(2)}) async-start(f32[4,64,640]{2,1,0:T(8,128)} %broadcast_in_dim.101), calls=%async_computation.10 | async-start | bytes 1310720 | tf_op jit(solution)/shard_map/all_to_all | solution.py:25
  186.4 2.3 %fusion.16 = f32[1024,256]{0,1:T(8,128)S(1)} fusion(f32[1024,256]{1,0:T(8,128)} %bitcast.70, f32[256,256]{1,0:T(8,128)S(1)} %copy-done.2, s32[256]{0:T(256)S(1)} %iota_add_fusion.1), kind=kOutput, calls=%fused_computation.26 | convolution fusion | flops 805437440 | bytes 2360320 | tf_op jit(solution)/shard_map/dot_general | solution.py:15
  188.7 8.3 %all-to-all-done.10 = f32[4,64,640]{2,1,0:T(8,128)S(1)} async-done(((f32[4,64,640]{2,1,0:T(8,128)}), f32[4,64,640]{2,1,0:T(8,128)S(1)}, u32[]{:S(2)}, u32[]{:S(2)}) %all-to-all-start.10) | async-done | bytes 655392 | tf_op jit(solution)/shard_map/all_to_all | solution.py:25
  203.8 4.8 %fusion.4 = f32[1024,512]{1,0:T(8,128)} fusion(f32[1024,512]{1,0:T(8,128)S(1)} %copy-done.1, f32[1024,256]{0,1:T(8,128)S(1)} %select_select_fusion, f32[1024,256]{0,1:T(8,128)S(1)} %fusion.16, f32[512,256]{0,1:T(8,128)S(1)} %fusion.6, f32[512,256]{0,1:T(8,128)S(1)} %collective-permute-done.1), kind=kOutput, calls=%fused_computation.5 | convolution fusion | flops 3222536192 | bytes 7340032 | tf_op jit(solution)/shard_map/dot_general | solution.py:15
  (72 shorter events, 20.1 us)
Async XLA Ops:
  24.3 3.8 %collective-permute-start = (f32[512,256]{1,0:T(8,128)S(1)}, f32[512,256]{1,0:T(8,128)S(1)}, u32[]{:S(2)}, u32[]{:S(2)}) collective-permute-start(f32[512,256]{1,0:T(8,128)S(1)} %bitcast.74), channel_id=1, source_target_pairs={{0,1},{1,0},{2,3},{3,2},{4,5},{5,4},{6,7},{7,6},{8,9},{9,8},{10,11... | collective-permute-start | bytes 1572872 | tf_op jit(solution)/shard_map/ppermute | solution.py:68
  31.0 7.1 %copy-start = (f32[1024,512]{1,0:T(8,128)S(1)}, f32[1024,512]{1,0:T(8,128)}, u32[]{:S(2)}) copy-start(f32[1024,512]{1,0:T(8,128)} %param.5) | copy-start | bytes 6291460
  31.2 33.3 %collective-permute-start.1 = (f32[512,256]{0,1:T(8,128)S(1)}, f32[512,256]{0,1:T(8,128)S(1)}, u32[]{:S(2)}, u32[]{:S(2)}) collective-permute-start(f32[512,256]{0,1:T(8,128)S(1)} %constant_dynamic-slice_fusion), channel_id=1, source_target_pairs={{0,0},{1,1},{2,32},{3,33},{4,64},{5,65},{6,96},{7,97},{8,128},{9,1... | collective-permute-start | bytes 1572872 | tf_op jit(solution)/shard_map/ppermute | solution.py:76
  40.8 16.4 %all-to-all-start.1 = ((f32[4,64,512]{2,1,0:T(8,128)}), f32[4,64,512]{2,1,0:T(8,128)S(1)}, u32[]{:S(2)}, u32[]{:S(2)}) async-start(f32[4,64,512]{2,1,0:T(8,128)} %fusion), calls=%async_computation.1 | async-start | bytes 1048576 | tf_op jit(solution)/shard_map/all_to_all | solution.py:25
  57.8 29.0 %all-to-all-start.2 = ((f32[4,16,512]{2,1,0:T(8,128)}), f32[4,16,512]{2,1,0:T(8,128)S(1)}, u32[]{:S(2)}, u32[]{:S(2)}) async-start(f32[4,16,512]{2,1,0:T(8,128)} %bitcast.10), calls=%async_computation.2 | async-start | bytes 262144 | tf_op jit(solution)/shard_map/all_to_all | solution.py:25
  68.0 1.4 copy-start.6
  69.3 18.2 %copy-start.3 = (f32[1024,256]{1,0:T(8,128)S(1)}, f32[1024,256]{1,0:T(8,128)}, u32[]{:S(2)}) copy-start(f32[1024,256]{1,0:T(8,128)} %copy.54) | copy-start | bytes 3145732
  92.4 30.5 %copy-start.5 = (f32[1024]{0:T(1024)S(1)}, f32[1024]{0:T(1024)}, u32[]{:S(2)}) copy-start(f32[1024]{0:T(1024)} %param.9) | copy-start | bytes 12292
  112.4 21.3 %copy-start.2 = (f32[256,256]{1,0:T(8,128)S(1)}, f32[256,256]{1,0:T(8,128)}, u32[]{:S(2)}) copy-start(f32[256,256]{1,0:T(8,128)} %param.7) | copy-start | bytes 786436
  113.2 16.4 %all-to-all-start.5 = ((f32[4,56,256]{2,1,0:T(8,128)}), f32[4,56,256]{2,1,0:T(8,128)S(1)}, u32[]{:S(2)}, u32[]{:S(2)}) async-start(f32[4,56,256]{2,1,0:T(8,128)} %pad_maximum_fusion.11), calls=%async_computation.5 | async-start | bytes 458752 | tf_op jit(solution)/shard_map/all_to_all | solution.py:25
  130.3 9.2 %all-to-all-start.6 = ((f32[4,32,256]{2,1,0:T(8,128)}), f32[4,32,256]{2,1,0:T(8,128)S(1)}, u32[]{:S(2)}, u32[]{:S(2)}) async-start(f32[4,32,256]{2,1,0:T(8,128)} %broadcast_in_dim.92), calls=%async_computation.6 | async-start | bytes 262144 | tf_op jit(solution)/shard_map/all_to_all | solution.py:25
  161.5 11.5 %all-to-all-start.7 = ((f32[4,128,256]{2,1,0:T(8,128)}), f32[4,128,256]{2,1,0:T(8,128)S(1)}, u32[]{:S(2)}, u32[]{:S(2)}) async-start(f32[4,128,256]{2,1,0:T(8,128)} %broadcast_in_dim.94), calls=%async_computation.7 | async-start | bytes 1048576 | tf_op jit(solution)/shard_map/all_to_all | solution.py:25
  179.4 17.6 %all-to-all-start.10 = ((f32[4,64,640]{2,1,0:T(8,128)}), f32[4,64,640]{2,1,0:T(8,128)S(1)}, u32[]{:S(2)}, u32[]{:S(2)}) async-start(f32[4,64,640]{2,1,0:T(8,128)} %broadcast_in_dim.101), calls=%async_computation.10 | async-start | bytes 1310720 | tf_op jit(solution)/shard_map/all_to_all | solution.py:25
  197.0 0.8 copy-start.4
  199.7 4.1 %copy-start.1 = (f32[1024,512]{1,0:T(8,128)S(1)}, f32[1024,512]{1,0:T(8,128)}, u32[]{:S(2)}) copy-start(f32[1024,512]{1,0:T(8,128)} %param.5) | copy-start | bytes 6291460

commit v2 on v1

v2 whole, which is shorter than its diff:
```python
import math

import jax
import jax.numpy as jnp
from jax import lax
from jax.experimental import pallas as pl
from jax.experimental.pallas import tpu as pltpu
from jax.sharding import Mesh, PartitionSpec as P


N = 16384
AXES = ("y", "zh", "x", "zl", "core")
SIZES = (4, 4, 4, 4, 2)
PREC = lax.Precision.HIGH


def dot(left, right, dims=((1,), (0,))):
    return lax.dot_general(left, right, (dims, ((), ())), precision=PREC)


def unit_lower(values, row_start):
    rows = row_start + lax.broadcasted_iota(jnp.int32, values.shape, 0)
    cols = lax.broadcasted_iota(jnp.int32, values.shape, 1)
    return jnp.where(rows > cols, values, jnp.where(rows == cols, 1.0, 0.0))


def exchange(parts, axis):
    return lax.all_to_all(parts, axis, 0, 0)


def gather(block, axis, size):
    parts = exchange(jnp.broadcast_to(block[None], (size,) + block.shape), axis)
    return parts.reshape((size * block.shape[0],) + block.shape[1:])


def reduce_scatter(block, axis, size):
    rows = block.shape[0] // size
    return jnp.sum(exchange(block.reshape(size, rows, block.shape[1]), axis), axis=0)


def reduce_both(block, small, axis, size):
    rows = block.shape[0] // size
    cut = block.reshape(size, rows, block.shape[1])
    both = jnp.concatenate([cut, jnp.broadcast_to(small[None], (size,) + small.shape)], axis=1)
    total = jnp.sum(exchange(both, axis), axis=0)
    return total[:rows], total[rows:]


def swap(block, axis, size, bit):
    return lax.ppermute(block, axis, [(i, i ^ bit) for i in range(size)])


def ordered(mine, other, bit, axis):
    own = jnp.expand_dims(mine, axis)
    far = jnp.expand_dims(other, axis)
    shape = own.shape[:axis] + (2,) + own.shape[axis + 1 :]
    out = jnp.zeros(shape, mine.dtype)
    out = lax.dynamic_update_slice(out, own, [bit if i == axis else 0 for i in range(len(shape))])
    return lax.dynamic_update_slice(out, far, [1 - bit if i == axis else 0 for i in range(len(shape))])


def double(block, axis, size, bit):
    index = lax.axis_index(axis)
    other = swap(block, axis, size, bit)
    out = ordered(block, other, (index & bit) // bit, 0)
    return out.reshape((2 * block.shape[0],) + block.shape[1:])


def transposition():
    pairs = []
    for y in range(4):
        for zh in range(4):
            for x in range(4):
                for zl in range(4):
                    for core in range(2):
                        src = (((y * 4 + zh) * 4 + x) * 4 + zl) * 2 + core
                        new_y = x % 2 * 2 + core
                        dst = (((new_y * 4 + zl) * 4 + y) * 4 + zh) * 2 + x // 2
                        pairs.append((src, dst))
    return pairs


def split(value):
    high = value.astype(jnp.bfloat16)
    return high, (value - high.astype(jnp.float32)).astype(jnp.bfloat16)


def mm(left, right, dims):
    def one(a, b):
        return lax.dot_general(a, b, (dims, ((), ())), preferred_element_type=jnp.float32)

    (lh, ll), (rh, rl) = left, right
    return one(lh, rh) + (one(lh, rl) + one(ll, rh))


NN = ((1,), (0,))
NT = ((1,), (1,))
TN = ((0,), (0,))
STEPS = 4


VMEM = pl.BlockSpec(memory_space=pltpu.VMEM)
SMEM = pl.BlockSpec(memory_space=pltpu.SMEM)
HBM = pl.BlockSpec(memory_space=pltpu.HBM)


def f32(*shape):
    return jax.ShapeDtypeStruct(shape, jnp.float32)


def block_copy(src, dst, sems, step):
    rows = src.shape[0] // STEPS
    part = pl.ds(step * rows, rows)
    return pltpu.make_async_copy(src.at[part], dst.at[part], sems.at[step])


def interleaved(lead, own, far):
    groups, shard, kdim = own.shape
    first = jnp.where(lead > 0.5, own, far)
    second = jnp.where(lead > 0.5, far, own)
    return jnp.concatenate([first, second], axis=1).reshape(2 * groups * shard, kdim)


def rows_kernel(where_ref, mine_ref, other_ref, check_ref, window_ref, v_ref, w_ref, u_ref, buf, sems):
    for step in range(STEPS):
        block_copy(window_ref, buf, sems, step).start()
    lead = jnp.where(where_ref[0] == 0, 1.0, 0.0)
    groups, rows = mine_ref.shape[0] // STEPS, v_ref.shape[0] // STEPS
    for step in range(STEPS):
        mine, other = (ref[step * groups : (step + 1) * groups] for ref in (mine_ref, other_ref))
        block = unit_lower(interleaved(lead, mine, other), where_ref[1] + step * rows)
        part = slice(step * rows, (step + 1) * rows)
        v_ref[part] = block
        parts = split(block)
        block_copy(window_ref, buf, sems, step).wait()
        w_part = mm(parts, split(buf[part]), TN)
        u_part = mm(split(jnp.broadcast_to(check_ref[:, part], (8, rows))), parts, NN)[:1]
        if step == 0:
            w_ref[...] = w_part
            u_ref[...] = u_part
        else:
            w_ref[...] += w_part
            u_ref[...] += u_part


def rows_call(where, mine, other, window, check):
    n_rows, n_cols = window.shape
    kdim = mine.shape[2]
    return pl.pallas_call(
        rows_kernel,
        in_specs=[SMEM, VMEM, VMEM, VMEM, HBM],
        out_specs=[VMEM] * 3,
        out_shape=[f32(n_rows, kdim), f32(kdim, n_cols), f32(1, kdim)],
        scratch_shapes=[pltpu.VMEM((n_rows, n_cols), jnp.float32), pltpu.SemaphoreType.DMA((STEPS,))],
        name="rows",
    )(where, mine, other, check.reshape(1, n_rows), window)


def cols_kernel(where_ref, own_ref, far_ref, check_ref, window_ref, v_ref, keep_ref, send_ref, tail_ref, buf, sems):
    for step in range(STEPS):
        block_copy(window_ref, buf, sems, step).start()
    lead = jnp.where(where_ref[0] == 0, 1.0, 0.0)
    block = unit_lower(interleaved(lead, own_ref[...], far_ref[...]), where_ref[1])
    v_ref[...] = block
    parts = split(block)
    line = lax.broadcasted_iota(jnp.int32, (8, check_ref.shape[1]), 0)
    tail = jnp.where(line == 0, check_ref[...], jnp.where(line == 1, 1.0, 0.0))
    tail_ref[...] = mm(split(tail), parts, NN)
    half, rows = STEPS // 2, window_ref.shape[0] // STEPS
    for step in range(STEPS):
        block_copy(window_ref, buf, sems, step).wait()
        x = mm(split(buf[step * rows : (step + 1) * rows]), parts, NN)
        part = slice(step % half * rows, (step % half + 1) * rows)

        @pl.when(where_ref[2] == step // half)
        def _():
            keep_ref[part] = x

        @pl.when(where_ref[2] != step // half)
        def _():
            send_ref[part] = x


def cols_call(where, own, far, check, window):
    n_rows, n_cols = window.shape
    kdim = own.shape[2]
    return pl.pallas_call(
        cols_kernel,
        in_specs=[SMEM, VMEM, VMEM, VMEM, HBM],
        out_specs=[VMEM] * 4,
        out_shape=[f32(n_cols, kdim), f32(n_rows // 2, kdim), f32(n_rows // 2, kdim), f32(8, kdim)],
        scratch_shapes=[pltpu.VMEM((n_rows, n_cols), jnp.float32), pltpu.SemaphoreType.DMA((STEPS,))],
        name="cols",
    )(where, own, far, check.reshape(1, n_cols), window)


def left_kernel(where_ref, own_ref, far_ref, c_ref, u_ref, vec_ref, row_ref, col_ref, window_ref, nrow_ref, ncol_ref, out_ref, buf, sems, done):
    for step in range(STEPS):
        block_copy(window_ref, buf, sems, step).start()
    c_parts = split(c_ref[...])
    vec = vec_ref[...]
    turned = mm(split(vec), split(u_ref[...]), NN)
    ncol_ref[...] = col_ref[...] - mm(split(turned), c_parts, NT)[1:2]
    vec_parts = split(vec)
    half, rows = STEPS // 2, window_ref.shape[0] // STEPS
    lead = jnp.where(where_ref[0] == 0, 1.0, 0.0)
    for step in range(STEPS):
        piece = slice(step % half * rows, (step % half + 1) * rows)
        mine = lead if step < half else 1.0 - lead
        y_parts = split(jnp.where(mine > 0.5, own_ref[piece], far_ref[piece]))
        part = slice(step * rows, (step + 1) * rows)
        out = mm(y_parts, c_parts, NT)
        block_copy(window_ref, buf, sems, step).wait()
        buf[part] = buf[part] - out
        block_copy(buf, out_ref, done, step).start()
        nrow_ref[:, part] = row_ref[:, part] - mm(vec_parts, y_parts, NT)[:1]
    for step in range(STEPS):
        block_copy(buf, out_ref, done, step).wait()


def left_call(where, own, far, v_cols, upper, vectors, row_check, col_check, window):
    n_rows, n_cols = window.shape
    return pl.pallas_call(
        left_kernel,
        in_specs=[SMEM] + [VMEM] * 7 + [HBM],
        out_specs=[VMEM, VMEM, HBM],
        out_shape=[f32(1, n_rows), f32(1, n_cols), f32(n_rows, n_cols)],
        scratch_shapes=[
            pltpu.VMEM((n_rows, n_cols), jnp.float32),
            pltpu.SemaphoreType.DMA((STEPS,)),
            pltpu.SemaphoreType.DMA((STEPS,)),
        ],
        name="left",
    )(where, own, far, v_cols, upper, vectors, row_check.reshape(1, n_rows), col_check.reshape(1, n_cols), window)


def right_kernel(v_ref, g_ref, u_ref, vec_ref, row_ref, col_ref, window_ref, nrow_ref, ncol_ref, out_ref, buf, sems, done):
    for step in range(STEPS):
        block_copy(window_ref, buf, sems, step).start()
    n_cols = window_ref.shape[1]
    kdim = u_ref.shape[0]
    upper = split(u_ref[...])
    g_all = g_ref[...]
    m_parts = split(mm(upper, split(g_all[:, :n_cols]), TN))
    ncol_ref[...] = col_ref[...] - mm(split(vec_ref[...]), m_parts, NN)[:1]
    lanes = g_all.shape[1] - n_cols
    extra = jnp.sum(g_all[:, n_cols:].reshape(16, kdim // 16, lanes), axis=0)
    inner = jnp.concatenate([extra[i : i + 1] for i in range(kdim // lanes)], axis=1)
    inner = split(mm(split(jnp.broadcast_to(inner, (8, kdim))), upper, NN))
    rows = window_ref.shape[0] // STEPS
    for step in range(STEPS):
        part = slice(step * rows, (step + 1) * rows)
        v_parts = split(v_ref[part])
        out = mm(v_parts, m_parts, NN)
        block_copy(window_ref, buf, sems, step).wait()
        buf[part] = buf[part] - out
        block_copy(buf, out_ref, done, step).start()
        nrow_ref[:, part] = row_ref[:, part] - mm(inner, v_parts, NT)[:1]
    for step in range(STEPS):
        block_copy(buf, out_ref, done, step).wait()


def right_call(v_rows, g_all, upper, vectors, row_part, col_part, window):
    n_rows, n_cols = window.shape
    return pl.pallas_call(
        right_kernel,
        in_specs=[VMEM] * 6 + [HBM],
        out_specs=[VMEM, VMEM, HBM],
        out_shape=[f32(1, n_rows), f32(1, n_cols), f32(n_rows, n_cols)],
        scratch_shapes=[
            pltpu.VMEM((n_rows, n_cols), jnp.float32),
            pltpu.SemaphoreType.DMA((STEPS,)),
            pltpu.SemaphoreType.DMA((STEPS,)),
        ],
        name="right",
    )(v_rows, g_all, upper, vectors, row_part, col_part, window)


def on_device(window, panel, factor, col_check, row_check):
    y, zh, core = lax.axis_index("y"), lax.axis_index("zh"), lax.axis_index("core")
    x, zl = lax.axis_index("x"), lax.axis_index("zl")
    prow = y * 4 + zh
    pcol = (x * 4 + zl) * 2 + core
    kdim = panel.shape[1]
    shard = panel.shape[0]
    n_rows, n_cols = window.shape
    upper = jnp.triu(factor)

    mine = gather(panel, ("x", "zl"), 16)
    quarter = lax.dynamic_slice_in_dim(mine, x // 2 * (n_cols // 2), n_cols // 2, 0)
    moved = lax.ppermute(quarter, AXES, transposition())
    other = swap(mine, "core", 2, 1)
    v_rows, w_part, row_part = rows_call(
        jnp.stack([core, prow * n_rows]).astype(jnp.int32),
        mine.reshape(-1, shard, kdim),
        other.reshape(-1, shard, kdim),
        window,
        row_check,
    )
    w_part = reduce_scatter(w_part, "y", 4)
    near = swap(moved, "y", 4, 1)
    w_slice = reduce_scatter(w_part, "zh", 4)

    k_rows = w_slice.shape[0]
    v_cols, keep, send, tail = cols_call(
        jnp.stack([y % 2, pcol * n_cols, core]).astype(jnp.int32),
        moved.reshape(-1, shard, kdim),
        near.reshape(-1, shard, kdim),
        col_check,
        window,
    )
    x_part = keep + swap(send, "core", 2, 1)
    small = jnp.concatenate([dot(w_slice, v_cols), tail], axis=0)
    x_part, small = reduce_both(x_part, small, "x", 4)
    x_slice, small = reduce_both(x_part, small, "zl", 4)
    small = small + swap(small, "core", 2, 1)
    p_slice, col_proj, sums = small[:k_rows], small[k_rows], small[k_rows + 1]
    scaled = sums / math.sqrt(N)
    vectors = jnp.concatenate([scaled[None], col_proj[None], jnp.zeros((6, kdim), jnp.float32)], axis=0)

    y_rows = dot(x_slice, upper)
    y_rows = double(y_rows, "zl", 4, 1)
    y_rows = double(y_rows, "zl", 4, 2)
    y_rows = gather(y_rows, "x", 4)
    y_far = swap(y_rows, "core", 2, 1)

    z_slice = dot(p_slice, upper)
    g_slice = w_slice - dot(z_slice, v_cols, ((1,), (1,)))
    z_scaled = dot(scaled[None], z_slice, ((1,), (1,)))
    lanes = 128
    owner = lax.broadcasted_iota(jnp.int32, (1, kdim), 1) // k_rows
    partial = row_part - jnp.where(owner == prow, jnp.tile(z_scaled, (1, kdim // k_rows)), 0.0)
    extra = jnp.pad(partial.reshape(kdim // lanes, lanes), ((0, k_rows - kdim // lanes), (0, 0)))
    g_all = gather(jnp.concatenate([g_slice, extra], axis=1), "zh", 4)
    g_all = gather(g_all, "y", 4)

    new_row, new_col, partly = left_call(
        core[None].astype(jnp.int32), y_rows, y_far, v_cols, upper, vectors, row_check, col_check, window
    )
    new_row, new_col, new_window = right_call(v_rows, g_all, upper, vectors, new_row, new_col, partly)
    return new_window, new_col.reshape(n_cols), new_row.reshape(n_rows)


def solution(mesh):
    fine = Mesh(mesh.devices.reshape(SIZES), AXES)
    rows, cols = ("y", "zh"), ("x", "zl", "core")
    placed = (P(rows, cols), P(AXES, None), P(), P(cols), P(rows))
    return jax.shard_map(
        on_device,
        mesh=fine,
        in_specs=placed,
        out_specs=(P(rows, cols), P(cols), P(rows)),
        check_vma=False,
    )
```

time: 212 us -> 203 us (0.958)
  blocking collectives: 73.9 us -> 35.3 us
  starting transfers between devices: 43.8 us -> 72.1 us
  Pallas kernels: 0 us -> 23.6 us
  matrix products: 20.1 us -> 1.02 us
    all_to_all x5 -> x2, blocking collectives: 73.9 us -> 35.3 us  [exchange(): return lax.all_to_all(parts, axis, 0, 0)]
    pallas_call x0 -> x4, Pallas kernels: none -> 23.6 us  [the longest x1 6.53 us: right_call(): pl.pallas_call(right_kernel, in_specs=[VMEM] * 6 + [HBM], out_specs=[VMEM...]
    dot_general x15 -> x5, matrix products: 20.1 us -> 1.02 us  [dot(): return lax.dot_general(left, right, (dims, ((), ())), precision=PREC)]
    all_to_all x6, waiting for transfers between devices: 54.6 us -> 37.3 us  [exchange(): return lax.all_to_all(parts, axis, 0, 0)]
    ppermute x2 -> x8, waiting for transfers between devices: 1.86 us -> 18.5 us  [the longest x1 12.2 us: on_device(): moved = lax.ppermute(quarter, AXES, transposition())]
    ppermute x2 -> x8, starting transfers between devices: 8.78 us -> 23.9 us  [the longest x7 16.8 us: swap(): return lax.ppermute(block, axis, [(i, i ^ bit) for i in range(size)])]
    all_to_all x6, starting transfers between devices: 35.1 us -> 48.3 us  [exchange(): return lax.all_to_all(parts, axis, 0, 0)]
    reshape x2 -> x0, local copies, waits for them, and re-layouts: 2.86 us -> none  [the longest x1 1.55 us: on_device(): v_rows = jnp.concatenate([first, second], axis=1).reshape(n_rows, kdim)]
  transfers between devices with their start and end apart: 8 -> 14, of which waited for: 7 -> 8; matrix products, arithmetic and copies ran while one was open for 7% -> 3% of each run, Pallas kernels for 0% -> 9%
where the time goes in v2:
time: 203 us; the launch traced here: 200 us
  starting transfers between devices  72.1 us (36%)
  waiting for transfers between devices  55.8 us (27%)
  blocking collectives  35.3 us (17%)
  Pallas kernels  23.6 us (12%)
  local copies, waits for them, and re-layouts  6.72 us (3%)
  other arithmetic  4.63 us (2%)
    all_to_all x6, starting transfers between devices, exchange(): return lax.all_to_all(parts, axis, 0, 0)  48.3 us
    all_to_all x6, waiting for transfers between devices, exchange(): return lax.all_to_all(parts, axis, 0, 0)  37.3 us
    all_to_all x2, blocking collectives, exchange(): return lax.all_to_all(parts, axis, 0, 0)  35.3 us
    ppermute x7, starting transfers between devices, swap(): return lax.ppermute(block, axis, [(i, i ^ bit) for i in range(size)])  16.8 us
    ppermute x1, waiting for transfers between devices, on_device(): moved = lax.ppermute(quarter, AXES, transposition())  12.2 us
    ppermute x1, starting transfers between devices, on_device(): moved = lax.ppermute(quarter, AXES, transposition())  7.02 us
    pallas_call x1, Pallas kernels, right_call(): pl.pallas_call(right_kernel, in_specs=[VMEM] * 6 + [HBM], out_specs=[VMEM...  6.53 us
    pallas_call x1, Pallas kernels, left_call(): pl.pallas_call(left_kernel, in_specs=[SMEM] + [VMEM] * 7 + [HBM], out_spe...  6.37 us
  transfers between devices with their start and end apart: 14, of which 8 were waited for; matrix products, arithmetic and copies ran while one was open for 3% of the time, Pallas kernels for 9%

profile of v2, /device:TPU:6, one launch (start us, length us, event | category | flops | bytes accessed | tf_op | source)
XLA Modules:
  0.0 200.3 jit_solution(17173434366761159654)
XLA Ops:
  1.4 22.9 %all_to_all.40.mine_ref = f32[16,32,256]{2,1,0:T(8,128)S(1)} all-to-all(f32[16,32,256]{2,1,0:T(8,128)S(1)} %broadcast_in_dim.67), channel_id=1, replica_groups=mesh['y'=4,'zh'=4,'x'=4,'zl'=4,'core'=2] {'x','zl'}, dimensions={0} | all-to-all | bytes 1048576 | tf_op jit(solution)/shard_map/all_to_all | solution.py:28
  26.3 7.0 %collective-permute-start.1 = (f32[256,256]{1,0:T(8,128)S(1)}, f32[256,256]{1,0:T(8,128)S(1)}, u32[]{:S(2)}, u32[]{:S(2)}) collective-permute-start(f32[256,256]{1,0:T(8,128)S(1)} %constant_dynamic-slice_fusion), channel_id=1, source_target_pairs={{0,0},{1,128},{2,32},{3,160},{4,64},{5,192},{6,96},{7,224},{8,256}... | collective-permute-start | bytes 786440 | tf_op jit(solution)/shard_map/ppermute | solution.py:291
  33.9 12.2 %collective-permute-done.1 = f32[256,256]{1,0:T(8,128)S(1)} collective-permute-done((f32[256,256]{1,0:T(8,128)S(1)}, f32[256,256]{1,0:T(8,128)S(1)}, u32[]{:S(2)}, u32[]{:S(2)}) %collective-permute-start.1) | collective-permute-done | bytes 262176 | tf_op jit(solution)/shard_map/ppermute | solution.py:291
  46.1 2.9 %collective-permute-start.2 = (f32[256,256]{1,0:T(8,128)S(1)}, f32[256,256]{1,0:T(8,128)S(1)}, u32[]{:S(2)}, u32[]{:S(2)}) collective-permute-start(f32[256,256]{1,0:T(8,128)S(1)} %collective-permute-done.1), channel_id=1, source_target_pairs={{0,128},{128,0},{256,384},{384,256},{1,129},{129,1},{257,385},{385... | collective-permute-start | bytes 786440 | tf_op jit(solution)/shard_map/ppermute | solution.py:50
  49.9 5.3 %rows.1 = (f32[1024,256]{1,0:T(8,128)}, f32[256,512]{1,0:T(8,128)}, f32[1,256]{1,0:T(1,128)}) custom-call(s32[2]{0:T(128)} %pad_add_fusion.where_ref, f32[16,32,256]{2,1,0:T(8,128)} %copy-done.2, f32[16,32,256]{2,1,0:T(8,128)} %bitcast.54, f32[1,1024]{1,0:T(1,128)} %bitcast.59, f32[1024,512]{1,0:T(8,128)} %window_ref.5), custom_call_target="tpu_custom_call" | custom-call | tf_op jit(solution)/shard_map/rows/pallas_call | solution.py:149
  55.1 3.5 %all-to-all-start.1 = ((f32[4,64,512]{2,1,0:T(8,128)}), f32[4,64,512]{2,1,0:T(8,128)S(1)}, u32[]{:S(2)}, u32[]{:S(2)}) async-start(f32[4,64,512]{2,1,0:T(8,128)} %bitcast.53), calls=%async_computation.1 | async-start | bytes 1048576 | tf_op jit(solution)/shard_map/all_to_all | solution.py:28
  60.0 5.5 %cols.1 = (f32[512,256]{1,0:T(8,128)}, f32[512,256]{1,0:T(8,128)}, f32[512,256]{1,0:T(8,128)}, f32[8,256]{1,0:T(8,128)}) custom-call(s32[3]{0:T(128)} %pad_add_fusion.1.where_ref, f32[8,32,256]{2,1,0:T(8,128)} %bitcast.55, f32[8,32,256]{2,1,0:T(8,128)} %bitcast.56, f32[1,512]{1,0:T(1,128)} %bitcast.61, f32[1024,512]{1,0:T(8,128)} %window_ref.5), custom_call_target="tpu_custom_call" | custom-call | tf_op jit(solution)/shard_map/cols/pallas_call | solution.py:187
  65.5 2.1 %collective-permute-start.3 = (f32[512,256]{1,0:T(8,128)}, f32[512,256]{1,0:T(8,128)S(1)}, u32[]{:S(2)}, u32[]{:S(2)}) collective-permute-start(f32[512,256]{1,0:T(8,128)} %get-tuple-element.19), channel_id=1, source_target_pairs={{0,1},{1,0},{2,3},{3,2},{4,5},{5,4},{6,7},{7,6},{8,9},{9,8},{10,11... | collective-permute-start | bytes 1572872 | tf_op jit(solution)/shard_map/ppermute | solution.py:50
  68.3 26.5 %all-to-all-start.2 = ((f32[4,16,512]{2,1,0:T(8,128)}), f32[4,16,512]{2,1,0:T(8,128)S(1)}, u32[]{:S(2)}, u32[]{:S(2)}) async-start(f32[4,16,512]{2,1,0:T(8,128)} %bitcast.6), calls=%async_computation.2 | async-start | bytes 262144 | tf_op jit(solution)/shard_map/all_to_all | solution.py:28
  95.9 12.7 %all-to-all-done.2 = f32[4,16,512]{2,1,0:T(8,128)S(1)} async-done(((f32[4,16,512]{2,1,0:T(8,128)}), f32[4,16,512]{2,1,0:T(8,128)S(1)}, u32[]{:S(2)}, u32[]{:S(2)}) %all-to-all-start.2) | async-done | bytes 131104 | tf_op jit(solution)/shard_map/all_to_all | solution.py:28
  109.0 12.4 %all_to_all.41 = f32[4,152,256]{2,1,0:T(8,128)S(1)} all-to-all(f32[4,152,256]{2,1,0:T(8,128)S(1)} %pad_maximum_fusion), channel_id=1, replica_groups=mesh['y'=4,'zh'=4,'x'=4,'zl'=4,'core'=2] {'x'}, dimensions={0} | all-to-all | bytes 1245184 | tf_op jit(solution)/shard_map/all_to_all | solution.py:28
  122.2 3.5 %all-to-all-start.4 = ((f32[4,56,256]{2,1,0:T(8,128)}), f32[4,56,256]{2,1,0:T(8,128)S(1)}, u32[]{:S(2)}, u32[]{:S(2)}) async-start(f32[4,56,256]{2,1,0:T(8,128)} %pad_maximum_fusion.1), calls=%async_computation.4 | async-start | bytes 458752 | tf_op jit(solution)/shard_map/all_to_all | solution.py:28
  125.9 6.3 %all-to-all-done.4 = f32[4,56,256]{2,1,0:T(8,128)S(1)} async-done(((f32[4,56,256]{2,1,0:T(8,128)}), f32[4,56,256]{2,1,0:T(8,128)S(1)}, u32[]{:S(2)}, u32[]{:S(2)}) %all-to-all-start.4) | async-done | bytes 229408 | tf_op jit(solution)/shard_map/all_to_all | solution.py:28
  134.4 3.4 %collective-permute-start.5 = (f32[32,256]{1,0:T(8,128)S(1)}, f32[32,256]{1,0:T(8,128)S(1)}, u32[]{:S(2)}, u32[]{:S(2)}) collective-permute-start(f32[32,256]{1,0:T(8,128)S(1)} %get-tuple-element.32), channel_id=1, source_target_pairs={{0,2},{2,0},{4,6},{6,4},{1,3},{3,1},{5,7},{7,5},{8,10},{10,8},{12,... | collective-permute-start | bytes 98312 | tf_op jit(solution)/shard_map/ppermute | solution.py:50
  138.2 2.0 collective-permute-done.5
  140.2 2.7 %collective-permute-start.6 = (f32[64,256]{1,0:T(8,128)S(1)}, f32[64,256]{1,0:T(8,128)S(1)}, u32[]{:S(2)}, u32[]{:S(2)}) collective-permute-start(f32[64,256]{1,0:T(8,128)S(1)} %bitcast.57), channel_id=1, source_target_pairs={{0,4},{2,6},{4,0},{6,2},{1,5},{3,7},{5,1},{7,3},{8,12},{10,14},{12... | collective-permute-start | bytes 196616 | tf_op jit(solution)/shard_map/ppermute | solution.py:50
  143.0 4.3 %collective-permute-done.6 = f32[64,256]{1,0:T(8,128)S(1)} collective-permute-done((f32[64,256]{1,0:T(8,128)S(1)}, f32[64,256]{1,0:T(8,128)S(1)}, u32[]{:S(2)}, u32[]{:S(2)}) %collective-permute-start.6) | collective-permute-done | bytes 65568 | tf_op jit(solution)/shard_map/ppermute | solution.py:50
  148.1 5.5 %all-to-all-start.7 = ((f32[4,128,256]{2,1,0:T(8,128)}), f32[4,128,256]{2,1,0:T(8,128)S(1)}, u32[]{:S(2)}, u32[]{:S(2)}) async-start(f32[4,128,256]{2,1,0:T(8,128)} %broadcast_in_dim.82), calls=%async_computation.7 | async-start | bytes 1048576 | tf_op jit(solution)/shard_map/all_to_all | solution.py:28
  154.0 5.7 %all-to-all-done.7 = f32[4,128,256]{2,1,0:T(8,128)S(1)} async-done(((f32[4,128,256]{2,1,0:T(8,128)}), f32[4,128,256]{2,1,0:T(8,128)S(1)}, u32[]{:S(2)}, u32[]{:S(2)}) %all-to-all-start.7) | async-done | bytes 524320 | tf_op jit(solution)/shard_map/all_to_all | solution.py:28
  160.5 4.5 %all-to-all-start.5 = ((f32[4,16,640]{2,1,0:T(8,128)}), f32[4,16,640]{2,1,0:T(8,128)S(1)}, u32[]{:S(2)}, u32[]{:S(2)}) async-start(f32[4,16,640]{2,1,0:T(8,128)} %broadcast_in_dim.72), calls=%async_computation.5 | async-start | bytes 327680 | tf_op jit(solution)/shard_map/all_to_all | solution.py:28
  166.8 11.7 %all-to-all-done.5 = f32[4,16,640]{2,1,0:T(8,128)S(1)} async-done(((f32[4,16,640]{2,1,0:T(8,128)}), f32[4,16,640]{2,1,0:T(8,128)S(1)}, u32[]{:S(2)}, u32[]{:S(2)}) %all-to-all-start.5) | async-done | bytes 163872 | tf_op jit(solution)/shard_map/all_to_all | solution.py:28
  179.4 4.7 %all-to-all-start.6 = ((f32[4,64,640]{2,1,0:T(8,128)}), f32[4,64,640]{2,1,0:T(8,128)S(1)}, u32[]{:S(2)}, u32[]{:S(2)}) async-start(f32[4,64,640]{2,1,0:T(8,128)} %broadcast_in_dim.74), calls=%async_computation.6 | async-start | bytes 1310720 | tf_op jit(solution)/shard_map/all_to_all | solution.py:28
  185.7 6.4 %left.1 = (f32[1,1024]{1,0:T(1,128)}, f32[1,512]{1,0:T(1,128)}, f32[1024,512]{1,0:T(8,128)}) custom-call(s32[1]{0:T(128)} %bitcast.where_ref, f32[512,256]{1,0:T(8,128)} %bitcast.48, f32[512,256]{1,0:T(8,128)} %copy-done.5, f32[512,256]{1,0:T(8,128)} %get-tuple-element.20.c_ref, f32[256,256]{1,0:T(8,128)} %copy-done, f32[8,256]{1,0:T(8,128)} %maximum_maximum_fusion.vec_ref, ...), custom_call_target="tpu_custom_call" | custom-call | tf_op jit(solution)/shard_map/left/pallas_call | solution.py:223
  193.8 6.5 %right.1 = (f32[1,1024]{1,0:T(1,128)}, f32[1,512]{1,0:T(1,128)}, f32[1024,512]{1,0:T(8,128)}) custom-call(f32[1024,256]{1,0:T(8,128)} %get-tuple-element.16.v_ref, f32[256,640]{1,0:T(8,128)} %bitcast.46, f32[256,256]{1,0:T(8,128)} %copy-done, f32[8,256]{1,0:T(8,128)} %maximum_maximum_fusion.vec_ref, f32[1,1024]{1,0:T(1,128)} %get-tuple-element.23.row_ref, ...), custom_call_target="tpu_custom_call" | custom-call | tf_op jit(solution)/shard_map/right/pallas_call | solution.py:265
  (75 shorter events, 19.0 us)
Async XLA Ops:
  24.3 24.8 %copy-start.2 = (f32[16,32,256]{2,1,0:T(8,128)}, f32[16,32,256]{2,1,0:T(8,128)S(1)}, u32[]{:S(2)}) copy-start(f32[16,32,256]{2,1,0:T(8,128)S(1)} %all_to_all.40.mine_ref) | copy-start | bytes 1572868
  24.3 24.7 %collective-permute-start = (f32[512,256]{1,0:T(8,128)S(1)}, f32[512,256]{1,0:T(8,128)S(1)}, u32[]{:S(2)}, u32[]{:S(2)}) collective-permute-start(f32[512,256]{1,0:T(8,128)S(1)} %bitcast.44), channel_id=1, source_target_pairs={{0,1},{1,0},{2,3},{3,2},{4,5},{5,4},{6,7},{7,6},{8,9},{9,8},{10,11... | collective-permute-start | bytes 1572872 | tf_op jit(solution)/shard_map/ppermute | solution.py:50
  26.3 19.8 %collective-permute-start.1 = (f32[256,256]{1,0:T(8,128)S(1)}, f32[256,256]{1,0:T(8,128)S(1)}, u32[]{:S(2)}, u32[]{:S(2)}) collective-permute-start(f32[256,256]{1,0:T(8,128)S(1)} %constant_dynamic-slice_fusion), channel_id=1, source_target_pairs={{0,0},{1,128},{2,32},{3,160},{4,64},{5,192},{6,96},{7,224},{8,256}... | collective-permute-start | bytes 786440 | tf_op jit(solution)/shard_map/ppermute | solution.py:291
  46.1 13.2 %copy-start.7 = (f32[256,256]{1,0:T(8,128)}, f32[256,256]{1,0:T(8,128)S(1)}, u32[]{:S(2)}) copy-start(f32[256,256]{1,0:T(8,128)S(1)} %collective-permute-done.1) | copy-start | bytes 786436
  46.1 13.2 %collective-permute-start.2 = (f32[256,256]{1,0:T(8,128)S(1)}, f32[256,256]{1,0:T(8,128)S(1)}, u32[]{:S(2)}, u32[]{:S(2)}) collective-permute-start(f32[256,256]{1,0:T(8,128)S(1)} %collective-permute-done.1), channel_id=1, source_target_pairs={{0,128},{128,0},{256,384},{384,256},{1,129},{129,1},{257,385},{385... | collective-permute-start | bytes 786440 | tf_op jit(solution)/shard_map/ppermute | solution.py:50
  55.1 12.4 %all-to-all-start.1 = ((f32[4,64,512]{2,1,0:T(8,128)}), f32[4,64,512]{2,1,0:T(8,128)S(1)}, u32[]{:S(2)}, u32[]{:S(2)}) async-start(f32[4,64,512]{2,1,0:T(8,128)} %bitcast.53), calls=%async_computation.1 | async-start | bytes 1048576 | tf_op jit(solution)/shard_map/all_to_all | solution.py:28
  65.5 43.2 %copy-start.1 = (f32[512,256]{1,0:T(8,128)S(1)}, f32[512,256]{1,0:T(8,128)}, u32[]{:S(2)}) copy-start(f32[512,256]{1,0:T(8,128)} %get-tuple-element.20.c_ref) | copy-start | bytes 1572868
  65.5 43.4 %copy-start.10 = (f32[8,256]{1,0:T(8,128)S(1)}, f32[8,256]{1,0:T(8,128)}, u32[]{:S(2)}) copy-start(f32[8,256]{1,0:T(8,128)} %get-tuple-element.21) | copy-start | bytes 24580
  65.5 29.3 %collective-permute-start.3 = (f32[512,256]{1,0:T(8,128)}, f32[512,256]{1,0:T(8,128)S(1)}, u32[]{:S(2)}, u32[]{:S(2)}) collective-permute-start(f32[512,256]{1,0:T(8,128)} %get-tuple-element.19), channel_id=1, source_target_pairs={{0,1},{1,0},{2,3},{3,2},{4,5},{5,4},{6,7},{7,6},{8,9},{9,8},{10,11... | collective-permute-start | bytes 1572872 | tf_op jit(solution)/shard_map/ppermute | solution.py:50
  68.3 40.4 %all-to-all-start.2 = ((f32[4,16,512]{2,1,0:T(8,128)}), f32[4,16,512]{2,1,0:T(8,128)S(1)}, u32[]{:S(2)}, u32[]{:S(2)}) async-start(f32[4,16,512]{2,1,0:T(8,128)} %bitcast.6), calls=%async_computation.2 | async-start | bytes 262144 | tf_op jit(solution)/shard_map/all_to_all | solution.py:28
  108.9 16.9 %copy-start.9 = (f32[256,256]{1,0:T(8,128)S(1)}, f32[256,256]{1,0:T(8,128)}, u32[]{:S(2)}) copy-start(f32[256,256]{1,0:T(8,128)} %param.7) | copy-start | bytes 786436
  122.2 31.4 %copy-start.11 = (f32[1,256]{1,0:T(1,128)S(1)}, f32[1,256]{1,0:T(1,128)}, u32[]{:S(2)}) copy-start(f32[1,256]{1,0:T(1,128)} %get-tuple-element.22) | copy-start | bytes 3076
  122.2 10.0 %all-to-all-start.4 = ((f32[4,56,256]{2,1,0:T(8,128)}), f32[4,56,256]{2,1,0:T(8,128)S(1)}, u32[]{:S(2)}, u32[]{:S(2)}) async-start(f32[4,56,256]{2,1,0:T(8,128)} %pad_maximum_fusion.1), calls=%async_computation.4 | async-start | bytes 458752 | tf_op jit(solution)/shard_map/all_to_all | solution.py:28
  125.9 34.5 %copy-start = (f32[256,256]{1,0:T(8,128)}, f32[256,256]{1,0:T(8,128)S(1)}, u32[]{:S(2)}) copy-start(f32[256,256]{1,0:T(8,128)S(1)} %fusion.u_ref) | copy-start | bytes 786436
  132.3 5.5 %collective-permute-start.4 = (f32[24,256]{1,0:T(8,128)S(1)}, f32[24,256]{1,0:T(8,128)S(1)}, u32[]{:S(2)}, u32[]{:S(2)}) collective-permute-start(f32[24,256]{1,0:T(8,128)S(1)} %slice.30), channel_id=1, source_target_pairs={{0,1},{1,0},{2,3},{3,2},{4,5},{5,4},{6,7},{7,6},{8,9},{9,8},{10,11... | collective-permute-start | bytes 73736 | tf_op jit(solution)/shard_map/ppermute | solution.py:50
  134.4 5.8 %collective-permute-start.5 = (f32[32,256]{1,0:T(8,128)S(1)}, f32[32,256]{1,0:T(8,128)S(1)}, u32[]{:S(2)}, u32[]{:S(2)}) collective-permute-start(f32[32,256]{1,0:T(8,128)S(1)} %get-tuple-element.32), channel_id=1, source_target_pairs={{0,2},{2,0},{4,6},{6,4},{1,3},{3,1},{5,7},{7,5},{8,10},{10,8},{12,... | collective-permute-start | bytes 98312 | tf_op jit(solution)/shard_map/ppermute | solution.py:50
  140.2 7.0 %collective-permute-start.6 = (f32[64,256]{1,0:T(8,128)S(1)}, f32[64,256]{1,0:T(8,128)S(1)}, u32[]{:S(2)}, u32[]{:S(2)}) collective-permute-start(f32[64,256]{1,0:T(8,128)S(1)} %bitcast.57), channel_id=1, source_target_pairs={{0,4},{2,6},{4,0},{6,2},{1,5},{3,7},{5,1},{7,3},{8,12},{10,14},{12... | collective-permute-start | bytes 196616 | tf_op jit(solution)/shard_map/ppermute | solution.py:50
  148.1 11.6 %all-to-all-start.7 = ((f32[4,128,256]{2,1,0:T(8,128)}), f32[4,128,256]{2,1,0:T(8,128)S(1)}, u32[]{:S(2)}, u32[]{:S(2)}) async-start(f32[4,128,256]{2,1,0:T(8,128)} %broadcast_in_dim.82), calls=%async_computation.7 | async-start | bytes 1048576 | tf_op jit(solution)/shard_map/all_to_all | solution.py:28
  159.7 25.2 %copy-start.4 = (f32[4,128,256]{2,1,0:T(8,128)}, f32[4,128,256]{2,1,0:T(8,128)S(1)}, u32[]{:S(2)}) copy-start(f32[4,128,256]{2,1,0:T(8,128)S(1)} %all-to-all-done.7) | copy-start | bytes 1572868
  160.5 18.1 %all-to-all-start.5 = ((f32[4,16,640]{2,1,0:T(8,128)}), f32[4,16,640]{2,1,0:T(8,128)S(1)}, u32[]{:S(2)}, u32[]{:S(2)}) async-start(f32[4,16,640]{2,1,0:T(8,128)} %broadcast_in_dim.72), calls=%async_computation.5 | async-start | bytes 327680 | tf_op jit(solution)/shard_map/all_to_all | solution.py:28
  164.9 20.0 %collective-permute-start.7 = (f32[512,256]{1,0:T(8,128)S(1)}, f32[512,256]{1,0:T(8,128)S(1)}, u32[]{:S(2)}, u32[]{:S(2)}) collective-permute-start(f32[512,256]{1,0:T(8,128)S(1)} %bitcast.47), channel_id=1, source_target_pairs={{0,1},{1,0},{2,3},{3,2},{4,5},{5,4},{6,7},{7,6},{8,9},{9,8},{10,11... | collective-permute-start | bytes 1572872 | tf_op jit(solution)/shard_map/ppermute | solution.py:50
  179.4 13.5 %all-to-all-start.6 = ((f32[4,64,640]{2,1,0:T(8,128)}), f32[4,64,640]{2,1,0:T(8,128)S(1)}, u32[]{:S(2)}, u32[]{:S(2)}) async-start(f32[4,64,640]{2,1,0:T(8,128)} %broadcast_in_dim.74), calls=%async_computation.6 | async-start | bytes 1310720 | tf_op jit(solution)/shard_map/all_to_all | solution.py:28
  184.9 0.8 copy-start.5
  192.9 0.8 copy-start.3
  (2 other events, 1.5 us)

commit v3 on v2

--- a/solution.py
+++ b/solution.py
@@ -48,22 +48,6 @@
 
 def swap(block, axis, size, bit):
     return lax.ppermute(block, axis, [(i, i ^ bit) for i in range(size)])
-
-
-def ordered(mine, other, bit, axis):
-    own = jnp.expand_dims(mine, axis)
-    far = jnp.expand_dims(other, axis)
-    shape = own.shape[:axis] + (2,) + own.shape[axis + 1 :]
-    out = jnp.zeros(shape, mine.dtype)
-    out = lax.dynamic_update_slice(out, own, [bit if i == axis else 0 for i in range(len(shape))])
-    return lax.dynamic_update_slice(out, far, [1 - bit if i == axis else 0 for i in range(len(shape))])
-
-
-def double(block, axis, size, bit):
-    index = lax.axis_index(axis)
-    other = swap(block, axis, size, bit)
-    out = ordered(block, other, (index & bit) // bit, 0)
-    return out.reshape((2 * block.shape[0],) + block.shape[1:])
 
 
 def transposition():
@@ -105,7 +89,11 @@
 
 
 def f32(*shape):
-    return jax.ShapeDtypeStruct(shape, jnp.float32)
+    return pltpu.VMEM(shape, jnp.float32)
+
+
+def vmem(value):
+    return pltpu.with_memory_space_constraint(value, pltpu.VMEM)
 
 
 def block_copy(src, dst, sems, step):
@@ -153,7 +141,7 @@
         out_shape=[f32(n_rows, kdim), f32(kdim, n_cols), f32(1, kdim)],
         scratch_shapes=[pltpu.VMEM((n_rows, n_cols), jnp.float32), pltpu.SemaphoreType.DMA((STEPS,))],
         name="rows",
-    )(where, mine, other, check.reshape(1, n_rows), window)
+    )(where, vmem(mine), vmem(other), check.reshape(1, n_rows), window)
 
 
 def cols_kernel(where_ref, own_ref, far_ref, check_ref, window_ref, v_ref, keep_ref, send_ref, tail_ref, buf, sems):
@@ -191,7 +179,7 @@
         out_shape=[f32(n_cols, kdim), f32(n_rows // 2, kdim), f32(n_rows // 2, kdim), f32(8, kdim)],
         scratch_shapes=[pltpu.VMEM((n_rows, n_cols), jnp.float32), pltpu.SemaphoreType.DMA((STEPS,))],
         name="cols",
-    )(where, own, far, check.reshape(1, n_cols), window)
+    )(where, vmem(own), vmem(far), check.reshape(1, n_cols), window)
 
 
 def left_kernel(where_ref, own_ref, far_ref, c_ref, u_ref, vec_ref, row_ref, col_ref, window_ref, nrow_ref, ncol_ref, out_ref, buf, sems, done):
@@ -224,14 +212,14 @@
         left_kernel,
         in_specs=[SMEM] + [VMEM] * 7 + [HBM],
         out_specs=[VMEM, VMEM, HBM],
-        out_shape=[f32(1, n_rows), f32(1, n_cols), f32(n_rows, n_cols)],
+        out_shape=[f32(1, n_rows), f32(1, n_cols), jax.ShapeDtypeStruct((n_rows, n_cols), jnp.float32)],
         scratch_shapes=[
             pltpu.VMEM((n_rows, n_cols), jnp.float32),
             pltpu.SemaphoreType.DMA((STEPS,)),
             pltpu.SemaphoreType.DMA((STEPS,)),
         ],
         name="left",
-    )(where, own, far, v_cols, upper, vectors, row_check.reshape(1, n_rows), col_check.reshape(1, n_cols), window)
+    )(where, vmem(own), vmem(far), v_cols, upper, vectors, row_check.reshape(1, n_rows), col_check.reshape(1, n_cols), window)
 
 
 def right_kernel(v_ref, g_ref, u_ref, vec_ref, row_ref, col_ref, window_ref, nrow_ref, ncol_ref, out_ref, buf, sems, done):
@@ -266,14 +254,14 @@
         right_kernel,
         in_specs=[VMEM] * 6 + [HBM],
         out_specs=[VMEM, VMEM, HBM],
-        out_shape=[f32(1, n_rows), f32(1, n_cols), f32(n_rows, n_cols)],
+        out_shape=[jax.ShapeDtypeStruct(shape, jnp.float32) for shape in ((1, n_rows), (1, n_cols), (n_rows, n_cols))],
         scratch_shapes=[
             pltpu.VMEM((n_rows, n_cols), jnp.float32),
             pltpu.SemaphoreType.DMA((STEPS,)),
             pltpu.SemaphoreType.DMA((STEPS,)),
         ],
         name="right",
-    )(v_rows, g_all, upper, vectors, row_part, col_part, window)
+    )(v_rows, vmem(g_all), upper, vectors, vmem(row_part), vmem(col_part), window)
 
 
 def on_device(window, panel, factor, col_check, row_check):
@@ -312,18 +300,16 @@
     x_part = keep + swap(send, "core", 2, 1)
     small = jnp.concatenate([dot(w_slice, v_cols), tail], axis=0)
     x_part, small = reduce_both(x_part, small, "x", 4)
-    x_slice, small = reduce_both(x_part, small, "zl", 4)
+    both = jnp.concatenate([x_part, small], axis=0)
+    total = jnp.sum(gather(both, "zl", 4).reshape((4,) + both.shape), axis=0)
+    x_rows, small = total[: x_part.shape[0]], total[x_part.shape[0] :]
+    y_rows = gather(dot(x_rows, upper), "x", 4)
+    y_far = swap(y_rows, "core", 2, 1)
+
     small = small + swap(small, "core", 2, 1)
     p_slice, col_proj, sums = small[:k_rows], small[k_rows], small[k_rows + 1]
     scaled = sums / math.sqrt(N)
     vectors = jnp.concatenate([scaled[None], col_proj[None], jnp.zeros((6, kdim), jnp.float32)], axis=0)
-
-    y_rows = dot(x_slice, upper)
-    y_rows = double(y_rows, "zl", 4, 1)
-    y_rows = double(y_rows, "zl", 4, 2)
-    y_rows = gather(y_rows, "x", 4)
-    y_far = swap(y_rows, "core", 2, 1)
-
     z_slice = dot(p_slice, upper)
     g_slice = w_slice - dot(z_slice, v_cols, ((1,), (1,)))
     z_scaled = dot(scaled[None], z_slice, ((1,), (1,)))

time: 203 us -> 201 us (level)
  waiting for transfers between devices: 55.8 us -> 64.6 us
  starting transfers between devices: 72.1 us -> 65.4 us
    all_to_all x6, waiting for transfers between devices: 37.3 us -> 52.3 us  [exchange(): return lax.all_to_all(parts, axis, 0, 0)]
    ppermute x7 -> x5, waiting for transfers between devices: 6.27 us -> 0.01 us  [swap(): return lax.ppermute(block, axis, [(i, i ^ bit) for i in range(size)])]
    ppermute x7 -> x5, starting transfers between devices: 16.8 us -> 10.6 us  [swap(): return lax.ppermute(block, axis, [(i, i ^ bit) for i in range(size)])]
  transfers between devices with their start and end apart: 14 -> 12, of which waited for: 8 -> 6; matrix products, arithmetic and copies ran while one was open for 3% -> 3% of each run, Pallas kernels for 9% -> 7%
where the time goes in v3:
time: 201 us; the launch traced here: 199 us
  starting transfers between devices  65.4 us (33%)
  waiting for transfers between devices  64.6 us (32%)
  blocking collectives  35.3 us (18%)
  Pallas kernels  21.6 us (11%)
  local copies, waits for them, and re-layouts  5.94 us (3%)
  other arithmetic  3.98 us (2%)
    all_to_all x6, waiting for transfers between devices, exchange(): return lax.all_to_all(parts, axis, 0, 0)  52.3 us
    all_to_all x6, starting transfers between devices, exchange(): return lax.all_to_all(parts, axis, 0, 0)  47.8 us
    all_to_all x2, blocking collectives, exchange(): return lax.all_to_all(parts, axis, 0, 0)  35.3 us
    ppermute x1, waiting for transfers between devices, on_device(): moved = lax.ppermute(quarter, AXES, transposition())  12.3 us
    ppermute x5, starting transfers between devices, swap(): return lax.ppermute(block, axis, [(i, i ^ bit) for i in range(size)])  10.6 us
    pallas_call x1, Pallas kernels, right_call(): pl.pallas_call(right_kernel, in_specs=[VMEM] * 6 + [HBM], out_specs=[VMEM...  7.06 us
    ppermute x1, starting transfers between devices, on_device(): moved = lax.ppermute(quarter, AXES, transposition())  7.02 us
    pallas_call x1, Pallas kernels, left_call(): pl.pallas_call(left_kernel, in_specs=[SMEM] + [VMEM] * 7 + [HBM], out_spe...  5.62 us
  transfers between devices with their start and end apart: 12, of which 6 were waited for; matrix products, arithmetic and copies ran while one was open for 3% of the time, Pallas kernels for 7%

profile of v3, /device:TPU:6, one launch (start us, length us, event | category | flops | bytes accessed | tf_op | source)
XLA Modules:
  0.0 198.8 jit_solution(16892950486335019660)
XLA Ops:
  1.4 22.9 %all_to_all.40.mine_ref = f32[16,32,256]{2,1,0:T(8,128)S(1)} all-to-all(f32[16,32,256]{2,1,0:T(8,128)S(1)} %broadcast_in_dim.24), channel_id=1, replica_groups=mesh['y'=4,'zh'=4,'x'=4,'zl'=4,'core'=2] {'x','zl'}, dimensions={0} | all-to-all | bytes 1048576 | tf_op jit(solution)/shard_map/all_to_all | solution.py:28
  24.3 1.9 collective-permute-start
  26.3 7.0 %collective-permute-start.1 = (f32[256,256]{1,0:T(8,128)S(1)}, f32[256,256]{1,0:T(8,128)S(1)}, u32[]{:S(2)}, u32[]{:S(2)}) collective-permute-start(f32[256,256]{1,0:T(8,128)S(1)} %constant_dynamic-slice_fusion), channel_id=1, source_target_pairs={{0,0},{1,128},{2,32},{3,160},{4,64},{5,192},{6,96},{7,224},{8,256}... | collective-permute-start | bytes 786440 | tf_op jit(solution)/shard_map/ppermute | solution.py:279
  33.9 12.3 %collective-permute-done.1 = f32[256,256]{1,0:T(8,128)S(1)} collective-permute-done((f32[256,256]{1,0:T(8,128)S(1)}, f32[256,256]{1,0:T(8,128)S(1)}, u32[]{:S(2)}, u32[]{:S(2)}) %collective-permute-start.1) | collective-permute-done | bytes 262176 | tf_op jit(solution)/shard_map/ppermute | solution.py:279
  46.1 2.9 %collective-permute-start.2 = (f32[256,256]{1,0:T(8,128)S(1)}, f32[256,256]{1,0:T(8,128)S(1)}, u32[]{:S(2)}, u32[]{:S(2)}) collective-permute-start(f32[256,256]{1,0:T(8,128)S(1)} %collective-permute-done.1), channel_id=1, source_target_pairs={{0,128},{128,0},{256,384},{384,256},{1,129},{129,1},{257,385},{385... | collective-permute-start | bytes 786440 | tf_op jit(solution)/shard_map/ppermute | solution.py:50
  49.1 4.7 %rows.1 = (f32[1024,256]{1,0:T(8,128)S(1)}, f32[256,512]{1,0:T(8,128)}, f32[1,256]{1,0:T(1,128)S(1)}) custom-call(s32[2]{0:T(128)} %pad_add_fusion.where_ref, f32[16,32,256]{2,1,0:T(8,128)S(1)} %all_to_all.40.mine_ref, f32[16,32,256]{2,1,0:T(8,128)S(1)} %bitcast.37, f32[1,1024]{1,0:T(1,128)} %bitcast.42, f32[1024,512]{1,0:T(8,128)} %window_ref.5), custom_call_target="tpu_custom_call" | custom-call | tf_op jit(solution)/shard_map/rows/pallas_call | solution.py:137
  53.8 4.2 %all-to-all-start.1 = ((f32[4,64,512]{2,1,0:T(8,128)}), f32[4,64,512]{2,1,0:T(8,128)}, u32[]{:S(2)}, u32[]{:S(2)}) async-start(f32[4,64,512]{2,1,0:T(8,128)} %bitcast.5), calls=%async_computation.1 | async-start | bytes 1048576 | tf_op jit(solution)/shard_map/all_to_all | solution.py:28
  60.3 4.1 %cols.1 = (f32[512,256]{1,0:T(8,128)S(1)}, f32[512,256]{1,0:T(8,128)S(1)}, f32[512,256]{1,0:T(8,128)S(1)}, f32[8,256]{1,0:T(8,128)S(1)}) custom-call(s32[3]{0:T(128)} %pad_add_fusion.1.where_ref, f32[8,32,256]{2,1,0:T(8,128)S(1)} %bitcast.38, f32[8,32,256]{2,1,0:T(8,128)S(1)} %bitcast.39, f32[1,512]{1,0:T(1,128)} %bitcast.44, f32[1024,512]{1,0:T(8,128)} %window_ref.5), custom_call_target="tpu_custom_call" | custom-call | tf_op jit(solution)/shard_map/cols/pallas_call | solution.py:175
  64.4 1.9 collective-permute-start.3
  68.1 26.5 %all-to-all-start.2 = ((f32[4,16,512]{2,1,0:T(8,128)}), f32[4,16,512]{2,1,0:T(8,128)S(1)}, u32[]{:S(2)}, u32[]{:S(2)}) async-start(f32[4,16,512]{2,1,0:T(8,128)} %bitcast.6), calls=%async_computation.2 | async-start | bytes 262144 | tf_op jit(solution)/shard_map/all_to_all | solution.py:28
  94.7 13.8 %all-to-all-done.2 = f32[4,16,512]{2,1,0:T(8,128)S(1)} async-done(((f32[4,16,512]{2,1,0:T(8,128)}), f32[4,16,512]{2,1,0:T(8,128)S(1)}, u32[]{:S(2)}, u32[]{:S(2)}) %all-to-all-start.2) | async-done | bytes 131104 | tf_op jit(solution)/shard_map/all_to_all | solution.py:28
  108.8 12.4 %all_to_all.41 = f32[4,152,256]{2,1,0:T(8,128)S(1)} all-to-all(f32[4,152,256]{2,1,0:T(8,128)S(1)} %pad_maximum_fusion), channel_id=1, replica_groups=mesh['y'=4,'zh'=4,'x'=4,'zl'=4,'core'=2] {'x'}, dimensions={0} | all-to-all | bytes 1245184 | tf_op jit(solution)/shard_map/all_to_all | solution.py:28
  122.2 3.5 %all-to-all-start.4 = ((f32[4,152,256]{2,1,0:T(8,128)}), f32[4,152,256]{2,1,0:T(8,128)S(1)}, u32[]{:S(2)}, u32[]{:S(2)}) async-start(f32[4,152,256]{2,1,0:T(8,128)} %broadcast_in_dim.26), calls=%async_computation.4 | async-start | bytes 1245184 | tf_op jit(solution)/shard_map/all_to_all | solution.py:28
  125.8 15.0 %all-to-all-done.4 = f32[4,152,256]{2,1,0:T(8,128)S(1)} async-done(((f32[4,152,256]{2,1,0:T(8,128)}), f32[4,152,256]{2,1,0:T(8,128)S(1)}, u32[]{:S(2)}, u32[]{:S(2)}) %all-to-all-start.4) | async-done | bytes 622624 | tf_op jit(solution)/shard_map/all_to_all | solution.py:28
  140.9 1.9 collective-permute-start.4
  143.9 5.5 %all-to-all-start.7 = ((f32[4,128,256]{2,1,0:T(8,128)}), f32[4,128,256]{2,1,0:T(8,128)S(1)}, u32[]{:S(2)}, u32[]{:S(2)}) async-start(f32[4,128,256]{2,1,0:T(8,128)} %broadcast_in_dim.60), calls=%async_computation.7 | async-start | bytes 1048576 | tf_op jit(solution)/shard_map/all_to_all | solution.py:28
  150.2 7.6 %all-to-all-done.7 = f32[4,128,256]{2,1,0:T(8,128)S(1)} async-done(((f32[4,128,256]{2,1,0:T(8,128)}), f32[4,128,256]{2,1,0:T(8,128)S(1)}, u32[]{:S(2)}, u32[]{:S(2)}) %all-to-all-start.7) | async-done | bytes 524320 | tf_op jit(solution)/shard_map/all_to_all | solution.py:28
  158.4 3.3 %all-to-all-start.5 = ((f32[4,16,640]{2,1,0:T(8,128)}), f32[4,16,640]{2,1,0:T(8,128)S(1)}, u32[]{:S(2)}, u32[]{:S(2)}) async-start(f32[4,16,640]{2,1,0:T(8,128)} %broadcast_in_dim.29), calls=%async_computation.5 | async-start | bytes 327680 | tf_op jit(solution)/shard_map/all_to_all | solution.py:28
  161.8 1.9 collective-permute-start.5
  163.7 13.6 %all-to-all-done.5 = f32[4,16,640]{2,1,0:T(8,128)S(1)} async-done(((f32[4,16,640]{2,1,0:T(8,128)}), f32[4,16,640]{2,1,0:T(8,128)S(1)}, u32[]{:S(2)}, u32[]{:S(2)}) %all-to-all-start.5) | async-done | bytes 163872 | tf_op jit(solution)/shard_map/all_to_all | solution.py:28
  178.2 4.7 %all-to-all-start.6 = ((f32[4,64,640]{2,1,0:T(8,128)}), f32[4,64,640]{2,1,0:T(8,128)S(1)}, u32[]{:S(2)}, u32[]{:S(2)}) async-start(f32[4,64,640]{2,1,0:T(8,128)} %broadcast_in_dim.58), calls=%async_computation.6 | async-start | bytes 1310720 | tf_op jit(solution)/shard_map/all_to_all | solution.py:28
  183.7 5.6 %left.1 = (f32[1,1024]{1,0:T(1,128)S(1)}, f32[1,512]{1,0:T(1,128)S(1)}, f32[1024,512]{1,0:T(8,128)}) custom-call(s32[1]{0:T(128)} %bitcast.where_ref, f32[512,256]{1,0:T(8,128)S(1)} %bitcast.36, f32[512,256]{1,0:T(8,128)S(1)} %collective-permute-done.5.far_ref, f32[512,256]{1,0:T(8,128)} %copy-done, f32[256,256]{1,0:T(8,128)} %copy-done.4, ...), custom_call_target="tpu_custom_call" | custom-call | tf_op jit(solution)/shard_map/left/pallas_call | solution.py:211
  189.3 2.4 %all-to-all-done.6 = f32[4,64,640]{2,1,0:T(8,128)S(1)} async-done(((f32[4,64,640]{2,1,0:T(8,128)}), f32[4,64,640]{2,1,0:T(8,128)S(1)}, u32[]{:S(2)}, u32[]{:S(2)}) %all-to-all-start.6) | async-done | bytes 655392 | tf_op jit(solution)/shard_map/all_to_all | solution.py:28
  191.7 7.1 %right.1 = (f32[1,1024]{1,0:T(1,128)}, f32[1,512]{1,0:T(1,128)}, f32[1024,512]{1,0:T(8,128)}) custom-call(f32[1024,256]{1,0:T(8,128)} %copy-done.1, f32[256,640]{1,0:T(8,128)S(1)} %bitcast.34, f32[256,256]{1,0:T(8,128)} %copy-done.4, f32[8,256]{1,0:T(8,128)} %maximum_maximum_fusion.vec_ref, f32[1,1024]{1,0:T(1,128)S(1)} %get-tuple-element.23.row_ref, ...), custom_call_target="tpu_custom_call" | custom-call | tf_op jit(solution)/shard_map/right/pallas_call | solution.py:253
  (51 shorter events, 11.0 us)
Async XLA Ops:
  24.3 24.7 %collective-permute-start = (f32[512,256]{1,0:T(8,128)S(1)}, f32[512,256]{1,0:T(8,128)S(1)}, u32[]{:S(2)}, u32[]{:S(2)}) collective-permute-start(f32[512,256]{1,0:T(8,128)S(1)} %bitcast.32), channel_id=1, source_target_pairs={{0,1},{1,0},{2,3},{3,2},{4,5},{5,4},{6,7},{7,6},{8,9},{9,8},{10,11... | collective-permute-start | bytes 1572872 | tf_op jit(solution)/shard_map/ppermute | solution.py:50
  26.3 19.8 %collective-permute-start.1 = (f32[256,256]{1,0:T(8,128)S(1)}, f32[256,256]{1,0:T(8,128)S(1)}, u32[]{:S(2)}, u32[]{:S(2)}) collective-permute-start(f32[256,256]{1,0:T(8,128)S(1)} %constant_dynamic-slice_fusion), channel_id=1, source_target_pairs={{0,0},{1,128},{2,32},{3,160},{4,64},{5,192},{6,96},{7,224},{8,256}... | collective-permute-start | bytes 786440 | tf_op jit(solution)/shard_map/ppermute | solution.py:279
  46.1 12.5 %collective-permute-start.2 = (f32[256,256]{1,0:T(8,128)S(1)}, f32[256,256]{1,0:T(8,128)S(1)}, u32[]{:S(2)}, u32[]{:S(2)}) collective-permute-start(f32[256,256]{1,0:T(8,128)S(1)} %collective-permute-done.1), channel_id=1, source_target_pairs={{0,128},{128,0},{256,384},{384,256},{1,129},{129,1},{257,385},{385... | collective-permute-start | bytes 786440 | tf_op jit(solution)/shard_map/ppermute | solution.py:50
  53.8 5.5 %copy-start.1 = (f32[1024,256]{1,0:T(8,128)}, f32[1024,256]{1,0:T(8,128)S(1)}, u32[]{:S(2)}) copy-start(f32[1024,256]{1,0:T(8,128)S(1)} %get-tuple-element.16.v_ref) | copy-start | bytes 3145732
  53.8 12.5 %all-to-all-start.1 = ((f32[4,64,512]{2,1,0:T(8,128)}), f32[4,64,512]{2,1,0:T(8,128)}, u32[]{:S(2)}, u32[]{:S(2)}) async-start(f32[4,64,512]{2,1,0:T(8,128)} %bitcast.5), calls=%async_computation.1 | async-start | bytes 1048576 | tf_op jit(solution)/shard_map/all_to_all | solution.py:28
  58.6 0.7 copy-start.2
  59.3 1.0 copy-start.3
  64.4 85.4 %copy-start = (f32[512,256]{1,0:T(8,128)}, f32[512,256]{1,0:T(8,128)S(1)}, u32[]{:S(2)}) copy-start(f32[512,256]{1,0:T(8,128)S(1)} %get-tuple-element.20.c_ref) | copy-start | bytes 1572868
  64.4 30.2 %collective-permute-start.3 = (f32[512,256]{1,0:T(8,128)S(1)}, f32[512,256]{1,0:T(8,128)S(1)}, u32[]{:S(2)}, u32[]{:S(2)}) collective-permute-start(f32[512,256]{1,0:T(8,128)S(1)} %get-tuple-element.19), channel_id=1, source_target_pairs={{0,1},{1,0},{2,3},{3,2},{4,5},{5,4},{6,7},{7,6},{8,9},{9,8},{10,11... | collective-permute-start | bytes 1572872 | tf_op jit(solution)/shard_map/ppermute | solution.py:50
  68.1 40.4 %all-to-all-start.2 = ((f32[4,16,512]{2,1,0:T(8,128)}), f32[4,16,512]{2,1,0:T(8,128)S(1)}, u32[]{:S(2)}, u32[]{:S(2)}) async-start(f32[4,16,512]{2,1,0:T(8,128)} %bitcast.6), calls=%async_computation.2 | async-start | bytes 262144 | tf_op jit(solution)/shard_map/all_to_all | solution.py:28
  108.8 16.9 %copy-start.5 = (f32[256,256]{1,0:T(8,128)S(1)}, f32[256,256]{1,0:T(8,128)}, u32[]{:S(2)}) copy-start(f32[256,256]{1,0:T(8,128)} %param.7) | copy-start | bytes 786436
  122.2 18.6 %all-to-all-start.4 = ((f32[4,152,256]{2,1,0:T(8,128)}), f32[4,152,256]{2,1,0:T(8,128)S(1)}, u32[]{:S(2)}, u32[]{:S(2)}) async-start(f32[4,152,256]{2,1,0:T(8,128)} %broadcast_in_dim.26), calls=%async_computation.4 | async-start | bytes 1245184 | tf_op jit(solution)/shard_map/all_to_all | solution.py:28
  125.8 32.6 %copy-start.4 = (f32[256,256]{1,0:T(8,128)}, f32[256,256]{1,0:T(8,128)S(1)}, u32[]{:S(2)}) copy-start(f32[256,256]{1,0:T(8,128)S(1)} %fusion.u_ref) | copy-start | bytes 786436
  140.9 8.5 %collective-permute-start.4 = (f32[24,256]{1,0:T(8,128)S(1)}, f32[24,256]{1,0:T(8,128)S(1)}, u32[]{:S(2)}, u32[]{:S(2)}) collective-permute-start(f32[24,256]{1,0:T(8,128)S(1)} %slice.23), channel_id=1, source_target_pairs={{0,1},{1,0},{2,3},{3,2},{4,5},{5,4},{6,7},{7,6},{8,9},{9,8},{10,11... | collective-permute-start | bytes 73736 | tf_op jit(solution)/shard_map/ppermute | solution.py:50
  143.9 13.9 %all-to-all-start.7 = ((f32[4,128,256]{2,1,0:T(8,128)}), f32[4,128,256]{2,1,0:T(8,128)S(1)}, u32[]{:S(2)}, u32[]{:S(2)}) async-start(f32[4,128,256]{2,1,0:T(8,128)} %broadcast_in_dim.60), calls=%async_computation.7 | async-start | bytes 1048576 | tf_op jit(solution)/shard_map/all_to_all | solution.py:28
  158.4 18.9 %all-to-all-start.5 = ((f32[4,16,640]{2,1,0:T(8,128)}), f32[4,16,640]{2,1,0:T(8,128)S(1)}, u32[]{:S(2)}, u32[]{:S(2)}) async-start(f32[4,16,640]{2,1,0:T(8,128)} %broadcast_in_dim.29), calls=%async_computation.5 | async-start | bytes 327680 | tf_op jit(solution)/shard_map/all_to_all | solution.py:28
  161.8 21.9 %collective-permute-start.5 = (f32[512,256]{1,0:T(8,128)S(1)}, f32[512,256]{1,0:T(8,128)S(1)}, u32[]{:S(2)}, u32[]{:S(2)}) collective-permute-start(f32[512,256]{1,0:T(8,128)S(1)} %bitcast.35), channel_id=1, source_target_pairs={{0,1},{1,0},{2,3},{3,2},{4,5},{5,4},{6,7},{7,6},{8,9},{9,8},{10,11... | collective-permute-start | bytes 1572872 | tf_op jit(solution)/shard_map/ppermute | solution.py:50
  178.2 13.5 %all-to-all-start.6 = ((f32[4,64,640]{2,1,0:T(8,128)}), f32[4,64,640]{2,1,0:T(8,128)S(1)}, u32[]{:S(2)}, u32[]{:S(2)}) async-start(f32[4,64,640]{2,1,0:T(8,128)} %broadcast_in_dim.58), calls=%async_computation.6 | async-start | bytes 1310720 | tf_op jit(solution)/shard_map/all_to_all | solution.py:28

commit v4 on v3

v4 whole, which is shorter than its diff:
```python
import math

import jax
import jax.numpy as jnp
from jax import lax
from jax.experimental import pallas as pl
from jax.experimental.pallas import tpu as pltpu
from jax.sharding import Mesh, PartitionSpec as P


N = 16384
AXES = ("y", "zh", "x", "zl", "core")
SIZES = (4, 4, 4, 4, 2)
PREC = lax.Precision.HIGH


def dot(left, right, dims=((1,), (0,))):
    return lax.dot_general(left, right, (dims, ((), ())), precision=PREC)


def unit_lower(values, row_start):
    rows = row_start + lax.broadcasted_iota(jnp.int32, values.shape, 0)
    cols = lax.broadcasted_iota(jnp.int32, values.shape, 1)
    return jnp.where(rows > cols, values, jnp.where(rows == cols, 1.0, 0.0))


def exchange(parts, axis):
    return lax.all_to_all(parts, axis, 0, 0)


def gather(block, axis, size):
    parts = exchange(jnp.broadcast_to(block[None], (size,) + block.shape), axis)
    return parts.reshape((size * block.shape[0],) + block.shape[1:])


def reduce_scatter(block, axis, size):
    rows = block.shape[0] // size
    return jnp.sum(exchange(block.reshape(size, rows, block.shape[1]), axis), axis=0)


def reduce_both(block, small, axis, size):
    rows = block.shape[0] // size
    cut = block.reshape(size, rows, block.shape[1])
    both = jnp.concatenate([cut, jnp.broadcast_to(small[None], (size,) + small.shape)], axis=1)
    total = jnp.sum(exchange(both, axis), axis=0)
    return total[:rows], total[rows:]


def swap(block, axis, size, bit):
    return lax.ppermute(block, axis, [(i, i ^ bit) for i in range(size)])


def transposition():
    pairs = []
    for y in range(4):
        for zh in range(4):
            for x in range(4):
                for zl in range(4):
                    for core in range(2):
                        src = (((y * 4 + zh) * 4 + x) * 4 + zl) * 2 + core
                        new_y = x % 2 * 2 + core
                        dst = (((new_y * 4 + zl) * 4 + y) * 4 + zh) * 2 + x // 2
                        pairs.append((src, dst))
    return pairs


def split(value):
    high = value.astype(jnp.bfloat16)
    return high, (value - high.astype(jnp.float32)).astype(jnp.bfloat16)


def left3(value, axis):
    high, low = split(value)
    return jnp.concatenate([high, high, low], axis=axis)


def right3(value, axis):
    high, low = split(value)
    return jnp.concatenate([high, low, high], axis=axis)


def mm3(left, right, dims):
    return lax.dot_general(left, right, (dims, ((), ())), preferred_element_type=jnp.float32)


def mm(left, right, dims):
    return mm3(left3(left, dims[0][0]), right3(right, dims[1][0]), dims)


def triu(ref):
    rows = lax.broadcasted_iota(jnp.int32, ref.shape, 0)
    cols = lax.broadcasted_iota(jnp.int32, ref.shape, 1)
    return jnp.where(rows <= cols, ref[...], 0.0)


NN = ((1,), (0,))
NT = ((1,), (1,))
TN = ((0,), (0,))
STEPS = 4
LANES = 128
VMEM = pl.BlockSpec(memory_space=pltpu.VMEM)
HBM = pl.BlockSpec(memory_space=pltpu.HBM)


def near_f32(*shape):
    return pltpu.VMEM(shape, jnp.float32)


def far_f32(*shape):
    return jax.ShapeDtypeStruct(shape, jnp.float32)


def vmem(value):
    return pltpu.with_memory_space_constraint(value, pltpu.VMEM)


def staged(shape, dtype=jnp.float32):
    return [pltpu.VMEM(shape, dtype), pltpu.SemaphoreType.DMA((STEPS,))]


def block_copy(src, dst, sems, step):
    rows = src.shape[0] // STEPS
    part = pl.ds(step * rows, rows)
    return pltpu.make_async_copy(src.at[part], dst.at[part], sems.at[step])


def interleaved(lead, own, far):
    groups, shard, kdim = own.shape
    first = jnp.where(lead > 0.5, own, far)
    second = jnp.where(lead > 0.5, far, own)
    return jnp.concatenate([first, second], axis=1).reshape(2 * groups * shard, kdim)


def flag(index):
    return jnp.where(index == 0, 1.0, 0.0)


def rows_kernel(mine_ref, other_ref, window_ref, v_ref, w_ref, buf, sems):
    for step in range(STEPS):
        block_copy(window_ref, buf, sems, step).start()
    lead = flag(lax.axis_index("core"))
    start = (lax.axis_index("y") * 4 + lax.axis_index("zh")) * v_ref.shape[0]
    groups, rows = mine_ref.shape[0] // STEPS, v_ref.shape[0] // STEPS
    for step in range(STEPS):
        mine, other = (ref[step * groups : (step + 1) * groups] for ref in (mine_ref, other_ref))
        block = unit_lower(interleaved(lead, mine, other), start + step * rows)
        part = slice(step * rows, (step + 1) * rows)
        v_ref[part] = block
        block_copy(window_ref, buf, sems, step).wait()
        w_part = mm(block, buf[part], TN)
        if step == 0:
            w_ref[...] = w_part
        else:
            w_ref[...] += w_part


def rows_call(mine, other, window):
    n_rows, n_cols = window.shape
    kdim = mine.shape[2]
    return pl.pallas_call(
        rows_kernel,
        in_specs=[VMEM, VMEM, HBM],
        out_specs=[VMEM] * 2,
        out_shape=[near_f32(n_rows, kdim), near_f32(kdim, n_cols)],
        scratch_shapes=staged((n_rows, n_cols)),
        name="rows",
    )(vmem(mine), vmem(other), window)


def cols_kernel(own_ref, far_ref, check_ref, window_ref, v_ref, keep_ref, send_ref, tail_ref, buf, sems):
    for step in range(STEPS):
        block_copy(window_ref, buf, sems, step).start()
    core = lax.axis_index("core")
    pcol = (lax.axis_index("x") * 4 + lax.axis_index("zl")) * 2 + core
    lead = flag(lax.axis_index("y") % 2)
    block = unit_lower(interleaved(lead, own_ref[...], far_ref[...]), pcol * v_ref.shape[0])
    v_ref[...] = block
    right = right3(block, 0)
    line = lax.broadcasted_iota(jnp.int32, (8, check_ref.shape[1]), 0)
    tail = jnp.where(line == 0, check_ref[...], jnp.where(line == 1, 1.0, 0.0))
    half, rows = STEPS // 2, window_ref.shape[0] // STEPS
    for step in range(STEPS):
        block_copy(window_ref, buf, sems, step).wait()
        chunk = buf[step * rows : (step + 1) * rows]
        if step == 0:
            chunk = jnp.concatenate([chunk, tail], axis=0)
        x = mm3(left3(chunk, 1), right, NN)
        if step == 0:
            tail_ref[...] = x[rows:]
            x = x[:rows]
        part = slice(step % half * rows, (step % half + 1) * rows)

        @pl.when(core == step // half)
        def _():
            keep_ref[part] = x

        @pl.when(core != step // half)
        def _():
            send_ref[part] = x


def cols_call(own, far, check, window):
    n_rows, n_cols = window.shape
    kdim = own.shape[2]
    half = near_f32(n_rows // 2, kdim)
    return pl.pallas_call(
        cols_kernel,
        in_specs=[VMEM, VMEM, VMEM, HBM],
        out_specs=[VMEM] * 4,
        out_shape=[near_f32(n_cols, kdim), half, half, near_f32(8, kdim)],
        scratch_shapes=staged((n_rows, n_cols)),
        name="cols",
    )(vmem(own), vmem(far), check.reshape(1, n_cols), window)


def prep_kernel(v_ref, u_ref, check_ref, turned_ref, part_ref):
    upper = right3(triu(u_ref), 1)
    rows = v_ref.shape[0] // STEPS
    total = None
    for step in range(STEPS):
        part = slice(step * rows, (step + 1) * rows)
        block = v_ref[part]
        turned_ref[part] = left3(mm3(left3(block, 1), upper, NT), 1)
        sums = mm(jnp.broadcast_to(check_ref[:, part], (8, rows)), block, NN)
        total = sums if step == 0 else total + sums
    part_ref[...] = total[:1]


def prep_call(v_rows, factor, check):
    n_rows, kdim = v_rows.shape
    return pl.pallas_call(
        prep_kernel,
        in_specs=[VMEM] * 3,
        out_specs=[VMEM] * 2,
        out_shape=[jax.ShapeDtypeStruct((n_rows, 3 * kdim), jnp.bfloat16), far_f32(1, kdim)],
        name="prep",
    )(v_rows, factor, check.reshape(1, n_rows))


def spread_kernel(parts_ref, u_ref, y_ref, small_ref):
    total = jnp.sum(parts_ref[...], axis=0)
    rows = y_ref.shape[1]
    y_rows = mm(total[:rows], triu(u_ref), NN)
    for j in range(y_ref.shape[0]):
        y_ref[j] = y_rows
    small_ref[...] = total[rows:]


def spread_call(parts, factor, rows):
    size, tall, kdim = parts.shape
    return pl.pallas_call(
        spread_kernel,
        in_specs=[VMEM] * 2,
        out_specs=[VMEM] * 2,
        out_shape=[near_f32(size, rows, kdim), near_f32(tall - rows, kdim)],
        name="spread",
    )(vmem(parts), factor)


def slice_kernel(own_ref, far_ref, w_ref, c_ref, u_ref, part_ref, g_ref, vec_ref):
    k_rows, n_cols = w_ref.shape
    kdim = u_ref.shape[0]
    small = own_ref[...] + far_ref[...]
    upper = triu(u_ref)
    scaled = small[k_rows + 1 : k_rows + 2] / math.sqrt(N)
    line = lax.broadcasted_iota(jnp.int32, (8, kdim), 0)
    turned = mm(jnp.broadcast_to(scaled, (8, kdim)), upper, NT)
    vec_ref[...] = jnp.where(line == 0, scaled, jnp.where(line == 1, small[k_rows : k_rows + 1], jnp.where(line == 2, turned, 0.0)))
    z = mm(small[:k_rows], upper, NN)
    g = w_ref[...] - mm(z, c_ref[...], NT)
    prow = lax.axis_index("y") * 4 + lax.axis_index("zh")
    owner = prow * k_rows + lax.broadcasted_iota(jnp.int32, (k_rows, kdim), 0)
    mine = lax.broadcasted_iota(jnp.int32, (k_rows, kdim), 1) == owner
    z_scaled = jnp.sum(z * scaled, axis=1, keepdims=True)
    partial = part_ref[...] - jnp.sum(jnp.where(mine, z_scaled, 0.0), axis=0, keepdims=True)
    row = lax.broadcasted_iota(jnp.int32, (k_rows, LANES), 0)
    extra = jnp.zeros((k_rows, LANES), jnp.float32)
    for i in range(kdim // LANES):
        extra = jnp.where(row == i, partial[:, i * LANES : (i + 1) * LANES], extra)
    for j in range(g_ref.shape[0]):
        g_ref[j, :, :n_cols] = g
        g_ref[j, :, n_cols:] = extra


def slice_call(own, far, w_slice, v_cols, factor, part):
    k_rows, n_cols = w_slice.shape
    kdim = factor.shape[0]
    return pl.pallas_call(
        slice_kernel,
        in_specs=[VMEM] * 6,
        out_specs=[VMEM] * 2,
        out_shape=[near_f32(4, k_rows, n_cols + LANES), near_f32(8, kdim)],
        name="slice",
    )(vmem(own), vmem(far), vmem(w_slice), vmem(v_cols), factor, part)


def left_kernel(own_ref, far_ref, c_ref, u_ref, vec_ref, row_ref, col_ref, window_ref, nrow_ref, ncol_ref, out_ref, buf, sems, done):
    for step in range(STEPS):
        block_copy(window_ref, buf, sems, step).start()
    right = right3(c_ref[...], 1)
    vec = vec_ref[...]
    turned = mm(vec, triu(u_ref), NN)
    ncol_ref[...] = col_ref[...] - mm3(left3(turned, 1), right, NT)[1:2]
    vec = left3(vec, 1)
    half, rows = STEPS // 2, window_ref.shape[0] // STEPS
    lead = flag(lax.axis_index("core"))
    for step in range(STEPS):
        piece = slice(step % half * rows, (step % half + 1) * rows)
        mine = lead if step < half else 1.0 - lead
        block = jnp.where(mine > 0.5, own_ref[piece], far_ref[piece])
        part = slice(step * rows, (step + 1) * rows)
        out = mm3(left3(block, 1), right, NT)
        block_copy(window_ref, buf, sems, step).wait()
        buf[part] = buf[part] - out
        block_copy(buf, out_ref, done, step).start()
        nrow_ref[:, part] = row_ref[:, part] - mm3(vec, right3(block, 1), NT)[:1]
    for step in range(STEPS):
        block_copy(buf, out_ref, done, step).wait()


def left_call(own, far, v_cols, factor, vectors, row_check, col_check, window):
    n_rows, n_cols = window.shape
    return pl.pallas_call(
        left_kernel,
        in_specs=[VMEM] * 7 + [HBM],
        out_specs=[VMEM, VMEM, HBM],
        out_shape=[near_f32(1, n_rows), near_f32(1, n_cols), far_f32(n_rows, n_cols)],
        scratch_shapes=staged((n_rows, n_cols)) + [pltpu.SemaphoreType.DMA((STEPS,))],
        name="left",
    )(
        vmem(own),
        vmem(far),
        vmem(v_cols),
        factor,
        vmem(vectors),
        row_check.reshape(1, n_rows),
        col_check.reshape(1, n_cols),
        window,
    )


def right_kernel(g_ref, vec_ref, row_ref, col_ref, turned_ref, window_ref, nrow_ref, ncol_ref, out_ref, tbuf, tsems, buf, sems, done):
    for step in range(STEPS):
        block_copy(turned_ref, tbuf, tsems, step).start()
        block_copy(window_ref, buf, sems, step).start()
    n_cols = window_ref.shape[1]
    kdim = g_ref.shape[0]
    g_all = g_ref[...]
    extra = jnp.sum(g_all[:, n_cols:].reshape(16, kdim // 16, LANES), axis=0)
    inner = jnp.concatenate([extra[i : i + 1] for i in range(kdim // LANES)], axis=1)
    inner = jnp.broadcast_to(inner, (LANES, kdim)).T
    right = right3(jnp.concatenate([g_all[:, :n_cols], inner], axis=1), 0)
    rows = window_ref.shape[0] // STEPS
    for step in range(STEPS):
        part = slice(step * rows, (step + 1) * rows)
        block_copy(turned_ref, tbuf, tsems, step).wait()
        left = tbuf[part]
        if step == 0:
            left = jnp.concatenate([left, left3(vec_ref[...], 1)], axis=0)
        out = mm3(left, right, NN)
        if step == 0:
            ncol_ref[...] = col_ref[...] - out[rows + 2 : rows + 3, :n_cols]
            out = out[:rows]
        block_copy(window_ref, buf, sems, step).wait()
        buf[part] = buf[part] - out[:, :n_cols]
        block_copy(buf, out_ref, done, step).start()
        nrow_ref[:, part] = row_ref[:, part] - out[:, n_cols:].T[:1]
    for step in range(STEPS):
        block_copy(buf, out_ref, done, step).wait()


def right_call(g_all, vectors, row_part, col_part, turned, window):
    n_rows, n_cols = window.shape
    return pl.pallas_call(
        right_kernel,
        in_specs=[VMEM] * 4 + [HBM] * 2,
        out_specs=[VMEM, VMEM, HBM],
        out_shape=[far_f32(1, n_rows), far_f32(1, n_cols), far_f32(n_rows, n_cols)],
        scratch_shapes=staged(turned.shape, turned.dtype) + staged((n_rows, n_cols)) + [pltpu.SemaphoreType.DMA((STEPS,))],
        name="right",
    )(vmem(g_all), vmem(vectors), vmem(row_part), vmem(col_part), turned, window)


def on_device(window, panel, factor, col_check, row_check):
    x = lax.axis_index("x")
    kdim = panel.shape[1]
    shard = panel.shape[0]
    n_rows, n_cols = window.shape

    line = gather(panel, "zl", 4)
    mine = gather(line, "x", 4)
    quarter = lax.dynamic_slice_in_dim(mine, x // 2 * (n_cols // 2), n_cols // 2, 0)
    moved = lax.ppermute(quarter, AXES, transposition())
    other = swap(mine, "core", 2, 1)
    v_rows, w_part = rows_call(mine.reshape(-1, shard, kdim), other.reshape(-1, shard, kdim), window)
    w_part = reduce_scatter(w_part, "y", 4)
    near = swap(moved, "y", 4, 1)
    w_slice = reduce_scatter(w_part, "zh", 4)

    v_cols, keep, send, tail = cols_call(moved.reshape(-1, shard, kdim), near.reshape(-1, shard, kdim), col_check, window)
    x_part = keep + swap(send, "core", 2, 1)
    small = jnp.concatenate([dot(w_slice, v_cols), tail], axis=0)
    x_part, small = reduce_both(x_part, small, "x", 4)
    both = jnp.concatenate([x_part, small], axis=0)
    parts = gather(both, "zl", 4).reshape((4,) + both.shape)
    turned, row_part = prep_call(v_rows, factor, row_check)
    y_parts, small = spread_call(parts, factor, x_part.shape[0])
    y_rows = exchange(y_parts, "x").reshape(n_rows // 2, kdim)
    y_far = swap(y_rows, "core", 2, 1)
    small_far = swap(small, "core", 2, 1)
    g_parts, vectors = slice_call(small, small_far, w_slice, v_cols, factor, row_part)
    g_some = exchange(g_parts, "zh").reshape(-1, n_cols + LANES)
    g_all = gather(g_some, "y", 4)

    new_row, new_col, partly = left_call(y_rows, y_far, v_cols, factor, vectors, row_check, col_check, window)
    new_row, new_col, new_window = right_call(g_all, vectors, new_row, new_col, turned, partly)
    return new_window, new_col.reshape(n_cols), new_row.reshape(n_rows)


def solution(mesh):
    fine = Mesh(mesh.devices.reshape(SIZES), AXES)
    rows, cols = ("y", "zh"), ("x", "zl", "core")
    placed = (P(rows, cols), P(AXES, None), P(), P(cols), P(rows))
    return jax.shard_map(
        on_device,
        mesh=fine,
        in_specs=placed,
        out_specs=(P(rows, cols), P(cols), P(rows)),
        check_vma=False,
    )
```

time: 201 us -> 190 us (0.945)
  waiting for transfers between devices: 64.6 us -> 44.1 us
  blocking collectives: 35.3 us -> 51 us
  starting transfers between devices: 65.4 us -> 60.5 us
  Pallas kernels: 21.6 us -> 25.3 us
  local copies, waits for them, and re-layouts: 5.94 us -> 3.42 us
  other arithmetic: 3.98 us -> 1.96 us
    all_to_all x6 -> x5, waiting for transfers between devices: 52.3 us -> 30.8 us  [exchange(): return lax.all_to_all(parts, axis, 0, 0)]
    all_to_all x2 -> x4, blocking collectives: 35.3 us -> 51 us  [exchange(): return lax.all_to_all(parts, axis, 0, 0)]
    all_to_all x6 -> x5, starting transfers between devices: 47.8 us -> 43.1 us  [exchange(): return lax.all_to_all(parts, axis, 0, 0)]
    pallas_call x4 -> x7, Pallas kernels: 21.6 us -> 25.3 us  [the longest x1 5.4 us: left_call(): pl.pallas_call(left_kernel, in_specs=[VMEM] * 7 + [HBM], out_specs=[VMEM,...]
    broadcast_in_dim x5 -> x4, local copies, waits for them, and re-layouts: 4.06 us -> 1.72 us  [gather(): parts = exchange(jnp.broadcast_to(block[None], (size,) + block.shape), axis)]
  transfers between devices with their start and end apart: 12 -> 11, of which waited for: 6 -> 5; matrix products, arithmetic and copies ran while one was open for 3% -> 1% of each run, Pallas kernels for 7% -> 10%
where the time goes in v4:
time: 190 us; the launch traced here: 187 us
  starting transfers between devices  60.5 us (32%)
  blocking collectives  51 us (27%)
  waiting for transfers between devices  44.1 us (23%)
  Pallas kernels  25.3 us (13%)
  local copies, waits for them, and re-layouts  3.42 us (2%)
  other arithmetic  1.96 us (1%)
    all_to_all x4, blocking collectives, exchange(): return lax.all_to_all(parts, axis, 0, 0)  51 us
    all_to_all x5, starting transfers between devices, exchange(): return lax.all_to_all(parts, axis, 0, 0)  43.1 us
    all_to_all x5, waiting for transfers between devices, exchange(): return lax.all_to_all(parts, axis, 0, 0)  30.8 us
    ppermute x1, waiting for transfers between devices, on_device(): moved = lax.ppermute(quarter, AXES, transposition())  13.3 us
    ppermute x5, starting transfers between devices, swap(): return lax.ppermute(block, axis, [(i, i ^ bit) for i in range(size)])  10.9 us
    ppermute x1, starting transfers between devices, on_device(): moved = lax.ppermute(quarter, AXES, transposition())  6.52 us
    pallas_call x1, Pallas kernels, left_call(): pl.pallas_call(left_kernel, in_specs=[VMEM] * 7 + [HBM], out_specs=[VMEM,...  5.4 us
    pallas_call x1, Pallas kernels, right_call(): pl.pallas_call(right_kernel, in_specs=[VMEM] * 4 + [HBM] * 2, out_specs=[...  4.97 us
  transfers between devices with their start and end apart: 11, of which 5 were waited for; matrix products, arithmetic and copies ran while one was open for 1% of the time, Pallas kernels for 10%

profile of v4, /device:TPU:6, one launch (start us, length us, event | category | flops | bytes accessed | tf_op | source)
XLA Modules:
  0.0 187.4 jit_solution(126651349989857835)
XLA Ops:
  1.4 11.8 %all_to_all.45 = f32[4,32,256]{2,1,0:T(8,128)S(1)} all-to-all(f32[4,32,256]{2,1,0:T(8,128)S(1)} %broadcast_in_dim.14), channel_id=1, replica_groups=mesh['y'=4,'zh'=4,'x'=4,'zl'=4,'core'=2] {'zl'}, dimensions={0} | all-to-all | bytes 262144 | tf_op jit(solution)/shard_map/all_to_all | solution.py:28
  13.2 10.8 %all_to_all.46 = f32[4,128,256]{2,1,0:T(8,128)S(1)} all-to-all(f32[4,128,256]{2,1,0:T(8,128)S(1)} %broadcast_in_dim.16), channel_id=1, replica_groups=mesh['y'=4,'zh'=4,'x'=4,'zl'=4,'core'=2] {'x'}, dimensions={0} | all-to-all | bytes 1048576 | tf_op jit(solution)/shard_map/all_to_all | solution.py:28
  26.0 6.5 %collective-permute-start = (f32[256,256]{1,0:T(8,128)S(1)}, f32[256,256]{1,0:T(8,128)S(1)}, u32[]{:S(2)}, u32[]{:S(2)}) collective-permute-start(f32[256,256]{1,0:T(8,128)S(1)} %constant_dynamic-slice_fusion), channel_id=1, source_target_pairs={{0,0},{1,128},{2,32},{3,160},{4,64},{5,192},{6,96},{7,224},{8,256}... | collective-permute-start | bytes 786440 | tf_op jit(solution)/shard_map/ppermute | solution.py:393
  32.5 13.3 %collective-permute-done = f32[256,256]{1,0:T(8,128)S(1)} collective-permute-done((f32[256,256]{1,0:T(8,128)S(1)}, f32[256,256]{1,0:T(8,128)S(1)}, u32[]{:S(2)}, u32[]{:S(2)}) %collective-permute-start) | collective-permute-done | bytes 262176 | tf_op jit(solution)/shard_map/ppermute | solution.py:393
  45.8 2.8 %collective-permute-start.1 = (f32[256,256]{1,0:T(8,128)S(1)}, f32[256,256]{1,0:T(8,128)S(1)}, u32[]{:S(2)}, u32[]{:S(2)}) collective-permute-start(f32[256,256]{1,0:T(8,128)S(1)} %collective-permute-done), channel_id=1, source_target_pairs={{0,128},{128,0},{256,384},{384,256},{1,129},{129,1},{257,385},{385... | collective-permute-start | bytes 786440 | tf_op jit(solution)/shard_map/ppermute | solution.py:50
  48.6 3.5 %rows.1 = (f32[1024,256]{1,0:T(8,128)S(1)}, f32[256,512]{1,0:T(8,128)}) custom-call(f32[16,32,256]{2,1,0:T(8,128)S(1)} %bitcast.20, f32[16,32,256]{2,1,0:T(8,128)S(1)} %bitcast.24, f32[1024,512]{1,0:T(8,128)} %window_ref.5), custom_call_target="tpu_custom_call" | custom-call | tf_op jit(solution)/shard_map/rows/pallas_call | solution.py:160
  52.1 4.2 %all-to-all-start.2 = ((f32[4,64,512]{2,1,0:T(8,128)}), f32[4,64,512]{2,1,0:T(8,128)}, u32[]{:S(2)}, u32[]{:S(2)}) async-start(f32[4,64,512]{2,1,0:T(8,128)} %bitcast.8), calls=%async_computation.2 | async-start | bytes 1048576 | tf_op jit(solution)/shard_map/all_to_all | solution.py:28
  57.9 4.0 %cols.1 = (f32[512,256]{1,0:T(8,128)S(1)}, f32[512,256]{1,0:T(8,128)S(1)}, f32[512,256]{1,0:T(8,128)S(1)}, f32[8,256]{1,0:T(8,128)S(1)}) custom-call(f32[8,32,256]{2,1,0:T(8,128)S(1)} %bitcast.25, f32[8,32,256]{2,1,0:T(8,128)S(1)} %bitcast.26, f32[1,512]{1,0:T(1,128)} %bitcast.32, f32[1024,512]{1,0:T(8,128)} %window_ref.5), custom_call_target="tpu_custom_call" | custom-call | tf_op jit(solution)/shard_map/cols/pallas_call | solution.py:206
  62.0 1.9 %collective-permute-start.2 = (f32[512,256]{1,0:T(8,128)S(1)}, f32[512,256]{1,0:T(8,128)S(1)}, u32[]{:S(2)}, u32[]{:S(2)}) collective-permute-start(f32[512,256]{1,0:T(8,128)S(1)} %get-tuple-element.22), channel_id=1, source_target_pairs={{0,1},{1,0},{2,3},{3,2},{4,5},{5,4},{6,7},{7,6},{8,9},{9,8},{10,11... | collective-permute-start | bytes 1572872 | tf_op jit(solution)/shard_map/ppermute | solution.py:50
  66.1 25.4 %all-to-all-start.3 = ((f32[4,16,512]{2,1,0:T(8,128)}), f32[4,16,512]{2,1,0:T(8,128)S(1)}, u32[]{:S(2)}, u32[]{:S(2)}) async-start(f32[4,16,512]{2,1,0:T(8,128)} %bitcast.9), calls=%async_computation.3 | async-start | bytes 262144 | tf_op jit(solution)/shard_map/all_to_all | solution.py:28
  91.6 13.5 %all-to-all-done.3 = f32[4,16,512]{2,1,0:T(8,128)S(1)} async-done(((f32[4,16,512]{2,1,0:T(8,128)}), f32[4,16,512]{2,1,0:T(8,128)S(1)}, u32[]{:S(2)}, u32[]{:S(2)}) %all-to-all-start.3) | async-done | bytes 131104 | tf_op jit(solution)/shard_map/all_to_all | solution.py:28
  105.4 11.6 %all_to_all.47 = f32[4,152,256]{2,1,0:T(8,128)S(1)} all-to-all(f32[4,152,256]{2,1,0:T(8,128)S(1)} %pad_maximum_fusion), channel_id=1, replica_groups=mesh['y'=4,'zh'=4,'x'=4,'zl'=4,'core'=2] {'x'}, dimensions={0} | all-to-all | bytes 1245184 | tf_op jit(solution)/shard_map/all_to_all | solution.py:28
  117.0 16.9 %all_to_all.48.parts_ref = f32[4,152,256]{2,1,0:T(8,128)S(1)} all-to-all(f32[4,152,256]{2,1,0:T(8,128)S(1)} %broadcast_in_dim.36), channel_id=1, replica_groups=mesh['y'=4,'zh'=4,'x'=4,'zl'=4,'core'=2] {'zl'}, dimensions={0} | all-to-all | bytes 1245184 | tf_op jit(solution)/shard_map/all_to_all | solution.py:28
  133.9 2.0 %spread.1 = (f32[4,128,256]{2,1,0:T(8,128)}, f32[24,256]{1,0:T(8,128)S(1)}) custom-call(f32[4,152,256]{2,1,0:T(8,128)S(1)} %all_to_all.48.parts_ref, f32[256,256]{1,0:T(8,128)} %u_ref.7), custom_call_target="tpu_custom_call" | custom-call | tf_op jit(solution)/shard_map/spread/pallas_call | solution.py:251
  135.9 5.5 %all-to-all-start.8 = ((f32[4,128,256]{2,1,0:T(8,128)}), f32[4,128,256]{2,1,0:T(8,128)S(1)}, u32[]{:S(2)}, u32[]{:S(2)}) async-start(f32[4,128,256]{2,1,0:T(8,128)} %get-tuple-element.31), calls=%async_computation.8 | async-start | bytes 1048576 | tf_op jit(solution)/shard_map/all_to_all | solution.py:28
  143.3 3.3 %prep.1 = (bf16[1024,768]{1,0:T(8,128)(2,1)}, f32[1,256]{1,0:T(1,128)}) custom-call(f32[1024,256]{1,0:T(8,128)} %copy-done, f32[256,256]{1,0:T(8,128)} %u_ref.7, f32[1,1024]{1,0:T(1,128)} %bitcast.30), custom_call_target="tpu_custom_call" | custom-call | tf_op jit(solution)/shard_map/prep/pallas_call | solution.py:231
  146.6 2.2 %slice.4 = (f32[4,16,640]{2,1,0:T(8,128)}, f32[8,256]{1,0:T(8,128)S(1)}) custom-call(f32[24,256]{1,0:T(8,128)S(1)} %get-tuple-element.26.own_ref, f32[24,256]{1,0:T(8,128)S(1)} %collective-permute-done.4.far_ref, f32[16,512]{1,0:T(8,128)S(1)} %reduce_sum.28.w_ref, f32[512,256]{1,0:T(8,128)S(1)} %get-tuple-element.24.c_ref, f32[256,256]{1,0:T(8,128)} %u_ref.7, ...), custom_call_target="tpu_custom_call" | custom-call | tf_op jit(solution)/shard_map/slice/pallas_call | solution.py:288
  148.8 3.3 %all-to-all-start.6 = ((f32[4,16,640]{2,1,0:T(8,128)}), f32[4,16,640]{2,1,0:T(8,128)S(1)}, u32[]{:S(2)}, u32[]{:S(2)}) async-start(f32[4,16,640]{2,1,0:T(8,128)} %get-tuple-element.29), calls=%async_computation.6 | async-start | bytes 327680 | tf_op jit(solution)/shard_map/all_to_all | solution.py:28
  152.2 2.4 %collective-permute-start.5 = (f32[512,256]{1,0:T(8,128)S(1)}, f32[512,256]{1,0:T(8,128)S(1)}, u32[]{:S(2)}, u32[]{:S(2)}) collective-permute-start(f32[512,256]{1,0:T(8,128)S(1)} %bitcast.22), channel_id=1, source_target_pairs={{0,1},{1,0},{2,3},{3,2},{4,5},{5,4},{6,7},{7,6},{8,9},{9,8},{10,11... | collective-permute-start | bytes 1572872 | tf_op jit(solution)/shard_map/ppermute | solution.py:50
  154.6 13.4 %all-to-all-done.6 = f32[4,16,640]{2,1,0:T(8,128)S(1)} async-done(((f32[4,16,640]{2,1,0:T(8,128)}), f32[4,16,640]{2,1,0:T(8,128)S(1)}, u32[]{:S(2)}, u32[]{:S(2)}) %all-to-all-start.6) | async-done | bytes 163872 | tf_op jit(solution)/shard_map/all_to_all | solution.py:28
  168.9 4.7 %all-to-all-start.7 = ((f32[4,64,640]{2,1,0:T(8,128)}), f32[4,64,640]{2,1,0:T(8,128)S(1)}, u32[]{:S(2)}, u32[]{:S(2)}) async-start(f32[4,64,640]{2,1,0:T(8,128)} %broadcast_in_dim.38), calls=%async_computation.7 | async-start | bytes 1310720 | tf_op jit(solution)/shard_map/all_to_all | solution.py:28
  173.6 5.4 %left.1 = (f32[1,1024]{1,0:T(1,128)S(1)}, f32[1,512]{1,0:T(1,128)S(1)}, f32[1024,512]{1,0:T(8,128)}) custom-call(f32[512,256]{1,0:T(8,128)S(1)} %bitcast.23, f32[512,256]{1,0:T(8,128)S(1)} %collective-permute-done.5.far_ref, f32[512,256]{1,0:T(8,128)S(1)} %get-tuple-element.24.c_ref, f32[256,256]{1,0:T(8,128)} %u_ref.7, ...), custom_call_target="tpu_custom_call" | custom-call | tf_op jit(solution)/shard_map/left/pallas_call | solution.py:323
  179.0 3.4 %all-to-all-done.7 = f32[4,64,640]{2,1,0:T(8,128)S(1)} async-done(((f32[4,64,640]{2,1,0:T(8,128)}), f32[4,64,640]{2,1,0:T(8,128)S(1)}, u32[]{:S(2)}, u32[]{:S(2)}) %all-to-all-start.7) | async-done | bytes 655392 | tf_op jit(solution)/shard_map/all_to_all | solution.py:28
  182.4 5.0 %right.1 = (f32[1,1024]{1,0:T(1,128)}, f32[1,512]{1,0:T(1,128)}, f32[1024,512]{1,0:T(8,128)}) custom-call(f32[256,640]{1,0:T(8,128)S(1)} %bitcast.21, f32[8,256]{1,0:T(8,128)S(1)} %get-tuple-element.30.vec_ref, f32[1,1024]{1,0:T(1,128)S(1)} %get-tuple-element.32.row_ref, f32[1,512]{1,0:T(1,128)S(1)} %get-tuple-element.33.col_ref, ...), custom_call_target="tpu_custom_call" | custom-call | tf_op jit(solution)/shard_map/right/pallas_call | solution.py:374
  (28 shorter events, 9.9 us)
Async XLA Ops:
  24.0 24.6 %collective-permute-start.3 = (f32[512,256]{1,0:T(8,128)S(1)}, f32[512,256]{1,0:T(8,128)S(1)}, u32[]{:S(2)}, u32[]{:S(2)}) collective-permute-start(f32[512,256]{1,0:T(8,128)S(1)} %bitcast.18), channel_id=1, source_target_pairs={{0,1},{1,0},{2,3},{3,2},{4,5},{5,4},{6,7},{7,6},{8,9},{9,8},{10,11... | collective-permute-start | bytes 1572872 | tf_op jit(solution)/shard_map/ppermute | solution.py:50
  26.0 19.9 %collective-permute-start = (f32[256,256]{1,0:T(8,128)S(1)}, f32[256,256]{1,0:T(8,128)S(1)}, u32[]{:S(2)}, u32[]{:S(2)}) collective-permute-start(f32[256,256]{1,0:T(8,128)S(1)} %constant_dynamic-slice_fusion), channel_id=1, source_target_pairs={{0,0},{1,128},{2,32},{3,160},{4,64},{5,192},{6,96},{7,224},{8,256}... | collective-permute-start | bytes 786440 | tf_op jit(solution)/shard_map/ppermute | solution.py:393
  45.8 10.4 %collective-permute-start.1 = (f32[256,256]{1,0:T(8,128)S(1)}, f32[256,256]{1,0:T(8,128)S(1)}, u32[]{:S(2)}, u32[]{:S(2)}) collective-permute-start(f32[256,256]{1,0:T(8,128)S(1)} %collective-permute-done), channel_id=1, source_target_pairs={{0,128},{128,0},{256,384},{384,256},{1,129},{129,1},{257,385},{385... | collective-permute-start | bytes 786440 | tf_op jit(solution)/shard_map/ppermute | solution.py:50
  52.1 4.9 %copy-start = (f32[1024,256]{1,0:T(8,128)}, f32[1024,256]{1,0:T(8,128)S(1)}, u32[]{:S(2)}) copy-start(f32[1024,256]{1,0:T(8,128)S(1)} %get-tuple-element.27.v_ref) | copy-start | bytes 3145732
  52.1 12.3 %all-to-all-start.2 = ((f32[4,64,512]{2,1,0:T(8,128)}), f32[4,64,512]{2,1,0:T(8,128)}, u32[]{:S(2)}, u32[]{:S(2)}) async-start(f32[4,64,512]{2,1,0:T(8,128)} %bitcast.8), calls=%async_computation.2 | async-start | bytes 1048576 | tf_op jit(solution)/shard_map/all_to_all | solution.py:28
  56.3 0.7 copy-start.1
  57.0 1.0 copy-start.2
  62.0 29.5 %collective-permute-start.2 = (f32[512,256]{1,0:T(8,128)S(1)}, f32[512,256]{1,0:T(8,128)S(1)}, u32[]{:S(2)}, u32[]{:S(2)}) collective-permute-start(f32[512,256]{1,0:T(8,128)S(1)} %get-tuple-element.22), channel_id=1, source_target_pairs={{0,1},{1,0},{2,3},{3,2},{4,5},{5,4},{6,7},{7,6},{8,9},{9,8},{10,11... | collective-permute-start | bytes 1572872 | tf_op jit(solution)/shard_map/ppermute | solution.py:50
  66.1 38.9 %all-to-all-start.3 = ((f32[4,16,512]{2,1,0:T(8,128)}), f32[4,16,512]{2,1,0:T(8,128)S(1)}, u32[]{:S(2)}, u32[]{:S(2)}) async-start(f32[4,16,512]{2,1,0:T(8,128)} %bitcast.9), calls=%async_computation.3 | async-start | bytes 262144 | tf_op jit(solution)/shard_map/all_to_all | solution.py:28
  135.9 12.9 %all-to-all-start.8 = ((f32[4,128,256]{2,1,0:T(8,128)}), f32[4,128,256]{2,1,0:T(8,128)S(1)}, u32[]{:S(2)}, u32[]{:S(2)}) async-start(f32[4,128,256]{2,1,0:T(8,128)} %get-tuple-element.31), calls=%async_computation.8 | async-start | bytes 1048576 | tf_op jit(solution)/shard_map/all_to_all | solution.py:28
  141.4 5.2 %collective-permute-start.4 = (f32[24,256]{1,0:T(8,128)S(1)}, f32[24,256]{1,0:T(8,128)S(1)}, u32[]{:S(2)}, u32[]{:S(2)}) collective-permute-start(f32[24,256]{1,0:T(8,128)S(1)} %get-tuple-element.26.own_ref), channel_id=1, source_target_pairs={{0,1},{1,0},{2,3},{3,2},{4,5},{5,4},{6,7},{7,6},{8,9},{9,8},{10,11... | collective-permute-start | bytes 73736 | tf_op jit(solution)/shard_map/ppermute | solution.py:50
  148.8 19.2 %all-to-all-start.6 = ((f32[4,16,640]{2,1,0:T(8,128)}), f32[4,16,640]{2,1,0:T(8,128)S(1)}, u32[]{:S(2)}, u32[]{:S(2)}) async-start(f32[4,16,640]{2,1,0:T(8,128)} %get-tuple-element.29), calls=%async_computation.6 | async-start | bytes 327680 | tf_op jit(solution)/shard_map/all_to_all | solution.py:28
  152.2 21.5 %collective-permute-start.5 = (f32[512,256]{1,0:T(8,128)S(1)}, f32[512,256]{1,0:T(8,128)S(1)}, u32[]{:S(2)}, u32[]{:S(2)}) collective-permute-start(f32[512,256]{1,0:T(8,128)S(1)} %bitcast.22), channel_id=1, source_target_pairs={{0,1},{1,0},{2,3},{3,2},{4,5},{5,4},{6,7},{7,6},{8,9},{9,8},{10,11... | collective-permute-start | bytes 1572872 | tf_op jit(solution)/shard_map/ppermute | solution.py:50
  168.9 13.5 %all-to-all-start.7 = ((f32[4,64,640]{2,1,0:T(8,128)}), f32[4,64,640]{2,1,0:T(8,128)S(1)}, u32[]{:S(2)}, u32[]{:S(2)}) async-start(f32[4,64,640]{2,1,0:T(8,128)} %broadcast_in_dim.38), calls=%async_computation.7 | async-start | bytes 1310720 | tf_op jit(solution)/shard_map/all_to_all | solution.py:28

commit v5 on v4

--- a/solution.py
+++ b/solution.py
@@ -48,6 +48,21 @@
 
 def swap(block, axis, size, bit):
     return lax.ppermute(block, axis, [(i, i ^ bit) for i in range(size)])
+
+
+def halved(block, axis, size, bit):
+    high = lax.axis_index(axis) // bit % 2
+    rows = block.shape[0] // 2
+    keep = lax.dynamic_slice_in_dim(block, high * rows, rows, 0)
+    send = lax.dynamic_slice_in_dim(block, (1 - high) * rows, rows, 0)
+    return keep + swap(send, axis, size, bit)
+
+
+def doubled(block, axis, size, bit, dim):
+    other = swap(block, axis, size, bit)
+    low = lax.axis_index(axis) // bit % 2 == 0
+    pair = [jnp.where(low, block, other), jnp.where(low, other, block)]
+    return jnp.stack(pair, axis=dim)
 
 
 def transposition():
@@ -235,26 +250,6 @@
         out_shape=[jax.ShapeDtypeStruct((n_rows, 3 * kdim), jnp.bfloat16), far_f32(1, kdim)],
         name="prep",
     )(v_rows, factor, check.reshape(1, n_rows))
-
-
-def spread_kernel(parts_ref, u_ref, y_ref, small_ref):
-    total = jnp.sum(parts_ref[...], axis=0)
-    rows = y_ref.shape[1]
-    y_rows = mm(total[:rows], triu(u_ref), NN)
-    for j in range(y_ref.shape[0]):
-        y_ref[j] = y_rows
-    small_ref[...] = total[rows:]
-
-
-def spread_call(parts, factor, rows):
-    size, tall, kdim = parts.shape
-    return pl.pallas_call(
-        spread_kernel,
-        in_specs=[VMEM] * 2,
-        out_specs=[VMEM] * 2,
-        out_shape=[near_f32(size, rows, kdim), near_f32(tall - rows, kdim)],
-        name="spread",
-    )(vmem(parts), factor)
 
 
 def slice_kernel(own_ref, far_ref, w_ref, c_ref, u_ref, part_ref, g_ref, vec_ref):
@@ -277,9 +272,8 @@
     extra = jnp.zeros((k_rows, LANES), jnp.float32)
     for i in range(kdim // LANES):
         extra = jnp.where(row == i, partial[:, i * LANES : (i + 1) * LANES], extra)
-    for j in range(g_ref.shape[0]):
-        g_ref[j, :, :n_cols] = g
-        g_ref[j, :, n_cols:] = extra
+    g_ref[:, :n_cols] = g
+    g_ref[:, n_cols:] = extra
 
 
 def slice_call(own, far, w_slice, v_cols, factor, part):
@@ -289,7 +283,7 @@
         slice_kernel,
         in_specs=[VMEM] * 6,
         out_specs=[VMEM] * 2,
-        out_shape=[near_f32(4, k_rows, n_cols + LANES), near_f32(8, kdim)],
+        out_shape=[near_f32(k_rows, n_cols + LANES), near_f32(8, kdim)],
         name="slice",
     )(vmem(own), vmem(far), vmem(w_slice), vmem(v_cols), factor, part)
 
@@ -395,21 +389,24 @@
     v_rows, w_part = rows_call(mine.reshape(-1, shard, kdim), other.reshape(-1, shard, kdim), window)
     w_part = reduce_scatter(w_part, "y", 4)
     near = swap(moved, "y", 4, 1)
-    w_slice = reduce_scatter(w_part, "zh", 4)
+    w_part = halved(w_part, "zh", 4, 2)
+    w_slice = halved(w_part, "zh", 4, 1)
 
     v_cols, keep, send, tail = cols_call(moved.reshape(-1, shard, kdim), near.reshape(-1, shard, kdim), col_check, window)
     x_part = keep + swap(send, "core", 2, 1)
     small = jnp.concatenate([dot(w_slice, v_cols), tail], axis=0)
     x_part, small = reduce_both(x_part, small, "x", 4)
     both = jnp.concatenate([x_part, small], axis=0)
-    parts = gather(both, "zl", 4).reshape((4,) + both.shape)
+    total = jnp.sum(gather(both, "zl", 4).reshape((4,) + both.shape), axis=0)
     turned, row_part = prep_call(v_rows, factor, row_check)
-    y_parts, small = spread_call(parts, factor, x_part.shape[0])
-    y_rows = exchange(y_parts, "x").reshape(n_rows // 2, kdim)
+    tall = x_part.shape[0]
+    small = total[tall:]
+    y_rows = gather(dot(total[:tall], jnp.triu(factor)), "x", 4)
     y_far = swap(y_rows, "core", 2, 1)
     small_far = swap(small, "core", 2, 1)
-    g_parts, vectors = slice_call(small, small_far, w_slice, v_cols, factor, row_part)
-    g_some = exchange(g_parts, "zh").reshape(-1, n_cols + LANES)
+    g_part, vectors = slice_call(small, small_far, w_slice, v_cols, factor, row_part)
+    g_some = doubled(g_part, "zh", 4, 2, 0)
+    g_some = doubled(g_some, "zh", 4, 1, 1).reshape(-1, n_cols + LANES)
     g_all = gather(g_some, "y", 4)
 
     new_row, new_col, partly = left_call(y_rows, y_far, v_cols, factor, vectors, row_check, col_check, window)

time: 190 us -> 190 us (level)
  waiting for transfers between devices: 44.1 us -> 32.4 us
  blocking collectives: 51 us -> 61.9 us
  starting transfers between devices: 60.5 us -> 65.6 us
  Pallas kernels: 25.3 us -> 22.6 us
    ppermute x5 -> x9, starting transfers between devices: 10.9 us -> 45.8 us  [swap(): return lax.ppermute(block, axis, [(i, i ^ bit) for i in range(size)])]
    all_to_all x5 -> x3, starting transfers between devices: 43.1 us -> 13.8 us  [exchange(): return lax.all_to_all(parts, axis, 0, 0)]
    ppermute x5 -> x9, waiting for transfers between devices: 0.01 us -> 19.8 us  [swap(): return lax.ppermute(block, axis, [(i, i ^ bit) for i in range(size)])]
    all_to_all x5 -> x3, waiting for transfers between devices: 30.8 us -> 12.6 us  [exchange(): return lax.all_to_all(parts, axis, 0, 0)]
    ppermute x1, waiting for transfers between devices: 13.3 us -> 0.01 us  [on_device(): moved = lax.ppermute(quarter, AXES, transposition())]
    all_to_all x4, blocking collectives: 51 us -> 61.9 us  [exchange(): return lax.all_to_all(parts, axis, 0, 0)]
    pallas_call x1 -> x0, Pallas kernels: 1.98 us -> none  [spread_call(): pl.pallas_call(spread_kernel, in_specs=[VMEM] * 2, out_specs=[VMEM] * 2,...]
  transfers between devices with their start and end apart: 11 -> 13, of which waited for: 5 -> 7; matrix products, arithmetic and copies ran while one was open for 1% -> 1% of each run, Pallas kernels for 10% -> 7%
where the time goes in v5:
time: 190 us; the launch traced here: 187 us
  starting transfers between devices  65.6 us (35%)
  blocking collectives  61.9 us (33%)
  waiting for transfers between devices  32.4 us (17%)
  Pallas kernels  22.6 us (12%)
  local copies, waits for them, and re-layouts  2.64 us (1%)
    all_to_all x4, blocking collectives, exchange(): return lax.all_to_all(parts, axis, 0, 0)  61.9 us
    ppermute x9, starting transfers between devices, swap(): return lax.ppermute(block, axis, [(i, i ^ bit) for i in range(size)])  45.8 us
    ppermute x9, waiting for transfers between devices, swap(): return lax.ppermute(block, axis, [(i, i ^ bit) for i in range(size)])  19.8 us
    all_to_all x3, starting transfers between devices, exchange(): return lax.all_to_all(parts, axis, 0, 0)  13.8 us
    all_to_all x3, waiting for transfers between devices, exchange(): return lax.all_to_all(parts, axis, 0, 0)  12.6 us
    ppermute x1, starting transfers between devices, on_device(): moved = lax.ppermute(quarter, AXES, transposition())  6.12 us
    pallas_call x1, Pallas kernels, left_call(): pl.pallas_call(left_kernel, in_specs=[VMEM] * 7 + [HBM], out_specs=[VMEM,...  5.4 us
    pallas_call x1, Pallas kernels, right_call(): pl.pallas_call(right_kernel, in_specs=[VMEM] * 4 + [HBM] * 2, out_specs=[...  4.98 us
  transfers between devices with their start and end apart: 13, of which 7 were waited for; matrix products, arithmetic and copies ran while one was open for 1% of the time, Pallas kernels for 7%

profile of v5, /device:TPU:6, one launch (start us, length us, event | category | flops | bytes accessed | tf_op | source)
XLA Modules:
  0.0 187.1 jit_solution(822064084408955742)
XLA Ops:
  1.4 11.8 %all_to_all.35 = f32[4,32,256]{2,1,0:T(8,128)S(1)} all-to-all(f32[4,32,256]{2,1,0:T(8,128)S(1)} %broadcast_in_dim.20), channel_id=1, replica_groups=mesh['y'=4,'zh'=4,'x'=4,'zl'=4,'core'=2] {'zl'}, dimensions={0} | all-to-all | bytes 262144 | tf_op jit(solution)/shard_map/all_to_all | solution.py:28
  13.2 10.8 %all_to_all.36 = f32[4,128,256]{2,1,0:T(8,128)S(1)} all-to-all(f32[4,128,256]{2,1,0:T(8,128)S(1)} %broadcast_in_dim.22), channel_id=1, replica_groups=mesh['y'=4,'zh'=4,'x'=4,'zl'=4,'core'=2] {'x'}, dimensions={0} | all-to-all | bytes 1048576 | tf_op jit(solution)/shard_map/all_to_all | solution.py:28
  27.8 3.4 %rows.1 = (f32[1024,256]{1,0:T(8,128)S(1)}, f32[256,512]{1,0:T(8,128)}) custom-call(f32[16,32,256]{2,1,0:T(8,128)S(1)} %bitcast.26, f32[16,32,256]{2,1,0:T(8,128)S(1)} %bitcast.31, f32[1024,512]{1,0:T(8,128)} %window_ref.5), custom_call_target="tpu_custom_call" | custom-call | tf_op jit(solution)/shard_map/rows/pallas_call | solution.py:175
  31.2 4.3 %all-to-all-start.2 = ((f32[4,64,512]{2,1,0:T(8,128)}), f32[4,64,512]{2,1,0:T(8,128)S(1)}, u32[]{:S(2)}, u32[]{:S(2)}) async-start(f32[4,64,512]{2,1,0:T(8,128)} %bitcast.8), calls=%async_computation.2 | async-start | bytes 1048576 | tf_op jit(solution)/shard_map/all_to_all | solution.py:28
  35.5 6.1 %collective-permute-start = (f32[256,256]{1,0:T(8,128)S(1)}, f32[256,256]{1,0:T(8,128)S(1)}, u32[]{:S(2)}, u32[]{:S(2)}) collective-permute-start(f32[256,256]{1,0:T(8,128)S(1)} %constant_dynamic-slice_fusion.2), channel_id=1, source_target_pairs={{0,0},{1,128},{2,32},{3,160},{4,64},{5,192},{6,96},{7,224},{8,256}... | collective-permute-start | bytes 786440 | tf_op jit(solution)/shard_map/ppermute | solution.py:387
  41.7 6.5 %all-to-all-done.2 = f32[4,64,512]{2,1,0:T(8,128)S(1)} async-done(((f32[4,64,512]{2,1,0:T(8,128)}), f32[4,64,512]{2,1,0:T(8,128)S(1)}, u32[]{:S(2)}, u32[]{:S(2)}) %all-to-all-start.2) | async-done | bytes 524320 | tf_op jit(solution)/shard_map/all_to_all | solution.py:28
  48.3 10.1 %collective-permute-start.4 = (f32[32,512]{1,0:T(8,128)S(1)}, f32[32,512]{1,0:T(8,128)S(1)}, u32[]{:S(2)}, u32[]{:S(2)}) collective-permute-start(f32[32,512]{1,0:T(8,128)S(1)} %constant_dynamic-slice_fusion.1), channel_id=1, source_target_pairs={{0,64},{32,96},{64,0},{96,32},{1,65},{33,97},{65,1},{97,33},{2,66}... | collective-permute-start | bytes 196616 | tf_op jit(solution)/shard_map/ppermute | solution.py:50
  58.4 2.5 %collective-permute-start.1 = (f32[256,256]{1,0:T(8,128)S(1)}, f32[256,256]{1,0:T(8,128)S(1)}, u32[]{:S(2)}, u32[]{:S(2)}) collective-permute-start(f32[256,256]{1,0:T(8,128)S(1)} %collective-permute-done), channel_id=1, source_target_pairs={{0,128},{128,0},{256,384},{384,256},{1,129},{129,1},{257,385},{385... | collective-permute-start | bytes 786440 | tf_op jit(solution)/shard_map/ppermute | solution.py:50
  60.9 3.2 %collective-permute-done.4 = f32[32,512]{1,0:T(8,128)S(1)} collective-permute-done((f32[32,512]{1,0:T(8,128)S(1)}, f32[32,512]{1,0:T(8,128)S(1)}, u32[]{:S(2)}, u32[]{:S(2)}) %collective-permute-start.4) | collective-permute-done | bytes 65568 | tf_op jit(solution)/shard_map/ppermute | solution.py:50
  64.1 16.2 %collective-permute-start.5 = (f32[16,512]{1,0:T(8,128)S(1)}, f32[16,512]{1,0:T(8,128)S(1)}, u32[]{:S(2)}, u32[]{:S(2)}) collective-permute-start(f32[16,512]{1,0:T(8,128)S(1)} %constant_dynamic-slice_fusion), channel_id=1, source_target_pairs={{0,32},{32,0},{64,96},{96,64},{1,33},{33,1},{65,97},{97,65},{2,34}... | collective-permute-start | bytes 98312 | tf_op jit(solution)/shard_map/ppermute | solution.py:50
  80.4 4.0 %cols.1 = (f32[512,256]{1,0:T(8,128)S(1)}, f32[512,256]{1,0:T(8,128)S(1)}, f32[512,256]{1,0:T(8,128)S(1)}, f32[8,256]{1,0:T(8,128)S(1)}) custom-call(f32[8,32,256]{2,1,0:T(8,128)S(1)} %bitcast.32, f32[8,32,256]{2,1,0:T(8,128)S(1)} %bitcast.33, f32[1,512]{1,0:T(1,128)} %bitcast.39, f32[1024,512]{1,0:T(8,128)} %window_ref.5), custom_call_target="tpu_custom_call" | custom-call | tf_op jit(solution)/shard_map/cols/pallas_call | solution.py:221
  88.3 13.1 %all_to_all.37 = f32[4,152,256]{2,1,0:T(8,128)S(1)} all-to-all(f32[4,152,256]{2,1,0:T(8,128)S(1)} %pad_maximum_fusion), channel_id=1, replica_groups=mesh['y'=4,'zh'=4,'x'=4,'zl'=4,'core'=2] {'x'}, dimensions={0} | all-to-all | bytes 1245184 | tf_op jit(solution)/shard_map/all_to_all | solution.py:28
  101.5 26.3 %all_to_all.38 = f32[4,152,256]{2,1,0:T(8,128)S(1)} all-to-all(f32[4,152,256]{2,1,0:T(8,128)S(1)} %broadcast_in_dim.46), channel_id=1, replica_groups=mesh['y'=4,'zh'=4,'x'=4,'zl'=4,'core'=2] {'zl'}, dimensions={0} | all-to-all | bytes 1245184 | tf_op jit(solution)/shard_map/all_to_all | solution.py:28
  129.8 3.3 %prep.1 = (bf16[1024,768]{1,0:T(8,128)(2,1)}, f32[1,256]{1,0:T(1,128)}) custom-call(f32[1024,256]{1,0:T(8,128)} %copy-done, f32[256,256]{1,0:T(8,128)} %u_ref.5, f32[1,1024]{1,0:T(1,128)} %bitcast.37), custom_call_target="tpu_custom_call" | custom-call | tf_op jit(solution)/shard_map/prep/pallas_call | solution.py:246
  134.5 4.1 %collective-permute-start.7 = (f32[16,640]{1,0:T(8,128)S(1)}, f32[16,640]{1,0:T(8,128)S(1)}, u32[]{:S(2)}, u32[]{:S(2)}) collective-permute-start(f32[16,640]{1,0:T(8,128)S(1)} %get-tuple-element.26), channel_id=1, source_target_pairs={{0,64},{32,96},{64,0},{96,32},{1,65},{33,97},{65,1},{97,33},{2,66}... | collective-permute-start | bytes 122888 | tf_op jit(solution)/shard_map/ppermute | solution.py:50
  139.8 5.5 %all-to-all-start.6 = ((f32[4,128,256]{2,1,0:T(8,128)}), f32[4,128,256]{2,1,0:T(8,128)S(1)}, u32[]{:S(2)}, u32[]{:S(2)}) async-start(f32[4,128,256]{2,1,0:T(8,128)} %broadcast_in_dim.50), calls=%async_computation.6 | async-start | bytes 1048576 | tf_op jit(solution)/shard_map/all_to_all | solution.py:28
  145.3 4.7 %collective-permute-done.7 = f32[16,640]{1,0:T(8,128)S(1)} collective-permute-done((f32[16,640]{1,0:T(8,128)S(1)}, f32[16,640]{1,0:T(8,128)S(1)}, u32[]{:S(2)}, u32[]{:S(2)}) %collective-permute-start.7) | collective-permute-done | bytes 40992 | tf_op jit(solution)/shard_map/ppermute | solution.py:50
  150.0 5.2 %collective-permute-start.8 = (f32[2,16,640]{2,1,0:T(8,128)S(1)}, f32[2,16,640]{2,1,0:T(8,128)S(1)}, u32[]{:S(2)}, u32[]{:S(2)}) collective-permute-start(f32[2,16,640]{2,1,0:T(8,128)S(1)} %pad_maximum_fusion.2), channel_id=1, source_target_pairs={{0,32},{32,0},{64,96},{96,64},{1,33},{33,1},{65,97},{97,65},{2,34}... | collective-permute-start | bytes 245768 | tf_op jit(solution)/shard_map/ppermute | solution.py:50
  155.2 8.5 %collective-permute-done.8 = f32[2,16,640]{2,1,0:T(8,128)S(1)} collective-permute-done((f32[2,16,640]{2,1,0:T(8,128)S(1)}, f32[2,16,640]{2,1,0:T(8,128)S(1)}, u32[]{:S(2)}, u32[]{:S(2)}) %collective-permute-start.8) | collective-permute-done | bytes 81952 | tf_op jit(solution)/shard_map/ppermute | solution.py:50
  163.7 1.9 %collective-permute-start.9 = (f32[512,256]{1,0:T(8,128)S(1)}, f32[512,256]{1,0:T(8,128)S(1)}, u32[]{:S(2)}, u32[]{:S(2)}) collective-permute-start(f32[512,256]{1,0:T(8,128)S(1)} %bitcast.29), channel_id=1, source_target_pairs={{0,1},{1,0},{2,3},{3,2},{4,5},{5,4},{6,7},{7,6},{8,9},{9,8},{10,11... | collective-permute-start | bytes 1572872 | tf_op jit(solution)/shard_map/ppermute | solution.py:50
  166.6 4.0 %all-to-all-start.5 = ((f32[4,64,640]{2,1,0:T(8,128)}), f32[4,64,640]{2,1,0:T(8,128)S(1)}, u32[]{:S(2)}, u32[]{:S(2)}) async-start(f32[4,64,640]{2,1,0:T(8,128)} %broadcast_in_dim.48), calls=%async_computation.5 | async-start | bytes 1310720 | tf_op jit(solution)/shard_map/all_to_all | solution.py:28
  170.6 5.4 %left.1 = (f32[1,1024]{1,0:T(1,128)S(1)}, f32[1,512]{1,0:T(1,128)S(1)}, f32[1024,512]{1,0:T(8,128)}) custom-call(f32[512,256]{1,0:T(8,128)S(1)} %bitcast.30, f32[512,256]{1,0:T(8,128)S(1)} %collective-permute-done.9.far_ref, f32[512,256]{1,0:T(8,128)S(1)} %get-tuple-element.22.c_ref, f32[256,256]{1,0:T(8,128)} %u_ref.5, ...), custom_call_target="tpu_custom_call" | custom-call | tf_op jit(solution)/shard_map/left/pallas_call | solution.py:317
  176.0 6.1 %all-to-all-done.5 = f32[4,64,640]{2,1,0:T(8,128)S(1)} async-done(((f32[4,64,640]{2,1,0:T(8,128)}), f32[4,64,640]{2,1,0:T(8,128)S(1)}, u32[]{:S(2)}, u32[]{:S(2)}) %all-to-all-start.5) | async-done | bytes 655392 | tf_op jit(solution)/shard_map/all_to_all | solution.py:28
  182.1 5.0 %right.1 = (f32[1,1024]{1,0:T(1,128)}, f32[1,512]{1,0:T(1,128)}, f32[1024,512]{1,0:T(8,128)}) custom-call(f32[256,640]{1,0:T(8,128)S(1)} %bitcast.28, f32[8,256]{1,0:T(8,128)S(1)} %get-tuple-element.27.vec_ref, f32[1,1024]{1,0:T(1,128)S(1)} %get-tuple-element.28.row_ref, f32[1,512]{1,0:T(1,128)S(1)} %get-tuple-element.29.col_ref, ...), custom_call_target="tpu_custom_call" | custom-call | tf_op jit(solution)/shard_map/right/pallas_call | solution.py:368
  (42 shorter events, 14.2 us)
Async XLA Ops:
  24.0 3.8 %collective-permute-start.3 = (f32[512,256]{1,0:T(8,128)S(1)}, f32[512,256]{1,0:T(8,128)S(1)}, u32[]{:S(2)}, u32[]{:S(2)}) collective-permute-start(f32[512,256]{1,0:T(8,128)S(1)} %bitcast.25), channel_id=1, source_target_pairs={{0,1},{1,0},{2,3},{3,2},{4,5},{5,4},{6,7},{7,6},{8,9},{9,8},{10,11... | collective-permute-start | bytes 1572872 | tf_op jit(solution)/shard_map/ppermute | solution.py:50
  31.2 49.1 %copy-start = (f32[1024,256]{1,0:T(8,128)}, f32[1024,256]{1,0:T(8,128)S(1)}, u32[]{:S(2)}) copy-start(f32[1024,256]{1,0:T(8,128)S(1)} %get-tuple-element.24.v_ref) | copy-start | bytes 3145732
  31.2 17.0 %all-to-all-start.2 = ((f32[4,64,512]{2,1,0:T(8,128)}), f32[4,64,512]{2,1,0:T(8,128)S(1)}, u32[]{:S(2)}, u32[]{:S(2)}) async-start(f32[4,64,512]{2,1,0:T(8,128)} %bitcast.8), calls=%async_computation.2 | async-start | bytes 1048576 | tf_op jit(solution)/shard_map/all_to_all | solution.py:28
  35.5 22.9 %collective-permute-start = (f32[256,256]{1,0:T(8,128)S(1)}, f32[256,256]{1,0:T(8,128)S(1)}, u32[]{:S(2)}, u32[]{:S(2)}) collective-permute-start(f32[256,256]{1,0:T(8,128)S(1)} %constant_dynamic-slice_fusion.2), channel_id=1, source_target_pairs={{0,0},{1,128},{2,32},{3,160},{4,64},{5,192},{6,96},{7,224},{8,256}... | collective-permute-start | bytes 786440 | tf_op jit(solution)/shard_map/ppermute | solution.py:387
  48.3 15.8 %collective-permute-start.4 = (f32[32,512]{1,0:T(8,128)S(1)}, f32[32,512]{1,0:T(8,128)S(1)}, u32[]{:S(2)}, u32[]{:S(2)}) collective-permute-start(f32[32,512]{1,0:T(8,128)S(1)} %constant_dynamic-slice_fusion.1), channel_id=1, source_target_pairs={{0,64},{32,96},{64,0},{96,32},{1,65},{33,97},{65,1},{97,33},{2,66}... | collective-permute-start | bytes 196616 | tf_op jit(solution)/shard_map/ppermute | solution.py:50
  58.4 21.9 %collective-permute-start.1 = (f32[256,256]{1,0:T(8,128)S(1)}, f32[256,256]{1,0:T(8,128)S(1)}, u32[]{:S(2)}, u32[]{:S(2)}) collective-permute-start(f32[256,256]{1,0:T(8,128)S(1)} %collective-permute-done), channel_id=1, source_target_pairs={{0,128},{128,0},{256,384},{384,256},{1,129},{129,1},{257,385},{385... | collective-permute-start | bytes 786440 | tf_op jit(solution)/shard_map/ppermute | solution.py:50
  64.1 22.2 %collective-permute-start.5 = (f32[16,512]{1,0:T(8,128)S(1)}, f32[16,512]{1,0:T(8,128)S(1)}, u32[]{:S(2)}, u32[]{:S(2)}) collective-permute-start(f32[16,512]{1,0:T(8,128)S(1)} %constant_dynamic-slice_fusion), channel_id=1, source_target_pairs={{0,32},{32,0},{64,96},{96,64},{1,33},{33,1},{65,97},{97,65},{2,34}... | collective-permute-start | bytes 98312 | tf_op jit(solution)/shard_map/ppermute | solution.py:50
  84.4 3.8 %collective-permute-start.2 = (f32[512,256]{1,0:T(8,128)S(1)}, f32[512,256]{1,0:T(8,128)S(1)}, u32[]{:S(2)}, u32[]{:S(2)}) collective-permute-start(f32[512,256]{1,0:T(8,128)S(1)} %get-tuple-element.20), channel_id=1, source_target_pairs={{0,1},{1,0},{2,3},{3,2},{4,5},{5,4},{6,7},{7,6},{8,9},{9,8},{10,11... | collective-permute-start | bytes 1572872 | tf_op jit(solution)/shard_map/ppermute | solution.py:50
  101.5 37.1 %copy-start.1 = (f32[256,256]{1,0:T(8,128)S(1)}, f32[256,256]{1,0:T(8,128)}, u32[]{:S(2)}) copy-start(f32[256,256]{1,0:T(8,128)} %u_ref.5) | copy-start | bytes 786436
  127.8 5.2 %collective-permute-start.6 = (f32[24,256]{1,0:T(8,128)S(1)}, f32[24,256]{1,0:T(8,128)S(1)}, u32[]{:S(2)}, u32[]{:S(2)}) collective-permute-start(f32[24,256]{1,0:T(8,128)S(1)} %slice.12.own_ref), channel_id=1, source_target_pairs={{0,1},{1,0},{2,3},{3,2},{4,5},{5,4},{6,7},{7,6},{8,9},{9,8},{10,11... | collective-permute-start | bytes 73736 | tf_op jit(solution)/shard_map/ppermute | solution.py:50
  134.5 15.4 %collective-permute-start.7 = (f32[16,640]{1,0:T(8,128)S(1)}, f32[16,640]{1,0:T(8,128)S(1)}, u32[]{:S(2)}, u32[]{:S(2)}) collective-permute-start(f32[16,640]{1,0:T(8,128)S(1)} %get-tuple-element.26), channel_id=1, source_target_pairs={{0,64},{32,96},{64,0},{96,32},{1,65},{33,97},{65,1},{97,33},{2,66}... | collective-permute-start | bytes 122888 | tf_op jit(solution)/shard_map/ppermute | solution.py:50
  139.8 23.9 %all-to-all-start.6 = ((f32[4,128,256]{2,1,0:T(8,128)}), f32[4,128,256]{2,1,0:T(8,128)S(1)}, u32[]{:S(2)}, u32[]{:S(2)}) async-start(f32[4,128,256]{2,1,0:T(8,128)} %broadcast_in_dim.50), calls=%async_computation.6 | async-start | bytes 1048576 | tf_op jit(solution)/shard_map/all_to_all | solution.py:28
  150.0 13.7 %collective-permute-start.8 = (f32[2,16,640]{2,1,0:T(8,128)S(1)}, f32[2,16,640]{2,1,0:T(8,128)S(1)}, u32[]{:S(2)}, u32[]{:S(2)}) collective-permute-start(f32[2,16,640]{2,1,0:T(8,128)S(1)} %pad_maximum_fusion.2), channel_id=1, source_target_pairs={{0,32},{32,0},{64,96},{96,64},{1,33},{33,1},{65,97},{97,65},{2,34}... | collective-permute-start | bytes 245768 | tf_op jit(solution)/shard_map/ppermute | solution.py:50
  163.7 6.8 %collective-permute-start.9 = (f32[512,256]{1,0:T(8,128)S(1)}, f32[512,256]{1,0:T(8,128)S(1)}, u32[]{:S(2)}, u32[]{:S(2)}) collective-permute-start(f32[512,256]{1,0:T(8,128)S(1)} %bitcast.29), channel_id=1, source_target_pairs={{0,1},{1,0},{2,3},{3,2},{4,5},{5,4},{6,7},{7,6},{8,9},{9,8},{10,11... | collective-permute-start | bytes 1572872 | tf_op jit(solution)/shard_map/ppermute | solution.py:50
  166.6 15.5 %all-to-all-start.5 = ((f32[4,64,640]{2,1,0:T(8,128)}), f32[4,64,640]{2,1,0:T(8,128)S(1)}, u32[]{:S(2)}, u32[]{:S(2)}) async-start(f32[4,64,640]{2,1,0:T(8,128)} %broadcast_in_dim.48), calls=%async_computation.5 | async-start | bytes 1310720 | tf_op jit(solution)/shard_map/all_to_all | solution.py:28

commit v6 on v4

--- a/solution.py
+++ b/solution.py
@@ -173,7 +173,10 @@
     core = lax.axis_index("core")
     pcol = (lax.axis_index("x") * 4 + lax.axis_index("zl")) * 2 + core
     lead = flag(lax.axis_index("y") % 2)
-    block = unit_lower(interleaved(lead, own_ref[...], far_ref[...]), pcol * v_ref.shape[0])
+    top = flag(lax.axis_index("y") // 2)
+    own, far = (interleaved(lead, ref[0], ref[1]) for ref in (own_ref, far_ref))
+    block = jnp.concatenate([jnp.where(top > 0.5, own, far), jnp.where(top > 0.5, far, own)], axis=0)
+    block = unit_lower(block, pcol * v_ref.shape[0])
     v_ref[...] = block
     right = right3(block, 0)
     line = lax.broadcasted_iota(jnp.int32, (8, check_ref.shape[1]), 0)
@@ -201,7 +204,7 @@
 
 def cols_call(own, far, check, window):
     n_rows, n_cols = window.shape
-    kdim = own.shape[2]
+    kdim = own.shape[3]
     half = near_f32(n_rows // 2, kdim)
     return pl.pallas_call(
         cols_kernel,
@@ -235,26 +238,6 @@
         out_shape=[jax.ShapeDtypeStruct((n_rows, 3 * kdim), jnp.bfloat16), far_f32(1, kdim)],
         name="prep",
     )(v_rows, factor, check.reshape(1, n_rows))
-
-
-def spread_kernel(parts_ref, u_ref, y_ref, small_ref):
-    total = jnp.sum(parts_ref[...], axis=0)
-    rows = y_ref.shape[1]
-    y_rows = mm(total[:rows], triu(u_ref), NN)
-    for j in range(y_ref.shape[0]):
-        y_ref[j] = y_rows
-    small_ref[...] = total[rows:]
-
-
-def spread_call(parts, factor, rows):
-    size, tall, kdim = parts.shape
-    return pl.pallas_call(
-        spread_kernel,
-        in_specs=[VMEM] * 2,
-        out_specs=[VMEM] * 2,
-        out_shape=[near_f32(size, rows, kdim), near_f32(tall - rows, kdim)],
-        name="spread",
-    )(vmem(parts), factor)
 
 
 def slice_kernel(own_ref, far_ref, w_ref, c_ref, u_ref, part_ref, g_ref, vec_ref):
@@ -382,30 +365,31 @@
 
 
 def on_device(window, panel, factor, col_check, row_check):
-    x = lax.axis_index("x")
     kdim = panel.shape[1]
     shard = panel.shape[0]
     n_rows, n_cols = window.shape
 
     line = gather(panel, "zl", 4)
+    moved = lax.ppermute(line, AXES, transposition())
     mine = gather(line, "x", 4)
-    quarter = lax.dynamic_slice_in_dim(mine, x // 2 * (n_cols // 2), n_cols // 2, 0)
-    moved = lax.ppermute(quarter, AXES, transposition())
     other = swap(mine, "core", 2, 1)
     v_rows, w_part = rows_call(mine.reshape(-1, shard, kdim), other.reshape(-1, shard, kdim), window)
     w_part = reduce_scatter(w_part, "y", 4)
     near = swap(moved, "y", 4, 1)
+    pair = jnp.stack([moved, near]).reshape(2, -1, shard, kdim)
+    far = swap(pair, "y", 4, 2)
     w_slice = reduce_scatter(w_part, "zh", 4)
 
-    v_cols, keep, send, tail = cols_call(moved.reshape(-1, shard, kdim), near.reshape(-1, shard, kdim), col_check, window)
+    v_cols, keep, send, tail = cols_call(pair, far, col_check, window)
     x_part = keep + swap(send, "core", 2, 1)
     small = jnp.concatenate([dot(w_slice, v_cols), tail], axis=0)
     x_part, small = reduce_both(x_part, small, "x", 4)
     both = jnp.concatenate([x_part, small], axis=0)
-    parts = gather(both, "zl", 4).reshape((4,) + both.shape)
+    total = jnp.sum(gather(both, "zl", 4).reshape((4,) + both.shape), axis=0)
     turned, row_part = prep_call(v_rows, factor, row_check)
-    y_parts, small = spread_call(parts, factor, x_part.shape[0])
-    y_rows = exchange(y_parts, "x").reshape(n_rows // 2, kdim)
+    tall = x_part.shape[0]
+    small = total[tall:]
+    y_rows = gather(dot(total[:tall], jnp.triu(factor)), "x", 4)
     y_far = swap(y_rows, "core", 2, 1)
     small_far = swap(small, "core", 2, 1)
     g_parts, vectors = slice_call(small, small_far, w_slice, v_cols, factor, row_part)

time: 190 us -> 188 us (0.989)
  blocking collectives: 51 us -> 35.6 us
  waiting for transfers between devices: 44.1 us -> 58.2 us
  Pallas kernels: 25.3 us -> 23.3 us
    all_to_all x4 -> x3, blocking collectives: 51 us -> 35.6 us  [exchange(): return lax.all_to_all(parts, axis, 0, 0)]
    all_to_all x5 -> x6, waiting for transfers between devices: 30.8 us -> 44.4 us  [exchange(): return lax.all_to_all(parts, axis, 0, 0)]
    ppermute x5 -> x6, waiting for transfers between devices: 0.01 us -> 6.06 us  [swap(): return lax.ppermute(block, axis, [(i, i ^ bit) for i in range(size)])]
    ppermute x1, waiting for transfers between devices: 13.3 us -> 7.72 us  [on_device(): moved = lax.ppermute(line, AXES, transposition())]
    pallas_call x1 -> x0, Pallas kernels: 1.98 us -> none  [spread_call(): pl.pallas_call(spread_kernel, in_specs=[VMEM] * 2, out_specs=[VMEM] * 2,...]
    ppermute x5 -> x6, starting transfers between devices: 10.9 us -> 12.8 us  [swap(): return lax.ppermute(block, axis, [(i, i ^ bit) for i in range(size)])]
    all_to_all x5 -> x6, starting transfers between devices: 43.1 us -> 42.3 us  [exchange(): return lax.all_to_all(parts, axis, 0, 0)]
  transfers between devices with their start and end apart: 11 -> 13, of which waited for: 5 -> 7; matrix products, arithmetic and copies ran while one was open for 1% -> 1% of each run, Pallas kernels for 10% -> 10%
where the time goes in v6:
time: 188 us; the launch traced here: 187 us
  starting transfers between devices  61.7 us (33%)
  waiting for transfers between devices  58.2 us (31%)
  blocking collectives  35.6 us (19%)
  Pallas kernels  23.3 us (12%)
  local copies, waits for them, and re-layouts  5.07 us (3%)
  other arithmetic  2.02 us (1%)
    all_to_all x6, waiting for transfers between devices, exchange(): return lax.all_to_all(parts, axis, 0, 0)  44.4 us
    all_to_all x6, starting transfers between devices, exchange(): return lax.all_to_all(parts, axis, 0, 0)  42.3 us
    all_to_all x3, blocking collectives, exchange(): return lax.all_to_all(parts, axis, 0, 0)  35.6 us
    ppermute x6, starting transfers between devices, swap(): return lax.ppermute(block, axis, [(i, i ^ bit) for i in range(size)])  12.8 us
    ppermute x1, waiting for transfers between devices, on_device(): moved = lax.ppermute(line, AXES, transposition())  7.72 us
    ppermute x1, starting transfers between devices, on_device(): moved = lax.ppermute(line, AXES, transposition())  6.52 us
    ppermute x6, waiting for transfers between devices, swap(): return lax.ppermute(block, axis, [(i, i ^ bit) for i in range(size)])  6.06 us
    pallas_call x1, Pallas kernels, left_call(): pl.pallas_call(left_kernel, in_specs=[VMEM] * 7 + [HBM], out_specs=[VMEM,...  5.41 us
  transfers between devices with their start and end apart: 13, of which 7 were waited for; matrix products, arithmetic and copies ran while one was open for 1% of the time, Pallas kernels for 10%

profile of v6, /device:TPU:6, one launch (start us, length us, event | category | flops | bytes accessed | tf_op | source)
XLA Modules:
  0.0 187.2 jit_solution(2889575306434172309)
XLA Ops:
  1.4 11.8 %all_to_all.45 = f32[4,32,256]{2,1,0:T(8,128)S(1)} all-to-all(f32[4,32,256]{2,1,0:T(8,128)S(1)} %broadcast_in_dim.18), channel_id=1, replica_groups=mesh['y'=4,'zh'=4,'x'=4,'zl'=4,'core'=2] {'zl'}, dimensions={0} | all-to-all | bytes 262144 | tf_op jit(solution)/shard_map/all_to_all | solution.py:28
  13.2 10.8 %all_to_all.46 = f32[4,128,256]{2,1,0:T(8,128)S(1)} all-to-all(f32[4,128,256]{2,1,0:T(8,128)S(1)} %broadcast_in_dim.19), channel_id=1, replica_groups=mesh['y'=4,'zh'=4,'x'=4,'zl'=4,'core'=2] {'x'}, dimensions={0} | all-to-all | bytes 1048576 | tf_op jit(solution)/shard_map/all_to_all | solution.py:28
  25.9 6.5 %collective-permute-start = (f32[128,256]{1,0:T(8,128)S(1)}, f32[128,256]{1,0:T(8,128)S(1)}, u32[]{:S(2)}, u32[]{:S(2)}) collective-permute-start(f32[128,256]{1,0:T(8,128)S(1)} %bitcast.27), channel_id=1, source_target_pairs={{0,0},{1,128},{2,32},{3,160},{4,64},{5,192},{6,96},{7,224},{8,256}... | collective-permute-start | bytes 393224 | tf_op jit(solution)/shard_map/ppermute | solution.py:373
  32.4 7.7 %collective-permute-done = f32[128,256]{1,0:T(8,128)S(1)} collective-permute-done((f32[128,256]{1,0:T(8,128)S(1)}, f32[128,256]{1,0:T(8,128)S(1)}, u32[]{:S(2)}, u32[]{:S(2)}) %collective-permute-start) | collective-permute-done | bytes 131104 | tf_op jit(solution)/shard_map/ppermute | solution.py:373
  40.2 2.8 %collective-permute-start.1 = (f32[128,256]{1,0:T(8,128)S(1)}, f32[128,256]{1,0:T(8,128)S(1)}, u32[]{:S(2)}, u32[]{:S(2)}) collective-permute-start(f32[128,256]{1,0:T(8,128)S(1)} %collective-permute-done), channel_id=1, source_target_pairs={{0,128},{128,0},{256,384},{384,256},{1,129},{129,1},{257,385},{385... | collective-permute-start | bytes 393224 | tf_op jit(solution)/shard_map/ppermute | solution.py:50
  42.9 5.2 %collective-permute-done.1 = f32[128,256]{1,0:T(8,128)S(1)} collective-permute-done((f32[128,256]{1,0:T(8,128)S(1)}, f32[128,256]{1,0:T(8,128)S(1)}, u32[]{:S(2)}, u32[]{:S(2)}) %collective-permute-start.1) | collective-permute-done | bytes 131104 | tf_op jit(solution)/shard_map/ppermute | solution.py:50
  50.1 3.5 %rows.1 = (f32[1024,256]{1,0:T(8,128)S(1)}, f32[256,512]{1,0:T(8,128)}) custom-call(f32[16,32,256]{2,1,0:T(8,128)S(1)} %bitcast.22, f32[16,32,256]{2,1,0:T(8,128)S(1)} %bitcast.23, f32[1024,512]{1,0:T(8,128)} %window_ref.5), custom_call_target="tpu_custom_call" | custom-call | tf_op jit(solution)/shard_map/rows/pallas_call | solution.py:160
  53.6 4.8 %all-to-all-start.2 = ((f32[4,64,512]{2,1,0:T(8,128)}), f32[4,64,512]{2,1,0:T(8,128)}, u32[]{:S(2)}, u32[]{:S(2)}) async-start(f32[4,64,512]{2,1,0:T(8,128)} %bitcast.8), calls=%async_computation.2 | async-start | bytes 1048576 | tf_op jit(solution)/shard_map/all_to_all | solution.py:28
  60.9 4.0 %cols.1 = (f32[512,256]{1,0:T(8,128)S(1)}, f32[512,256]{1,0:T(8,128)S(1)}, f32[512,256]{1,0:T(8,128)S(1)}, f32[8,256]{1,0:T(8,128)S(1)}) custom-call(f32[2,4,32,256]{3,2,1,0:T(8,128)S(1)} %pad_maximum_fusion.1.own_ref, f32[2,4,32,256]{3,2,1,0:T(8,128)S(1)} %copy-done.2, f32[1,512]{1,0:T(1,128)} %bitcast.32, f32[1024,512]{1,0:T(8,128)} %window_ref.5), custom_call_target="tpu_custom_call" | custom-call | tf_op jit(solution)/shard_map/cols/pallas_call | solution.py:209
  68.6 20.3 %all-to-all-start.3 = ((f32[4,16,512]{2,1,0:T(8,128)}), f32[4,16,512]{2,1,0:T(8,128)S(1)}, u32[]{:S(2)}, u32[]{:S(2)}) async-start(f32[4,16,512]{2,1,0:T(8,128)} %bitcast.9), calls=%async_computation.3 | async-start | bytes 262144 | tf_op jit(solution)/shard_map/all_to_all | solution.py:28
  89.0 13.5 %all-to-all-done.3 = f32[4,16,512]{2,1,0:T(8,128)S(1)} async-done(((f32[4,16,512]{2,1,0:T(8,128)}), f32[4,16,512]{2,1,0:T(8,128)S(1)}, u32[]{:S(2)}, u32[]{:S(2)}) %all-to-all-start.3) | async-done | bytes 131104 | tf_op jit(solution)/shard_map/all_to_all | solution.py:28
  102.8 13.1 %all_to_all.47 = f32[4,152,256]{2,1,0:T(8,128)S(1)} all-to-all(f32[4,152,256]{2,1,0:T(8,128)S(1)} %pad_maximum_fusion), channel_id=1, replica_groups=mesh['y'=4,'zh'=4,'x'=4,'zl'=4,'core'=2] {'x'}, dimensions={0} | all-to-all | bytes 1245184 | tf_op jit(solution)/shard_map/all_to_all | solution.py:28
  116.8 3.5 %all-to-all-start.5 = ((f32[4,152,256]{2,1,0:T(8,128)}), f32[4,152,256]{2,1,0:T(8,128)S(1)}, u32[]{:S(2)}, u32[]{:S(2)}) async-start(f32[4,152,256]{2,1,0:T(8,128)} %broadcast_in_dim.21), calls=%async_computation.5 | async-start | bytes 1245184 | tf_op jit(solution)/shard_map/all_to_all | solution.py:28
  120.3 13.6 %all-to-all-done.5 = f32[4,152,256]{2,1,0:T(8,128)S(1)} async-done(((f32[4,152,256]{2,1,0:T(8,128)}), f32[4,152,256]{2,1,0:T(8,128)S(1)}, u32[]{:S(2)}, u32[]{:S(2)}) %all-to-all-start.5) | async-done | bytes 622624 | tf_op jit(solution)/shard_map/all_to_all | solution.py:28
  135.1 5.5 %all-to-all-start.8 = ((f32[4,128,256]{2,1,0:T(8,128)}), f32[4,128,256]{2,1,0:T(8,128)S(1)}, u32[]{:S(2)}, u32[]{:S(2)}) async-start(f32[4,128,256]{2,1,0:T(8,128)} %broadcast_in_dim.47), calls=%async_computation.8 | async-start | bytes 1048576 | tf_op jit(solution)/shard_map/all_to_all | solution.py:28
  142.5 3.3 %prep.1 = (bf16[1024,768]{1,0:T(8,128)(2,1)}, f32[1,256]{1,0:T(1,128)}) custom-call(f32[1024,256]{1,0:T(8,128)} %copy-done, f32[256,256]{1,0:T(8,128)} %u_ref.5, f32[1,1024]{1,0:T(1,128)} %bitcast.30), custom_call_target="tpu_custom_call" | custom-call | tf_op jit(solution)/shard_map/prep/pallas_call | solution.py:234
  145.8 2.2 %slice.16 = (f32[4,16,640]{2,1,0:T(8,128)}, f32[8,256]{1,0:T(8,128)S(1)}) custom-call(f32[24,256]{1,0:T(8,128)S(1)} %slice.12.own_ref, f32[24,256]{1,0:T(8,128)S(1)} %collective-permute-done.5.far_ref, f32[16,512]{1,0:T(8,128)S(1)} %reduce_sum.37.w_ref, f32[512,256]{1,0:T(8,128)S(1)} %get-tuple-element.22.c_ref, f32[256,256]{1,0:T(8,128)} %u_ref.5, ...), custom_call_target="tpu_custom_call" | custom-call | tf_op jit(solution)/shard_map/slice/pallas_call | solution.py:271
  148.0 3.3 %all-to-all-start.6 = ((f32[4,16,640]{2,1,0:T(8,128)}), f32[4,16,640]{2,1,0:T(8,128)S(1)}, u32[]{:S(2)}, u32[]{:S(2)}) async-start(f32[4,16,640]{2,1,0:T(8,128)} %get-tuple-element.26), calls=%async_computation.6 | async-start | bytes 327680 | tf_op jit(solution)/shard_map/all_to_all | solution.py:28
  151.4 2.4 %collective-permute-start.6 = (f32[512,256]{1,0:T(8,128)S(1)}, f32[512,256]{1,0:T(8,128)S(1)}, u32[]{:S(2)}, u32[]{:S(2)}) collective-permute-start(f32[512,256]{1,0:T(8,128)S(1)} %bitcast.19), channel_id=1, source_target_pairs={{0,1},{1,0},{2,3},{3,2},{4,5},{5,4},{6,7},{7,6},{8,9},{9,8},{10,11... | collective-permute-start | bytes 1572872 | tf_op jit(solution)/shard_map/ppermute | solution.py:50
  153.8 13.9 %all-to-all-done.6 = f32[4,16,640]{2,1,0:T(8,128)S(1)} async-done(((f32[4,16,640]{2,1,0:T(8,128)}), f32[4,16,640]{2,1,0:T(8,128)S(1)}, u32[]{:S(2)}, u32[]{:S(2)}) %all-to-all-start.6) | async-done | bytes 163872 | tf_op jit(solution)/shard_map/all_to_all | solution.py:28
  168.6 4.9 %all-to-all-start.7 = ((f32[4,64,640]{2,1,0:T(8,128)}), f32[4,64,640]{2,1,0:T(8,128)S(1)}, u32[]{:S(2)}, u32[]{:S(2)}) async-start(f32[4,64,640]{2,1,0:T(8,128)} %broadcast_in_dim.23), calls=%async_computation.7 | async-start | bytes 1310720 | tf_op jit(solution)/shard_map/all_to_all | solution.py:28
  173.5 5.4 %left.1 = (f32[1,1024]{1,0:T(1,128)S(1)}, f32[1,512]{1,0:T(1,128)S(1)}, f32[1024,512]{1,0:T(8,128)}) custom-call(f32[512,256]{1,0:T(8,128)S(1)} %bitcast.20, f32[512,256]{1,0:T(8,128)S(1)} %collective-permute-done.6.far_ref, f32[512,256]{1,0:T(8,128)S(1)} %get-tuple-element.22.c_ref, f32[256,256]{1,0:T(8,128)} %u_ref.5, ...), custom_call_target="tpu_custom_call" | custom-call | tf_op jit(solution)/shard_map/left/pallas_call | solution.py:306
  178.9 3.4 %all-to-all-done.7 = f32[4,64,640]{2,1,0:T(8,128)S(1)} async-done(((f32[4,64,640]{2,1,0:T(8,128)}), f32[4,64,640]{2,1,0:T(8,128)S(1)}, u32[]{:S(2)}, u32[]{:S(2)}) %all-to-all-start.7) | async-done | bytes 655392 | tf_op jit(solution)/shard_map/all_to_all | solution.py:28
  182.2 5.0 %right.1 = (f32[1,1024]{1,0:T(1,128)}, f32[1,512]{1,0:T(1,128)}, f32[1024,512]{1,0:T(8,128)}) custom-call(f32[256,640]{1,0:T(8,128)S(1)} %bitcast.18, f32[8,256]{1,0:T(8,128)S(1)} %get-tuple-element.27.vec_ref, f32[1,1024]{1,0:T(1,128)S(1)} %get-tuple-element.28.row_ref, f32[1,512]{1,0:T(1,128)S(1)} %get-tuple-element.29.col_ref, ...), custom_call_target="tpu_custom_call" | custom-call | tf_op jit(solution)/shard_map/right/pallas_call | solution.py:357
  (37 shorter events, 16.1 us)
Async XLA Ops:
  24.0 26.1 %collective-permute-start.4 = (f32[512,256]{1,0:T(8,128)S(1)}, f32[512,256]{1,0:T(8,128)S(1)}, u32[]{:S(2)}, u32[]{:S(2)}) collective-permute-start(f32[512,256]{1,0:T(8,128)S(1)} %bitcast.21), channel_id=1, source_target_pairs={{0,1},{1,0},{2,3},{3,2},{4,5},{5,4},{6,7},{7,6},{8,9},{9,8},{10,11... | collective-permute-start | bytes 1572872 | tf_op jit(solution)/shard_map/ppermute | solution.py:50
  25.9 14.2 %collective-permute-start = (f32[128,256]{1,0:T(8,128)S(1)}, f32[128,256]{1,0:T(8,128)S(1)}, u32[]{:S(2)}, u32[]{:S(2)}) collective-permute-start(f32[128,256]{1,0:T(8,128)S(1)} %bitcast.27), channel_id=1, source_target_pairs={{0,0},{1,128},{2,32},{3,160},{4,64},{5,192},{6,96},{7,224},{8,256}... | collective-permute-start | bytes 393224 | tf_op jit(solution)/shard_map/ppermute | solution.py:373
  40.2 8.0 %collective-permute-start.1 = (f32[128,256]{1,0:T(8,128)S(1)}, f32[128,256]{1,0:T(8,128)S(1)}, u32[]{:S(2)}, u32[]{:S(2)}) collective-permute-start(f32[128,256]{1,0:T(8,128)S(1)} %collective-permute-done), channel_id=1, source_target_pairs={{0,128},{128,0},{256,384},{384,256},{1,129},{129,1},{257,385},{385... | collective-permute-start | bytes 393224 | tf_op jit(solution)/shard_map/ppermute | solution.py:50
  48.2 11.0 %collective-permute-start.2 = (f32[2,4,32,256]{3,2,1,0:T(8,128)S(1)}, f32[2,4,32,256]{3,2,1,0:T(8,128)S(1)}, u32[]{:S(2)}, u32[]{:S(2)}) collective-permute-start(f32[2,4,32,256]{3,2,1,0:T(8,128)S(1)} %pad_maximum_fusion.1.own_ref), channel_id=1, source_target_pairs={{0,256},{128,384},{256,0},{384,128},{1,257},{129,385},{257,1},{385... | collective-permute-start | bytes 786440 | tf_op jit(solution)/shard_map/ppermute | solution.py:50
  53.6 5.6 %copy-start = (f32[1024,256]{1,0:T(8,128)}, f32[1024,256]{1,0:T(8,128)S(1)}, u32[]{:S(2)}) copy-start(f32[1024,256]{1,0:T(8,128)S(1)} %get-tuple-element.24.v_ref) | copy-start | bytes 3145732
  53.6 13.3 %all-to-all-start.2 = ((f32[4,64,512]{2,1,0:T(8,128)}), f32[4,64,512]{2,1,0:T(8,128)}, u32[]{:S(2)}, u32[]{:S(2)}) async-start(f32[4,64,512]{2,1,0:T(8,128)} %bitcast.8), calls=%async_computation.2 | async-start | bytes 1048576 | tf_op jit(solution)/shard_map/all_to_all | solution.py:28
  59.2 0.7 copy-start.1
  60.0 0.9 copy-start.2
  64.9 24.0 %collective-permute-start.3 = (f32[512,256]{1,0:T(8,128)S(1)}, f32[512,256]{1,0:T(8,128)S(1)}, u32[]{:S(2)}, u32[]{:S(2)}) collective-permute-start(f32[512,256]{1,0:T(8,128)S(1)} %get-tuple-element.20), channel_id=1, source_target_pairs={{0,1},{1,0},{2,3},{3,2},{4,5},{5,4},{6,7},{7,6},{8,9},{9,8},{10,11... | collective-permute-start | bytes 1572872 | tf_op jit(solution)/shard_map/ppermute | solution.py:50
  68.6 33.8 %all-to-all-start.3 = ((f32[4,16,512]{2,1,0:T(8,128)}), f32[4,16,512]{2,1,0:T(8,128)S(1)}, u32[]{:S(2)}, u32[]{:S(2)}) async-start(f32[4,16,512]{2,1,0:T(8,128)} %bitcast.9), calls=%async_computation.3 | async-start | bytes 262144 | tf_op jit(solution)/shard_map/all_to_all | solution.py:28
  115.9 18.1 %copy-start.3 = (f32[256,256]{1,0:T(8,128)S(1)}, f32[256,256]{1,0:T(8,128)}, u32[]{:S(2)}) copy-start(f32[256,256]{1,0:T(8,128)} %u_ref.5) | copy-start | bytes 786436
  116.8 17.1 %all-to-all-start.5 = ((f32[4,152,256]{2,1,0:T(8,128)}), f32[4,152,256]{2,1,0:T(8,128)S(1)}, u32[]{:S(2)}, u32[]{:S(2)}) async-start(f32[4,152,256]{2,1,0:T(8,128)} %broadcast_in_dim.21), calls=%async_computation.5 | async-start | bytes 1245184 | tf_op jit(solution)/shard_map/all_to_all | solution.py:28
  135.1 12.9 %all-to-all-start.8 = ((f32[4,128,256]{2,1,0:T(8,128)}), f32[4,128,256]{2,1,0:T(8,128)S(1)}, u32[]{:S(2)}, u32[]{:S(2)}) async-start(f32[4,128,256]{2,1,0:T(8,128)} %broadcast_in_dim.47), calls=%async_computation.8 | async-start | bytes 1048576 | tf_op jit(solution)/shard_map/all_to_all | solution.py:28
  140.6 5.2 %collective-permute-start.5 = (f32[24,256]{1,0:T(8,128)S(1)}, f32[24,256]{1,0:T(8,128)S(1)}, u32[]{:S(2)}, u32[]{:S(2)}) collective-permute-start(f32[24,256]{1,0:T(8,128)S(1)} %slice.12.own_ref), channel_id=1, source_target_pairs={{0,1},{1,0},{2,3},{3,2},{4,5},{5,4},{6,7},{7,6},{8,9},{9,8},{10,11... | collective-permute-start | bytes 73736 | tf_op jit(solution)/shard_map/ppermute | solution.py:50
  148.0 19.7 %all-to-all-start.6 = ((f32[4,16,640]{2,1,0:T(8,128)}), f32[4,16,640]{2,1,0:T(8,128)S(1)}, u32[]{:S(2)}, u32[]{:S(2)}) async-start(f32[4,16,640]{2,1,0:T(8,128)} %get-tuple-element.26), calls=%async_computation.6 | async-start | bytes 327680 | tf_op jit(solution)/shard_map/all_to_all | solution.py:28
  151.4 22.1 %collective-permute-start.6 = (f32[512,256]{1,0:T(8,128)S(1)}, f32[512,256]{1,0:T(8,128)S(1)}, u32[]{:S(2)}, u32[]{:S(2)}) collective-permute-start(f32[512,256]{1,0:T(8,128)S(1)} %bitcast.19), channel_id=1, source_target_pairs={{0,1},{1,0},{2,3},{3,2},{4,5},{5,4},{6,7},{7,6},{8,9},{9,8},{10,11... | collective-permute-start | bytes 1572872 | tf_op jit(solution)/shard_map/ppermute | solution.py:50
  168.6 13.7 %all-to-all-start.7 = ((f32[4,64,640]{2,1,0:T(8,128)}), f32[4,64,640]{2,1,0:T(8,128)S(1)}, u32[]{:S(2)}, u32[]{:S(2)}) async-start(f32[4,64,640]{2,1,0:T(8,128)} %broadcast_in_dim.23), calls=%async_computation.7 | async-start | bytes 1310720 | tf_op jit(solution)/shard_map/all_to_all | solution.py:28

commit v7 on v6

--- a/solution.py
+++ b/solution.py
@@ -216,8 +216,9 @@
     )(vmem(own), vmem(far), check.reshape(1, n_cols), window)
 
 
-def prep_kernel(v_ref, u_ref, check_ref, turned_ref, part_ref):
-    upper = right3(triu(u_ref), 1)
+def prep_kernel(v_ref, u_ref, check_ref, turned_ref, part_ref, upper_ref):
+    upper_ref[...] = triu(u_ref)
+    upper = right3(upper_ref[...], 1)
     rows = v_ref.shape[0] // STEPS
     total = None
     for step in range(STEPS):
@@ -234,8 +235,8 @@
     return pl.pallas_call(
         prep_kernel,
         in_specs=[VMEM] * 3,
-        out_specs=[VMEM] * 2,
-        out_shape=[jax.ShapeDtypeStruct((n_rows, 3 * kdim), jnp.bfloat16), far_f32(1, kdim)],
+        out_specs=[VMEM] * 3,
+        out_shape=[jax.ShapeDtypeStruct((n_rows, 3 * kdim), jnp.bfloat16), near_f32(1, kdim), near_f32(kdim, kdim)],
         name="prep",
     )(v_rows, factor, check.reshape(1, n_rows))
 
@@ -244,7 +245,7 @@
     k_rows, n_cols = w_ref.shape
     kdim = u_ref.shape[0]
     small = own_ref[...] + far_ref[...]
-    upper = triu(u_ref)
+    upper = u_ref[...]
     scaled = small[k_rows + 1 : k_rows + 2] / math.sqrt(N)
     line = lax.broadcasted_iota(jnp.int32, (8, kdim), 0)
     turned = mm(jnp.broadcast_to(scaled, (8, kdim)), upper, NT)
@@ -274,7 +275,7 @@
         out_specs=[VMEM] * 2,
         out_shape=[near_f32(4, k_rows, n_cols + LANES), near_f32(8, kdim)],
         name="slice",
-    )(vmem(own), vmem(far), vmem(w_slice), vmem(v_cols), factor, part)
+    )(vmem(own), vmem(far), vmem(w_slice), vmem(v_cols), vmem(factor), vmem(part))
 
 
 def left_kernel(own_ref, far_ref, c_ref, u_ref, vec_ref, row_ref, col_ref, window_ref, nrow_ref, ncol_ref, out_ref, buf, sems, done):
@@ -282,7 +283,7 @@
         block_copy(window_ref, buf, sems, step).start()
     right = right3(c_ref[...], 1)
     vec = vec_ref[...]
-    turned = mm(vec, triu(u_ref), NN)
+    turned = mm(vec, u_ref[...], NN)
     ncol_ref[...] = col_ref[...] - mm3(left3(turned, 1), right, NT)[1:2]
     vec = left3(vec, 1)
     half, rows = STEPS // 2, window_ref.shape[0] // STEPS
@@ -311,10 +312,10 @@
         scratch_shapes=staged((n_rows, n_cols)) + [pltpu.SemaphoreType.DMA((STEPS,))],
         name="left",
     )(
-        vmem(own),
+        own,
         vmem(far),
         vmem(v_cols),
-        factor,
+        vmem(factor),
         vmem(vectors),
         row_check.reshape(1, n_rows),
         col_check.reshape(1, n_cols),
@@ -386,17 +387,17 @@
     x_part, small = reduce_both(x_part, small, "x", 4)
     both = jnp.concatenate([x_part, small], axis=0)
     total = jnp.sum(gather(both, "zl", 4).reshape((4,) + both.shape), axis=0)
-    turned, row_part = prep_call(v_rows, factor, row_check)
+    turned, row_part, upper = prep_call(v_rows, factor, row_check)
     tall = x_part.shape[0]
     small = total[tall:]
-    y_rows = gather(dot(total[:tall], jnp.triu(factor)), "x", 4)
+    y_rows = gather(dot(total[:tall], upper), "x", 4)
     y_far = swap(y_rows, "core", 2, 1)
     small_far = swap(small, "core", 2, 1)
-    g_parts, vectors = slice_call(small, small_far, w_slice, v_cols, factor, row_part)
+    g_parts, vectors = slice_call(small, small_far, w_slice, v_cols, upper, row_part)
     g_some = exchange(g_parts, "zh").reshape(-1, n_cols + LANES)
     g_all = gather(g_some, "y", 4)
 
-    new_row, new_col, partly = left_call(y_rows, y_far, v_cols, factor, vectors, row_check, col_check, window)
+    new_row, new_col, partly = left_call(y_rows, y_far, v_cols, upper, vectors, row_check, col_check, window)
     new_row, new_col, new_window = right_call(g_all, vectors, new_row, new_col, turned, partly)
     return new_window, new_col.reshape(n_cols), new_row.reshape(n_rows)
 

time: 188 us -> 184 us (0.979)
    all_to_all x6, waiting for transfers between devices: 44.4 us -> 41.9 us  [exchange(): return lax.all_to_all(parts, axis, 0, 0)]
  transfers between devices with their start and end apart: 13 -> 13, of which waited for: 7 -> 9; matrix products, arithmetic and copies ran while one was open for 1% -> 1% of each run, Pallas kernels for 10% -> 9%
where the time goes in v7:
time: 184 us; the launch traced here: 183 us
  starting transfers between devices  61 us (33%)
  waiting for transfers between devices  56.8 us (31%)
  blocking collectives  35.7 us (19%)
  Pallas kernels  22 us (12%)
  local copies, waits for them, and re-layouts  5.06 us (3%)
    all_to_all x6, starting transfers between devices, exchange(): return lax.all_to_all(parts, axis, 0, 0)  42.1 us
    all_to_all x6, waiting for transfers between devices, exchange(): return lax.all_to_all(parts, axis, 0, 0)  41.9 us
    all_to_all x3, blocking collectives, exchange(): return lax.all_to_all(parts, axis, 0, 0)  35.7 us
    ppermute x6, starting transfers between devices, swap(): return lax.ppermute(block, axis, [(i, i ^ bit) for i in range(size)])  12.3 us
    ppermute x1, waiting for transfers between devices, on_device(): moved = lax.ppermute(line, AXES, transposition())  7.72 us
    ppermute x6, waiting for transfers between devices, swap(): return lax.ppermute(block, axis, [(i, i ^ bit) for i in range(size)])  7.26 us
    ppermute x1, starting transfers between devices, on_device(): moved = lax.ppermute(line, AXES, transposition())  6.52 us
    pallas_call x1, Pallas kernels, left_call(): pl.pallas_call(left_kernel, in_specs=[VMEM] * 7 + [HBM], out_specs=[VMEM,...  4.99 us
  transfers between devices with their start and end apart: 13, of which 9 were waited for; matrix products, arithmetic and copies ran while one was open for 1% of the time, Pallas kernels for 9%

profile of v7, /device:TPU:6, one launch (start us, length us, event | category | flops | bytes accessed | tf_op | source)
XLA Modules:
  0.0 182.8 jit_solution(16190857975104141845)
XLA Ops:
  1.4 11.8 %all_to_all.45 = f32[4,32,256]{2,1,0:T(8,128)S(1)} all-to-all(f32[4,32,256]{2,1,0:T(8,128)S(1)} %broadcast_in_dim.14), channel_id=1, replica_groups=mesh['y'=4,'zh'=4,'x'=4,'zl'=4,'core'=2] {'zl'}, dimensions={0} | all-to-all | bytes 262144 | tf_op jit(solution)/shard_map/all_to_all | solution.py:28
  13.2 10.8 %all_to_all.46 = f32[4,128,256]{2,1,0:T(8,128)S(1)} all-to-all(f32[4,128,256]{2,1,0:T(8,128)S(1)} %broadcast_in_dim.15), channel_id=1, replica_groups=mesh['y'=4,'zh'=4,'x'=4,'zl'=4,'core'=2] {'x'}, dimensions={0} | all-to-all | bytes 1048576 | tf_op jit(solution)/shard_map/all_to_all | solution.py:28
  25.9 6.5 %collective-permute-start = (f32[128,256]{1,0:T(8,128)S(1)}, f32[128,256]{1,0:T(8,128)S(1)}, u32[]{:S(2)}, u32[]{:S(2)}) collective-permute-start(f32[128,256]{1,0:T(8,128)S(1)} %bitcast.28), channel_id=1, source_target_pairs={{0,0},{1,128},{2,32},{3,160},{4,64},{5,192},{6,96},{7,224},{8,256}... | collective-permute-start | bytes 393224 | tf_op jit(solution)/shard_map/ppermute | solution.py:374
  32.4 7.7 %collective-permute-done = f32[128,256]{1,0:T(8,128)S(1)} collective-permute-done((f32[128,256]{1,0:T(8,128)S(1)}, f32[128,256]{1,0:T(8,128)S(1)}, u32[]{:S(2)}, u32[]{:S(2)}) %collective-permute-start) | collective-permute-done | bytes 131104 | tf_op jit(solution)/shard_map/ppermute | solution.py:374
  40.2 2.8 %collective-permute-start.1 = (f32[128,256]{1,0:T(8,128)S(1)}, f32[128,256]{1,0:T(8,128)S(1)}, u32[]{:S(2)}, u32[]{:S(2)}) collective-permute-start(f32[128,256]{1,0:T(8,128)S(1)} %collective-permute-done), channel_id=1, source_target_pairs={{0,128},{128,0},{256,384},{384,256},{1,129},{129,1},{257,385},{385... | collective-permute-start | bytes 393224 | tf_op jit(solution)/shard_map/ppermute | solution.py:50
  42.9 5.2 %collective-permute-done.1 = f32[128,256]{1,0:T(8,128)S(1)} collective-permute-done((f32[128,256]{1,0:T(8,128)S(1)}, f32[128,256]{1,0:T(8,128)S(1)}, u32[]{:S(2)}, u32[]{:S(2)}) %collective-permute-start.1) | collective-permute-done | bytes 131104 | tf_op jit(solution)/shard_map/ppermute | solution.py:50
  48.2 1.9 %collective-permute-start.2 = (f32[2,4,32,256]{3,2,1,0:T(8,128)S(1)}, f32[2,4,32,256]{3,2,1,0:T(8,128)S(1)}, u32[]{:S(2)}, u32[]{:S(2)}) collective-permute-start(f32[2,4,32,256]{3,2,1,0:T(8,128)S(1)} %pad_maximum_fusion.1.own_ref), channel_id=1, source_target_pairs={{0,256},{128,384},{256,0},{384,128},{1,257},{129,385},{257,1},{385... | collective-permute-start | bytes 786440 | tf_op jit(solution)/shard_map/ppermute | solution.py:50
  50.1 3.4 %rows.1 = (f32[1024,256]{1,0:T(8,128)S(1)}, f32[256,512]{1,0:T(8,128)}) custom-call(f32[16,32,256]{2,1,0:T(8,128)S(1)} %bitcast.21, f32[16,32,256]{2,1,0:T(8,128)S(1)} %bitcast.22, f32[1024,512]{1,0:T(8,128)} %window_ref.5), custom_call_target="tpu_custom_call" | custom-call | tf_op jit(solution)/shard_map/rows/pallas_call | solution.py:160
  53.6 4.8 %all-to-all-start.2 = ((f32[4,64,512]{2,1,0:T(8,128)}), f32[4,64,512]{2,1,0:T(8,128)S(1)}, u32[]{:S(2)}, u32[]{:S(2)}) async-start(f32[4,64,512]{2,1,0:T(8,128)} %bitcast.8), calls=%async_computation.2 | async-start | bytes 1048576 | tf_op jit(solution)/shard_map/all_to_all | solution.py:28
  60.9 4.0 %cols.1 = (f32[512,256]{1,0:T(8,128)S(1)}, f32[512,256]{1,0:T(8,128)S(1)}, f32[512,256]{1,0:T(8,128)S(1)}, f32[8,256]{1,0:T(8,128)S(1)}) custom-call(f32[2,4,32,256]{3,2,1,0:T(8,128)S(1)} %pad_maximum_fusion.1.own_ref, f32[2,4,32,256]{3,2,1,0:T(8,128)S(1)} %copy-done.2, f32[1,512]{1,0:T(1,128)} %bitcast.33, f32[1024,512]{1,0:T(8,128)} %window_ref.5), custom_call_target="tpu_custom_call" | custom-call | tf_op jit(solution)/shard_map/cols/pallas_call | solution.py:209
  64.9 1.9 %collective-permute-start.3 = (f32[512,256]{1,0:T(8,128)S(1)}, f32[512,256]{1,0:T(8,128)S(1)}, u32[]{:S(2)}, u32[]{:S(2)}) collective-permute-start(f32[512,256]{1,0:T(8,128)S(1)} %get-tuple-element.21), channel_id=1, source_target_pairs={{0,1},{1,0},{2,3},{3,2},{4,5},{5,4},{6,7},{7,6},{8,9},{9,8},{10,11... | collective-permute-start | bytes 1572872 | tf_op jit(solution)/shard_map/ppermute | solution.py:50
  67.6 19.8 %all-to-all-start.3 = ((f32[4,16,512]{2,1,0:T(8,128)}), f32[4,16,512]{2,1,0:T(8,128)S(1)}, u32[]{:S(2)}, u32[]{:S(2)}) async-start(f32[4,16,512]{2,1,0:T(8,128)} %bitcast.9), calls=%async_computation.3 | async-start | bytes 262144 | tf_op jit(solution)/shard_map/all_to_all | solution.py:28
  87.4 13.1 %all-to-all-done.3 = f32[4,16,512]{2,1,0:T(8,128)S(1)} async-done(((f32[4,16,512]{2,1,0:T(8,128)}), f32[4,16,512]{2,1,0:T(8,128)S(1)}, u32[]{:S(2)}, u32[]{:S(2)}) %all-to-all-start.3) | async-done | bytes 131104 | tf_op jit(solution)/shard_map/all_to_all | solution.py:28
  100.9 13.2 %all_to_all.47 = f32[4,152,256]{2,1,0:T(8,128)S(1)} all-to-all(f32[4,152,256]{2,1,0:T(8,128)S(1)} %pad_maximum_fusion), channel_id=1, replica_groups=mesh['y'=4,'zh'=4,'x'=4,'zl'=4,'core'=2] {'x'}, dimensions={0} | all-to-all | bytes 1245184 | tf_op jit(solution)/shard_map/all_to_all | solution.py:28
  115.0 3.5 %all-to-all-start.5 = ((f32[4,152,256]{2,1,0:T(8,128)}), f32[4,152,256]{2,1,0:T(8,128)S(1)}, u32[]{:S(2)}, u32[]{:S(2)}) async-start(f32[4,152,256]{2,1,0:T(8,128)} %broadcast_in_dim.17), calls=%async_computation.5 | async-start | bytes 1245184 | tf_op jit(solution)/shard_map/all_to_all | solution.py:28
  118.5 3.3 %prep.1 = (bf16[1024,768]{1,0:T(8,128)(2,1)}, f32[1,256]{1,0:T(1,128)S(1)}, f32[256,256]{1,0:T(8,128)S(1)}) custom-call(f32[1024,256]{1,0:T(8,128)} %copy-done, f32[256,256]{1,0:T(8,128)} %u_ref.1, f32[1,1024]{1,0:T(1,128)} %bitcast.31), custom_call_target="tpu_custom_call" | custom-call | tf_op jit(solution)/shard_map/prep/pallas_call | solution.py:235
  121.8 11.0 %all-to-all-done.5 = f32[4,152,256]{2,1,0:T(8,128)S(1)} async-done(((f32[4,152,256]{2,1,0:T(8,128)}), f32[4,152,256]{2,1,0:T(8,128)S(1)}, u32[]{:S(2)}, u32[]{:S(2)}) %all-to-all-start.5) | async-done | bytes 622624 | tf_op jit(solution)/shard_map/all_to_all | solution.py:28
  133.9 5.5 %all-to-all-start.8 = ((f32[4,128,256]{2,1,0:T(8,128)}), f32[4,128,256]{2,1,0:T(8,128)S(1)}, u32[]{:S(2)}, u32[]{:S(2)}) async-start(f32[4,128,256]{2,1,0:T(8,128)} %broadcast_in_dim.20), calls=%async_computation.8 | async-start | bytes 1048576 | tf_op jit(solution)/shard_map/all_to_all | solution.py:28
  145.4 5.0 %all-to-all-start.6 = ((f32[4,16,640]{2,1,0:T(8,128)}), f32[4,16,640]{2,1,0:T(8,128)S(1)}, u32[]{:S(2)}, u32[]{:S(2)}) async-start(f32[4,16,640]{2,1,0:T(8,128)} %get-tuple-element.28), calls=%async_computation.6 | async-start | bytes 327680 | tf_op jit(solution)/shard_map/all_to_all | solution.py:28
  152.4 12.1 %all-to-all-done.6 = f32[4,16,640]{2,1,0:T(8,128)S(1)} async-done(((f32[4,16,640]{2,1,0:T(8,128)}), f32[4,16,640]{2,1,0:T(8,128)S(1)}, u32[]{:S(2)}, u32[]{:S(2)}) %all-to-all-start.6) | async-done | bytes 163872 | tf_op jit(solution)/shard_map/all_to_all | solution.py:28
  165.4 3.5 %all-to-all-start.7 = ((f32[4,64,640]{2,1,0:T(8,128)}), f32[4,64,640]{2,1,0:T(8,128)S(1)}, u32[]{:S(2)}, u32[]{:S(2)}) async-start(f32[4,64,640]{2,1,0:T(8,128)} %broadcast_in_dim.19), calls=%async_computation.7 | async-start | bytes 1310720 | tf_op jit(solution)/shard_map/all_to_all | solution.py:28
  168.9 5.0 %left.1 = (f32[1,1024]{1,0:T(1,128)S(1)}, f32[1,512]{1,0:T(1,128)S(1)}, f32[1024,512]{1,0:T(8,128)}) custom-call(f32[512,256]{1,0:T(8,128)} %bitcast.24, f32[512,256]{1,0:T(8,128)S(1)} %collective-permute-done.6.far_ref, f32[512,256]{1,0:T(8,128)S(1)} %get-tuple-element.23.c_ref, f32[256,256]{1,0:T(8,128)S(1)} %get-tuple-element.26.u_ref, ...), custom_call_target="tpu_custom_call" | custom-call | tf_op jit(solution)/shard_map/left/pallas_call | solution.py:307
  173.9 3.9 %all-to-all-done.7 = f32[4,64,640]{2,1,0:T(8,128)S(1)} async-done(((f32[4,64,640]{2,1,0:T(8,128)}), f32[4,64,640]{2,1,0:T(8,128)S(1)}, u32[]{:S(2)}, u32[]{:S(2)}) %all-to-all-start.7) | async-done | bytes 655392 | tf_op jit(solution)/shard_map/all_to_all | solution.py:28
  177.8 5.0 %right.1 = (f32[1,1024]{1,0:T(1,128)}, f32[1,512]{1,0:T(1,128)}, f32[1024,512]{1,0:T(8,128)}) custom-call(f32[256,640]{1,0:T(8,128)S(1)} %bitcast.19, f32[8,256]{1,0:T(8,128)S(1)} %get-tuple-element.29.vec_ref, f32[1,1024]{1,0:T(1,128)S(1)} %get-tuple-element.30.row_ref, f32[1,512]{1,0:T(1,128)S(1)} %get-tuple-element.31.col_ref, ...), custom_call_target="tpu_custom_call" | custom-call | tf_op jit(solution)/shard_map/right/pallas_call | solution.py:358
  (36 shorter events, 17.1 us)
Async XLA Ops:
  24.0 26.1 %collective-permute-start.4 = (f32[512,256]{1,0:T(8,128)S(1)}, f32[512,256]{1,0:T(8,128)S(1)}, u32[]{:S(2)}, u32[]{:S(2)}) collective-permute-start(f32[512,256]{1,0:T(8,128)S(1)} %bitcast.20), channel_id=1, source_target_pairs={{0,1},{1,0},{2,3},{3,2},{4,5},{5,4},{6,7},{7,6},{8,9},{9,8},{10,11... | collective-permute-start | bytes 1572872 | tf_op jit(solution)/shard_map/ppermute | solution.py:50
  25.9 14.2 %collective-permute-start = (f32[128,256]{1,0:T(8,128)S(1)}, f32[128,256]{1,0:T(8,128)S(1)}, u32[]{:S(2)}, u32[]{:S(2)}) collective-permute-start(f32[128,256]{1,0:T(8,128)S(1)} %bitcast.28), channel_id=1, source_target_pairs={{0,0},{1,128},{2,32},{3,160},{4,64},{5,192},{6,96},{7,224},{8,256}... | collective-permute-start | bytes 393224 | tf_op jit(solution)/shard_map/ppermute | solution.py:374
  40.2 8.0 %collective-permute-start.1 = (f32[128,256]{1,0:T(8,128)S(1)}, f32[128,256]{1,0:T(8,128)S(1)}, u32[]{:S(2)}, u32[]{:S(2)}) collective-permute-start(f32[128,256]{1,0:T(8,128)S(1)} %collective-permute-done), channel_id=1, source_target_pairs={{0,128},{128,0},{256,384},{384,256},{1,129},{129,1},{257,385},{385... | collective-permute-start | bytes 393224 | tf_op jit(solution)/shard_map/ppermute | solution.py:50
  48.2 11.1 %collective-permute-start.2 = (f32[2,4,32,256]{3,2,1,0:T(8,128)S(1)}, f32[2,4,32,256]{3,2,1,0:T(8,128)S(1)}, u32[]{:S(2)}, u32[]{:S(2)}) collective-permute-start(f32[2,4,32,256]{3,2,1,0:T(8,128)S(1)} %pad_maximum_fusion.1.own_ref), channel_id=1, source_target_pairs={{0,256},{128,384},{256,0},{384,128},{1,257},{129,385},{257,1},{385... | collective-permute-start | bytes 786440 | tf_op jit(solution)/shard_map/ppermute | solution.py:50
  53.6 5.7 %copy-start = (f32[1024,256]{1,0:T(8,128)}, f32[1024,256]{1,0:T(8,128)S(1)}, u32[]{:S(2)}) copy-start(f32[1024,256]{1,0:T(8,128)S(1)} %get-tuple-element.25.v_ref) | copy-start | bytes 3145732
  53.6 13.3 %all-to-all-start.2 = ((f32[4,64,512]{2,1,0:T(8,128)}), f32[4,64,512]{2,1,0:T(8,128)S(1)}, u32[]{:S(2)}, u32[]{:S(2)}) async-start(f32[4,64,512]{2,1,0:T(8,128)} %bitcast.8), calls=%async_computation.2 | async-start | bytes 1048576 | tf_op jit(solution)/shard_map/all_to_all | solution.py:28
  59.2 0.7 copy-start.1
  60.0 0.9 copy-start.2
  64.9 22.4 %collective-permute-start.3 = (f32[512,256]{1,0:T(8,128)S(1)}, f32[512,256]{1,0:T(8,128)S(1)}, u32[]{:S(2)}, u32[]{:S(2)}) collective-permute-start(f32[512,256]{1,0:T(8,128)S(1)} %get-tuple-element.21), channel_id=1, source_target_pairs={{0,1},{1,0},{2,3},{3,2},{4,5},{5,4},{6,7},{7,6},{8,9},{9,8},{10,11... | collective-permute-start | bytes 1572872 | tf_op jit(solution)/shard_map/ppermute | solution.py:50
  67.6 33.0 %all-to-all-start.3 = ((f32[4,16,512]{2,1,0:T(8,128)}), f32[4,16,512]{2,1,0:T(8,128)S(1)}, u32[]{:S(2)}, u32[]{:S(2)}) async-start(f32[4,16,512]{2,1,0:T(8,128)} %bitcast.9), calls=%async_computation.3 | async-start | bytes 262144 | tf_op jit(solution)/shard_map/all_to_all | solution.py:28
  115.0 17.8 %all-to-all-start.5 = ((f32[4,152,256]{2,1,0:T(8,128)}), f32[4,152,256]{2,1,0:T(8,128)S(1)}, u32[]{:S(2)}, u32[]{:S(2)}) async-start(f32[4,152,256]{2,1,0:T(8,128)} %broadcast_in_dim.17), calls=%async_computation.5 | async-start | bytes 1245184 | tf_op jit(solution)/shard_map/all_to_all | solution.py:28
  133.9 11.5 %all-to-all-start.8 = ((f32[4,128,256]{2,1,0:T(8,128)}), f32[4,128,256]{2,1,0:T(8,128)S(1)}, u32[]{:S(2)}, u32[]{:S(2)}) async-start(f32[4,128,256]{2,1,0:T(8,128)} %broadcast_in_dim.20), calls=%async_computation.8 | async-start | bytes 1048576 | tf_op jit(solution)/shard_map/all_to_all | solution.py:28
  139.4 3.1 %collective-permute-start.5 = (f32[24,256]{1,0:T(8,128)S(1)}, f32[24,256]{1,0:T(8,128)S(1)}, u32[]{:S(2)}, u32[]{:S(2)}) collective-permute-start(f32[24,256]{1,0:T(8,128)S(1)} %slice.12.own_ref), channel_id=1, source_target_pairs={{0,1},{1,0},{2,3},{3,2},{4,5},{5,4},{6,7},{7,6},{8,9},{9,8},{10,11... | collective-permute-start | bytes 73736 | tf_op jit(solution)/shard_map/ppermute | solution.py:50
  145.4 23.5 %copy-start.3 = (f32[4,128,256]{2,1,0:T(8,128)}, f32[4,128,256]{2,1,0:T(8,128)S(1)}, u32[]{:S(2)}) copy-start(f32[4,128,256]{2,1,0:T(8,128)S(1)} %all-to-all-done.8) | copy-start | bytes 1572868
  145.4 19.1 %all-to-all-start.6 = ((f32[4,16,640]{2,1,0:T(8,128)}), f32[4,16,640]{2,1,0:T(8,128)S(1)}, u32[]{:S(2)}, u32[]{:S(2)}) async-start(f32[4,16,640]{2,1,0:T(8,128)} %get-tuple-element.28), calls=%async_computation.6 | async-start | bytes 327680 | tf_op jit(solution)/shard_map/all_to_all | solution.py:28
  150.5 18.4 %collective-permute-start.6 = (f32[512,256]{1,0:T(8,128)S(1)}, f32[512,256]{1,0:T(8,128)S(1)}, u32[]{:S(2)}, u32[]{:S(2)}) collective-permute-start(f32[512,256]{1,0:T(8,128)S(1)} %bitcast.23), channel_id=1, source_target_pairs={{0,1},{1,0},{2,3},{3,2},{4,5},{5,4},{6,7},{7,6},{8,9},{9,8},{10,11... | collective-permute-start | bytes 1572872 | tf_op jit(solution)/shard_map/ppermute | solution.py:50
  165.4 12.4 %all-to-all-start.7 = ((f32[4,64,640]{2,1,0:T(8,128)}), f32[4,64,640]{2,1,0:T(8,128)S(1)}, u32[]{:S(2)}, u32[]{:S(2)}) async-start(f32[4,64,640]{2,1,0:T(8,128)} %broadcast_in_dim.19), calls=%async_computation.7 | async-start | bytes 1310720 | tf_op jit(solution)/shard_map/all_to_all | solution.py:28
